TPU v7x, 128 devices: a whole 4x4x4 slice. The times are simulated.
128 devices in a mesh: slab: 32 (over z, x, core), cross: 4 (over y).
Axes of the slice: x: 4, y: 4, z: 4, core: 2. Of those that a mesh axis runs over, the one named last changes fastest.
Arguments:
- velocity: float32 [3, 512, 256, 256], P(None, 'slab', 'cross'), may hold values from -6 to 6
- shape_weight: float32 [32, 384], replicated, may hold values from -6 to 6
- w_in: bfloat16 [384, 1024], replicated, may hold values from -0.3125 to 0.3125
- w_out: bfloat16 [1024, 4096], replicated, may hold values from -0.1875 to 0.1875
- decay: float32 [1024], replicated, may hold values from 0.1 to 2
- rotor_states: float32 [32, 1024], P('slab'), may hold values from -6 to 6
- slot_of_rotor: int32 [32], replicated, may hold values from 0 to 31, each once
- entry_rotor: int32 [131072, 1], P(('slab', 'cross')), may hold values from 0 to 31; in each aligned block of 1024 rows (0 to 1023, 1024 to 2047, ...) at most 64 rows name the same one
- entry_tile: int32 [131072], P(('slab', 'cross')), may hold values from 0 to 2047
- entry_sub: int32 [131072], P(('slab', 'cross')), may hold values from 0 to 31
Outputs:
- advanced: float32 [3, 512, 256, 256], P(None, 'slab', 'cross')
- new_states: float32 [32, 1024], P('slab')
Inputs may be any that keep to these rules, and one draw needn't show every extreme that they name: `entry_rotor`: in the rows of one device no rotor is named more than 64 times, a bound that some block reaches; every rotor is named by some entry. Each slot once; rotor r is owned by slab slot_of_rotor[r].
All inputs are finite; a program needn't handle non-finite values.
Results may differ from a plain program's by a relative error of at most 0.0026.
Values may be sent and summed in bfloat16 or wider, within the bound.
A program may use at most 64 MiB of HBM per device.

v0:
```python
import jax
import jax.numpy as jnp
from jax import lax
from jax.sharding import PartitionSpec as P

TILE = 128
R = 32
NSUB = 32


time_step = 0.1
viscosity = 0.3
pool_scale = 1.0 / 64.0
state_step = 0.5
force_scale = 0.5


def extended(cells, sides, width):
    for axis, dim in sides:
        count = lax.axis_size(axis)
        ends = count - 1
        head = lax.slice_in_dim(cells, 0, width, axis=dim)
        tail = lax.slice_in_dim(cells, cells.shape[dim] - width, cells.shape[dim], axis=dim)
        cells = jnp.concatenate(
            [
                lax.ppermute(tail, axis, [(i, (i + 1) % count) for i in range(ends)]),
                cells,
                lax.ppermute(head, axis, [((i + 1) % count, i) for i in range(ends)]),
            ],
            axis=dim,
        )
    return cells


def combine_terms(velocity, east, west, north, south, upper, lower):
    laplace = east + west + north + south + upper + lower - 6.0 * velocity
    advect = (
        velocity[0:1] * ((east - west) * 0.5)
        + velocity[1:2] * ((north - south) * 0.5)
        + velocity[2:3] * ((upper - lower) * 0.5)
    )
    return velocity + time_step * (viscosity * laplace - advect)


def on_device(
    velocity,
    shape_weight,
    w_in,
    w_out,
    decay,
    rotor_states,
    slot_of_rotor,
    entry_rotor,
    entry_tile,
    entry_sub,
):
    local_x, local_y, local_z = (velocity.shape[1], velocity.shape[2], velocity.shape[3])
    tile_count = local_x * local_y * local_z // TILE
    entry_count = entry_tile.shape[0]
    rotor_hot = (entry_rotor == jnp.arange(R, dtype=jnp.int32)[None, :]).astype(jnp.int32)
    slots = jnp.sum(rotor_hot * slot_of_rotor[None, :], axis=1)
    flat_cells = velocity.reshape(3, tile_count, TILE)
    picked = jnp.take(flat_cells, entry_tile, axis=1)
    payload = jnp.transpose(picked, (1, 0, 2)).reshape(entry_count, 3 * TILE).astype(jnp.bfloat16)
    sub_range = jnp.arange(NSUB, dtype=jnp.int32)
    sub_hot = (entry_sub[:, None] == sub_range[None, :]).astype(jnp.float32)
    gains = jnp.dot(sub_hot, shape_weight, precision=lax.Precision.HIGHEST)
    weighted = gains * payload.astype(jnp.float32)
    slot_hot = (slots[:, None] == jnp.arange(R, dtype=jnp.int32)[None, :]).astype(jnp.float32)
    per_rotor = jnp.dot(slot_hot.T, weighted, precision=lax.Precision.HIGHEST)
    partial_value = lax.psum_scatter(per_rotor, "slab", scatter_dimension=0, tiled=True)
    pooled = lax.psum(partial_value, "cross")
    pooled_b = (pooled * pool_scale).astype(jnp.bfloat16)
    drive = jnp.dot(pooled_b, w_in, preferred_element_type=jnp.float32)
    new_states = rotor_states + state_step * (drive - decay[None, :] * rotor_states)
    own_sources = jnp.dot(
        new_states.astype(jnp.bfloat16), w_out, preferred_element_type=jnp.float32
    ).astype(jnp.bfloat16)
    all_sources = lax.all_gather(own_sources, "slab", axis=0, tiled=True)
    rows = all_sources.reshape(R * NSUB, TILE)[slots * NSUB + entry_sub].astype(jnp.float32)
    forcing = jnp.zeros((tile_count, TILE), jnp.float32).at[entry_tile].add(rows)
    vertical = jnp.pad(velocity, ((0, 0), (0, 0), (0, 0), (1, 1)))
    upper = vertical[:, :, :, 2:]
    lower = vertical[:, :, :, :-2]
    padded = extended(velocity.astype(jnp.bfloat16), (("slab", 1), ("cross", 2)), 1).astype(
        velocity.dtype
    )
    east = padded[:, 2:, 1:-1, :]
    west = padded[:, :-2, 1:-1, :]
    north = padded[:, 1:-1, 2:, :]
    south = padded[:, 1:-1, :-2, :]
    advanced = combine_terms(velocity, east, west, north, south, upper, lower)
    advanced = advanced.at[0].add(-force_scale * forcing.reshape(local_x, local_y, local_z))
    return (advanced, new_states)


def solution(mesh):
    in_specs = (
        P(None, "slab", "cross", None),
        P(),
        P(),
        P(),
        P(),
        P("slab", None),
        P(),
        P(("slab", "cross"), None),
        P(("slab", "cross")),
        P(("slab", "cross")),
    )
    out_specs = (P(None, "slab", "cross", None), P("slab", None))
    return jax.shard_map(
        on_device, mesh=mesh, in_specs=in_specs, out_specs=out_specs, check_vma=False
    )
```

profile of v0, /device:TPU:1, one launch (start us, length us, event | category | flops | bytes accessed | tf_op | source)
XLA Modules:
  0.0 236.0 jit_solution(2177905941122030248)
XLA Ops:
  0.6 2.2 convert_element_type.40
  3.5 4.5 %collective-permute-start = (bf16[3,1,64,256]{3,2,1,0:T(8,128)(2,1)}, bf16[3,1,64,256]{3,2,1,0:T(8,128)(2,1)S(1)}, u32[]{:S(2)}, u32[]{:S(2)}) collective-permute-start(bf16[3,1,64,256]{3,2,1,0:T(8,128)(2,1)} %get-tuple-element.19), channel_id=1, source_target_pairs={{0,4},{4,8},{8,12},{12,16},{16,20},{20,24},{24,28},{28,32},{32,36}... | collective-permute-start | bytes 294920 | tf_op jit(solution)/shard_map/ppermute | solution.py:26
  8.0 1.9 collective-permute-start.1
  10.0 4.0 %reshape.83 = bf16[3,2048,128]{2,1,0:T(8,128)(2,1)} reshape(f32[3,16,64,256]{3,2,1,0:T(8,128)} %param.12) | data formatting | bytes 4718592 | tf_op jit(solution)/shard_map/reshape | solution.py:62
  14.0 4.2 %copy.22 = bf16[3,2048,128]{2,0,1:T(4,128)(2,1)} copy(bf16[3,2048,128]{2,1,0:T(8,128)(2,1)} %reshape.83) | data formatting | bytes 3145728 | tf_op jit(solution)/shard_map/reshape | solution.py:62
  18.1 5.1 %gather_fusion = bf16[1024,3,128]{2,1,0:T(4,128)(2,1)S(1)} fusion(bf16[3,2048,128]{2,0,1:T(4,128)(2,1)} %copy.22, s32[1024]{0:T(1024)S(1)} %get-tuple-element.21), kind=kCustom, calls=%fused_computation | custom fusion | bytes 1576960 | tf_op jit(solution)/shard_map/jit(_take)/gather | solution.py:63
  23.3 1.3 fusion.6
  24.7 3.1 %copy.24 = f32[1024,3,128]{0,2,1:T(8,128)} copy(f32[1024,3,128]{2,0,1:T(8,128)} %fusion.6) | data formatting | bytes 3145728 | tf_op jit(solution)/shard_map/convert_element_type | solution.py:68
  27.7 3.0 %copy.25 = f32[1024,384]{1,0:T(8,128)} copy(f32[1024,384]{0,1:T(8,128)} %bitcast.24) | data formatting | bytes 3145728 | tf_op jit(solution)/shard_map/convert_element_type | solution.py:68
  31.7 2.3 fusion.1
  34.0 124.0 %all-reduce.1 = f32[32,384]{1,0:T(8,128)S(1)} all-reduce(f32[32,384]{1,0:T(8,128)S(1)} %fusion.1), channel_id=3, replica_groups=mesh['slab'=32,'cross'=4] {'slab'}, use_global_device_ids=true, to_apply=%region_1.2.clone | all-reduce | flops 12288 | bytes 98304
  159.2 8.7 %psum.7 = f32[1,384]{1,0:T(1,128)S(1)} all-reduce(f32[1,384]{1,0:T(1,128)S(1)} %constant_dynamic-slice_fusion), channel_id=1, replica_groups=mesh['slab'=32,'cross'=4] {'cross'}, use_global_device_ids=true, to_apply=%region_2.3 | all-reduce | flops 384 | bytes 3072 | tf_op jit(solution)/shard_map/psum | solution.py:72
  168.2 4.6 %fusion.14 = f32[1,4096]{1,0:T(1,128)S(1)} fusion(bf16[1024,4096]{1,0:T(8,128)(2,1)} %param.15, f32[1,1024]{1,0:T(1,128)S(1)} %fusion.4), kind=kOutput, calls=%fused_computation.37 | convolution fusion | flops 8389632 | bytes 8409088 | tf_op jit(solution)/shard_map/dot_general | solution.py:76
  172.8 32.1 %all-gather = bf16[131072]{0:T(1024)(128)(2,1)} all-gather(bf16[4096]{0:T(1024)(128)(2,1)S(1)} %convert_element_type.48), channel_id=2, replica_groups=mesh['slab'=32,'cross'=4] {'slab'}, dimensions={0}, use_global_device_ids=true | all-gather | bytes 270336 | tf_op jit(solution)/shard_map/all_gather | solution.py:79
  204.8 12.5 %scatter_custom_fusion = f32[2048,128]{1,0:T(8,128)S(1)} fusion(s32[1024]{0:T(1024)S(1)} %get-tuple-element.22, f32[]{:T(128)} %constant.53.clone.1, bf16[1024,128]{1,0:T(8,128)(2,1)} %bitcast.25, s32[1024]{0:T(1024)S(1)} %fusion.13), kind=kCustom, calls=%fused_computation.21 | custom fusion | flops 262144 | bytes 1314820 | tf_op jit(solution)/shard_map/scatter-add | solution.py:81
  217.4 1.0 broadcast_multiply_fusion
  218.4 1.7 pad_maximum_fusion.2
  220.1 1.9 collective-permute-start.2
  222.0 1.3 collective-permute-start.3
  223.3 1.8 multiply_bitcast_fusion.2
  225.1 1.5 mul.136
  227.2 1.9 maximum_convert_fusion
  229.3 4.8 %multiply_add_fusion = f32[3,16,64,256]{3,2,1,0:T(8,128)S(1)} fusion(f32[3,16,64,256]{3,2,1,0:T(8,128)S(1)} %copy-done.2, f32[3,18,66,256]{3,2,1,0:T(8,128)S(1)} %maximum_convert_fusion, f32[16,64,256]{2,1,0:T(8,128)S(1)} %copy-done.5, f32[16,64,256]{2,1,0:T(8,128)} %get-tuple-element.16, f32[16,64,256]{2,1,0:T(8,128)S(1)} %copy-done.4), kind=kLoop, calls=%fused_computation.5 | loop fusion | flops 14942208 | bytes 22020096 | tf_op jit(solution)/shard_map/add | solution.py:42
  234.4 1.7 copy-done.3
  (44 shorter events, 4.0 us)
Async XLA Ops:
  0.6 167.3 %copy-start = (bf16[384,1024]{1,0:T(8,128)(2,1)S(1)}, bf16[384,1024]{1,0:T(8,128)(2,1)}, u32[]{:S(2)}) copy-start(bf16[384,1024]{1,0:T(8,128)(2,1)} %param.14) | copy-start | bytes 2359300
  2.8 11.1 %copy-start.9 = (s32[1024]{0:T(1024)S(1)}, s32[1024]{0:T(1024)}, u32[]{:S(2)}) copy-start(s32[1024]{0:T(1024)} %param.20) | copy-start | bytes 12292
  3.5 214.9 %collective-permute-start = (bf16[3,1,64,256]{3,2,1,0:T(8,128)(2,1)}, bf16[3,1,64,256]{3,2,1,0:T(8,128)(2,1)S(1)}, u32[]{:S(2)}, u32[]{:S(2)}) collective-permute-start(bf16[3,1,64,256]{3,2,1,0:T(8,128)(2,1)} %get-tuple-element.19), channel_id=1, source_target_pairs={{0,4},{4,8},{8,12},{12,16},{16,20},{20,24},{24,28},{28,32},{32,36}... | collective-permute-start | bytes 294920 | tf_op jit(solution)/shard_map/ppermute | solution.py:26
  8.0 210.4 %collective-permute-start.1 = (bf16[3,1,64,256]{3,2,1,0:T(8,128)(2,1)}, bf16[3,1,64,256]{3,2,1,0:T(8,128)(2,1)}, u32[]{:S(2)}, u32[]{:S(2)}) collective-permute-start(bf16[3,1,64,256]{3,2,1,0:T(8,128)(2,1)} %get-tuple-element.20), channel_id=1, source_target_pairs={{4,0},{8,4},{12,8},{16,12},{20,16},{24,20},{28,24},{32,28},{36,32}... | collective-permute-start | bytes 294920 | tf_op jit(solution)/shard_map/ppermute | solution.py:28
  24.6 6.1 %copy-start.12 = (s32[1024,1]{0,1:T(1,128)S(1)}, s32[1024,1]{0,1:T(1,128)}, u32[]{:S(2)}) copy-start(s32[1024,1]{0,1:T(1,128)} %param.19) | copy-start | bytes 12292
  24.6 6.1 %copy-start.13 = (s32[32]{0:T(128)S(1)}, s32[32]{0:T(128)}, u32[]{:S(2)}) copy-start(s32[32]{0:T(128)} %param.18) | copy-start | bytes 388
  24.6 6.2 %copy-start.6 = (f32[32,384]{1,0:T(8,128)S(1)}, f32[32,384]{1,0:T(8,128)}, u32[]{:S(2)}) copy-start(f32[32,384]{1,0:T(8,128)} %param.13) | copy-start | bytes 147460
  24.6 6.2 %copy-start.8 = (s32[1024]{0:T(1024)S(1)}, s32[1024]{0:T(1024)}, u32[]{:S(2)}) copy-start(s32[1024]{0:T(1024)} %param.21) | copy-start | bytes 12292
  30.7 127.2 %copy-start.14 = (u32[128]{0:T(128)S(1)}, u32[128]{0:T(128)}, u32[]{:S(2)}) copy-start(u32[128]{0:T(128)} %constant.72) | copy-start | bytes 1540
  30.8 137.2 %copy-start.10 = (f32[1,1024]{1,0:T(1,128)S(1)}, f32[1,1024]{1,0:T(1,128)}, u32[]{:S(2)}) copy-start(f32[1,1024]{1,0:T(1,128)} %param.17) | copy-start | bytes 12292
  30.8 137.2 %copy-start.11 = (f32[1024]{0:T(1024)S(1)}, f32[1024]{0:T(1024)}, u32[]{:S(2)}) copy-start(f32[1024]{0:T(1024)} %param.16) | copy-start | bytes 12292
  168.2 4.6 %copy-start.7 = (f32[1,1024]{1,0:T(1,128)}, f32[1,1024]{1,0:T(1,128)S(1)}, u32[]{:S(2)}) copy-start(f32[1,1024]{1,0:T(1,128)S(1)} %fusion.4) | copy-start | bytes 12292
  217.4 6.0 %copy-start.1 = (f32[3,16,64,256]{3,2,1,0:T(8,128)S(1)}, f32[3,16,64,256]{3,2,1,0:T(8,128)}, u32[]{:S(2)}) copy-start(f32[3,16,64,256]{3,2,1,0:T(8,128)} %param.12) | copy-start | bytes 9437188
  220.1 6.6 %collective-permute-start.2 = (bf16[3,18,1,256]{3,2,1,0:T(2,128)(2,1)}, bf16[3,18,1,256]{3,2,1,0:T(2,128)(2,1)}, u32[]{:S(2)}, u32[]{:S(2)}) collective-permute-start(bf16[3,18,1,256]{3,2,1,0:T(2,128)(2,1)} %get-tuple-element.17), channel_id=1, source_target_pairs={{0,1},{1,2},{2,3},{4,5},{5,6},{6,7},{8,9},{9,10},{10,11},{12,13},{... | collective-permute-start | bytes 82952 | tf_op jit(solution)/shard_map/ppermute | solution.py:26
  222.0 5.2 %collective-permute-start.3 = (bf16[3,18,1,256]{3,2,1,0:T(2,128)(2,1)}, bf16[3,18,1,256]{3,2,1,0:T(2,128)(2,1)}, u32[]{:S(2)}, u32[]{:S(2)}) collective-permute-start(bf16[3,18,1,256]{3,2,1,0:T(2,128)(2,1)} %get-tuple-element.18), channel_id=1, source_target_pairs={{1,0},{2,1},{3,2},{5,4},{6,5},{7,6},{9,8},{10,9},{11,10},{13,12},{... | collective-permute-start | bytes 82952 | tf_op jit(solution)/shard_map/ppermute | solution.py:28
  226.7 2.5 %copy-start.2 = (f32[3,16,64,256]{3,2,1,0:T(8,128)S(1)}, f32[3,16,64,256]{3,2,1,0:T(8,128)}, u32[]{:S(2)}) copy-start(f32[3,16,64,256]{3,2,1,0:T(8,128)} %param.12) | copy-start | bytes 9437188
  226.7 2.5 %copy-start.4 = (f32[16,64,256]{2,1,0:T(8,128)S(1)}, f32[16,64,256]{2,1,0:T(8,128)}, u32[]{:S(2)}) copy-start(f32[16,64,256]{2,1,0:T(8,128)} %get-tuple-element.14) | copy-start | bytes 3145732
  226.7 2.6 %copy-start.5 = (f32[16,64,256]{2,1,0:T(8,128)S(1)}, f32[16,64,256]{2,1,0:T(8,128)}, u32[]{:S(2)}) copy-start(f32[16,64,256]{2,1,0:T(8,128)} %get-tuple-element.15) | copy-start | bytes 3145732
  234.3 1.7 copy-start.3
where the time goes:
time: 237 us; the launch traced here: 236 us
  blocking collectives  165 us (70%)
  other arithmetic  27.7 us (12%)
  local copies, waits for them, and re-layouts  24.6 us (10%)
  starting transfers between devices  9.6 us (4%)
  matrix products  7.91 us (3%)
    unnamed x1, blocking collectives  124 us
    all_gather x1, blocking collectives, on_device(): all_sources = lax.all_gather(own_sources, 'slab', axis=0, tiled=True)  32.1 us
    scatter-add x1, other arithmetic, on_device(): jnp.zeros((tile_count, TILE), jnp.float32).at[entry_tile].add(rows)  12.5 us
    psum x1, blocking collectives, on_device(): pooled = lax.psum(partial_value, 'cross')  8.74 us
    reshape x2, local copies, waits for them, and re-layouts, on_device(): flat_cells = velocity.reshape(3, tile_count, TILE)  8.15 us
    ppermute x2, starting transfers between devices, extended(): lax.ppermute(tail, axis, [(i, (i + 1) % count) for i in range(ends)])  6.39 us
    convert_element_type x2, local copies, waits for them, and re-layouts, on_device(): weighted = gains * payload.astype(jnp.float32)  6.1 us
    gather x1, local copies, waits for them, and re-layouts, on_device(): picked = jnp.take(flat_cells, entry_tile, axis=1)  5.14 us
  transfers between devices with their start and end apart: 4, of which 1 were waited for; matrix products, arithmetic and copies ran while one was open for 20% of the time, Pallas kernels for 0%

commit v1 on v0

--- a/solution.py
+++ b/solution.py
@@ -13,6 +13,55 @@
 pool_scale = 1.0 / 64.0
 state_step = 0.5
 force_scale = 0.5
+
+
+def ring_perm(size, stride, n, shift):
+    pairs = []
+    for s in range(size):
+        base = (s // (stride * n)) * stride * n + s % stride
+        pos = (s // stride) % n
+        pairs.append((s, base + ((pos + shift) % n) * stride))
+    return pairs
+
+
+def ring_sum(value, axis, stride, n):
+    size = lax.axis_size(axis)
+    if n == 2:
+        return value + lax.ppermute(value, axis, ring_perm(size, stride, n, 1))
+    got = [lax.ppermute(value, axis, ring_perm(size, stride, n, j)) for j in (1, 2, 3)]
+    return (value + got[1]) + (got[0] + got[2])
+
+
+def ring_gather(value, axis, stride, n):
+    size = lax.axis_size(axis)
+    pos = (lax.axis_index(axis) // stride) % n
+    got = [value] + [lax.ppermute(value, axis, ring_perm(size, stride, n, j)) for j in range(1, n)]
+    parts = []
+    for p in range(n):
+        pick = got[0]
+        for j in range(1, n):
+            pick = jnp.where((pos - j) % n == p, got[j], pick)
+        parts.append(jnp.where(pos == p, got[0], pick))
+    return jnp.concatenate(parts, axis=0)
+
+
+def mesh_rings():
+    slab = lax.axis_size("slab")
+    rings = [("slab", 1, 2), ("slab", 2, 4), ("slab", 8, slab // 8)]
+    return rings
+
+
+def all_sum(value):
+    for axis, stride, n in mesh_rings() + [("cross", 1, lax.axis_size("cross"))]:
+        value = ring_sum(value, axis, stride, n)
+    return value
+
+
+def slab_gather(value):
+    parts = value
+    for axis, stride, n in mesh_rings():
+        parts = ring_gather(parts, axis, stride, n)
+    return parts
 
 
 def extended(cells, sides, width):
@@ -56,29 +105,31 @@
 ):
     local_x, local_y, local_z = (velocity.shape[1], velocity.shape[2], velocity.shape[3])
     tile_count = local_x * local_y * local_z // TILE
-    entry_count = entry_tile.shape[0]
+    all_states = slab_gather(rotor_states)
     rotor_hot = (entry_rotor == jnp.arange(R, dtype=jnp.int32)[None, :]).astype(jnp.int32)
     slots = jnp.sum(rotor_hot * slot_of_rotor[None, :], axis=1)
-    flat_cells = velocity.reshape(3, tile_count, TILE)
-    picked = jnp.take(flat_cells, entry_tile, axis=1)
-    payload = jnp.transpose(picked, (1, 0, 2)).reshape(entry_count, 3 * TILE).astype(jnp.bfloat16)
     sub_range = jnp.arange(NSUB, dtype=jnp.int32)
     sub_hot = (entry_sub[:, None] == sub_range[None, :]).astype(jnp.float32)
     gains = jnp.dot(sub_hot, shape_weight, precision=lax.Precision.HIGHEST)
-    weighted = gains * payload.astype(jnp.float32)
     slot_hot = (slots[:, None] == jnp.arange(R, dtype=jnp.int32)[None, :]).astype(jnp.float32)
-    per_rotor = jnp.dot(slot_hot.T, weighted, precision=lax.Precision.HIGHEST)
-    partial_value = lax.psum_scatter(per_rotor, "slab", scatter_dimension=0, tiled=True)
-    pooled = lax.psum(partial_value, "cross")
+    per_rotor = []
+    for c in range(3):
+        cells = velocity[c].reshape(tile_count, TILE)
+        picked = jnp.take(cells, entry_tile, axis=0).astype(jnp.bfloat16).astype(jnp.float32)
+        weighted = gains[:, c * TILE:(c + 1) * TILE] * picked
+        per_rotor.append(jnp.dot(slot_hot.T, weighted, precision=lax.Precision.HIGHEST))
+    per_rotor = jnp.concatenate(per_rotor, axis=1)
+    pooled = all_sum(per_rotor)
     pooled_b = (pooled * pool_scale).astype(jnp.bfloat16)
     drive = jnp.dot(pooled_b, w_in, preferred_element_type=jnp.float32)
-    new_states = rotor_states + state_step * (drive - decay[None, :] * rotor_states)
-    own_sources = jnp.dot(
-        new_states.astype(jnp.bfloat16), w_out, preferred_element_type=jnp.float32
+    all_new = all_states + state_step * (drive - decay[None, :] * all_states)
+    all_sources = jnp.dot(
+        all_new.astype(jnp.bfloat16), w_out, preferred_element_type=jnp.float32
     ).astype(jnp.bfloat16)
-    all_sources = lax.all_gather(own_sources, "slab", axis=0, tiled=True)
-    rows = all_sources.reshape(R * NSUB, TILE)[slots * NSUB + entry_sub].astype(jnp.float32)
-    forcing = jnp.zeros((tile_count, TILE), jnp.float32).at[entry_tile].add(rows)
+    new_states = lax.dynamic_slice_in_dim(all_new, lax.axis_index("slab"), 1, axis=0)
+    rows = all_sources.reshape(R * NSUB, TILE)[slots * NSUB + entry_sub]
+    tile_hot = (jnp.arange(tile_count, dtype=jnp.int32)[:, None] == entry_tile[None, :]).astype(jnp.bfloat16)
+    forcing = jnp.dot(tile_hot, rows, preferred_element_type=jnp.float32)
     vertical = jnp.pad(velocity, ((0, 0), (0, 0), (0, 0), (1, 1)))
     upper = vertical[:, :, :, 2:]
     lower = vertical[:, :, :, :-2]

time: 237 us -> 91 us (0.38)
  the two profiles are of different devices: /device:TPU:1 before, /device:TPU:0 now
where the time goes in v1:
time: 91 us; the launch traced here: 90.6 us
  starting transfers between devices  35.7 us (39%)
  local copies, waits for them, and re-layouts  18.5 us (20%)
  other arithmetic  14.9 us (16%)
  waiting for transfers between devices  11.7 us (13%)
  matrix products  8.67 us (10%)
  between operations  1.14 us (1%)
    ppermute x9, starting transfers between devices, ring_sum(): lax.ppermute(value, axis, ring_perm(size, stride, n, j))  12.7 us
    ppermute x7, starting transfers between devices, ring_gather(): lax.ppermute(value, axis, ring_perm(size, stride, n, j))  11.9 us
    gather x3, local copies, waits for them, and re-layouts, on_device(): jnp.take(cells, entry_tile, axis=0).astype(jnp.bfloat16).astype(jnp.float32)  10.7 us
    ppermute x2, starting transfers between devices, extended(): lax.ppermute(tail, axis, [(i, (i + 1) % count) for i in range(ends)])  8.48 us
    ppermute x7, waiting for transfers between devices, ring_gather(): lax.ppermute(value, axis, ring_perm(size, stride, n, j))  7.92 us
    add x1, other arithmetic, combine_terms(): return velocity + time_step * (viscosity * laplace - advect)  4.92 us
    ppermute x9, waiting for transfers between devices, ring_sum(): lax.ppermute(value, axis, ring_perm(size, stride, n, j))  3.81 us
    dot_general x3, matrix products, on_device(): jnp.dot(slot_hot.T, weighted, precision=lax.Precision.HIGHEST)  3.67 us
  transfers between devices with their start and end apart: 21, of which 6 were waited for; matrix products, arithmetic and copies ran while one was open for 32% of the time, Pallas kernels for 0%

profile of v1, /device:TPU:0, one launch (start us, length us, event | category | flops | bytes accessed | tf_op | source)
XLA Modules:
  0.0 90.6 jit_solution(5048104722058381585)
XLA Ops:
  0.7 2.3 %convert_element_type.39 = bf16[3,16,64,256]{3,2,1,0:T(8,128)(2,1)S(1)} convert(f32[3,16,64,256]{3,2,1,0:T(8,128)} %param.14) | non-fusion elementwise | flops 786432 | bytes 4718592 | tf_op jit(solution)/shard_map/convert_element_type | solution.py:136
  4.9 3.7 %collective-permute-start = (bf16[3,1,64,256]{3,2,1,0:T(8,128)(2,1)}, bf16[3,1,64,256]{3,2,1,0:T(8,128)(2,1)}, u32[]{:S(2)}, u32[]{:S(2)}) collective-permute-start(bf16[3,1,64,256]{3,2,1,0:T(8,128)(2,1)} %get-tuple-element.23), channel_id=1, source_target_pairs={{0,4},{4,8},{8,12},{12,16},{16,20},{20,24},{24,28},{28,32},{32,36}... | collective-permute-start | bytes 294920 | tf_op jit(solution)/shard_map/ppermute | solution.py:75
  9.2 1.7 %multiply_bitcast_fusion.2 = (f32[16,64,256]{2,1,0:T(8,128)}, f32[16,64,256]{2,1,0:T(8,128)}, f32[16,64,256]{2,1,0:T(8,128)}) fusion(f32[3,16,64,256]{3,2,1,0:T(8,128)S(1)} %copy-done.1), kind=kLoop, calls=%fused_computation.20 | loop fusion | flops 786432 | bytes 6291456 | tf_op jit(solution)/shard_map/mul | solution.py:87
  13.6 4.3 %gather_fusion.3 = bf16[1024,128]{1,0:T(8,128)(2,1)} fusion(bf16[2048,128]{1,0:T(8,128)(2,1)S(1)} %reshape_squeeze.11, s32[1024]{0:T(1024)S(1)} %fusion.26), kind=kCustom, calls=%fused_computation.2.clone | custom fusion | bytes 528384 | tf_op jit(solution)/shard_map/jit(_take)/gather | solution.py:118
  17.9 3.2 %gather_fusion.2 = bf16[1024,128]{1,0:T(8,128)(2,1)S(1)} fusion(bf16[2048,128]{1,0:T(8,128)(2,1)S(1)} %reshape_squeeze.10, s32[1024]{0:T(1024)S(1)} %fusion.26), kind=kCustom, calls=%fused_computation.1.clone | custom fusion | bytes 528384 | tf_op jit(solution)/shard_map/jit(_take)/gather | solution.py:118
  21.2 1.7 %fusion.12 = f32[1024,384]{1,0:T(8,128)S(1)} fusion(f32[32,384]{1,0:T(8,128)} %param.15, s32[1024]{0:T(1024)S(1)} %copy-done.9), kind=kOutput, calls=%fused_computation.35 | convolution fusion | flops 151027712 | bytes 1626112 | tf_op jit(solution)/shard_map/dot_general | solution.py:113
  25.0 3.2 %gather_fusion.1 = bf16[1024,128]{1,0:T(8,128)(2,1)S(1)} fusion(bf16[2048,128]{1,0:T(8,128)(2,1)S(1)} %reshape_squeeze.9, s32[1024]{0:T(1024)S(1)} %fusion.26), kind=kCustom, calls=%fused_computation.clone | custom fusion | bytes 528384 | tf_op jit(solution)/shard_map/jit(_take)/gather | solution.py:118
  28.2 1.9 %fusion.8 = f32[32,128]{1,0:T(8,128)S(1)} fusion(f32[1024,384]{1,0:T(8,128)} %copy-done.3, bf16[1024,128]{1,0:T(8,128)(2,1)S(1)} %gather_fusion.1, s32[1024]{0:T(1024)S(1)} %select_reduce_fusion, pred[1024]{0:T(1024)(128)(4,1)S(1)} %compare_and_fusion), kind=kOutput, calls=%fused_computation.26 | convolution fusion | flops 50757632 | bytes 807936 | tf_op jit(solution)/shard_map/dot_general | solution.py:120
  30.8 4.9 %collective-permute-start.5 = (f32[2,1024]{1,0:T(2,128)S(1)}, f32[2,1024]{1,0:T(2,128)S(1)}, u32[]{:S(2)}, u32[]{:S(2)}) collective-permute-start(f32[2,1024]{1,0:T(2,128)S(1)} %pad_maximum_fusion.6), channel_id=1, source_target_pairs={{0,24},{4,28},{8,0},{12,4},{16,8},{20,12},{24,16},{28,20},{32,56},... | collective-permute-start | bytes 24584 | tf_op jit(solution)/shard_map/ppermute | solution.py:38
  37.1 3.8 %collective-permute-done.6 = f32[2,1024]{1,0:T(2,128)S(1)} collective-permute-done((f32[2,1024]{1,0:T(2,128)S(1)}, f32[2,1024]{1,0:T(2,128)S(1)}, u32[]{:S(2)}, u32[]{:S(2)}) %collective-permute-start.6) | collective-permute-done | bytes 8224 | tf_op jit(solution)/shard_map/ppermute | solution.py:38
  41.0 2.5 %collective-permute-start.8 = (f32[8,1024]{1,0:T(8,128)S(1)}, f32[8,1024]{1,0:T(8,128)S(1)}, u32[]{:S(2)}, u32[]{:S(2)}) collective-permute-start(f32[8,1024]{1,0:T(8,128)S(1)} %pad_maximum_fusion.5), channel_id=1, source_target_pairs={{0,96},{4,100},{8,104},{12,108},{16,112},{20,116},{24,120},{28,124... | collective-permute-start | bytes 98312 | tf_op jit(solution)/shard_map/ppermute | solution.py:38
  46.5 2.5 %collective-permute-done.9 = f32[8,1024]{1,0:T(8,128)S(1)} collective-permute-done((f32[8,1024]{1,0:T(8,128)S(1)}, f32[8,1024]{1,0:T(8,128)S(1)}, u32[]{:S(2)}, u32[]{:S(2)}) %collective-permute-start.9) | collective-permute-done | bytes 32800 | tf_op jit(solution)/shard_map/ppermute | solution.py:38
  50.4 3.2 %collective-permute-start.14 = (f32[32,384]{1,0:T(8,128)S(1)}, f32[32,384]{1,0:T(8,128)S(1)}, u32[]{:S(2)}, u32[]{:S(2)}) collective-permute-start(f32[32,384]{1,0:T(8,128)S(1)} %fusion.31), channel_id=1, source_target_pairs={{0,24},{4,28},{8,0},{12,4},{16,8},{20,12},{24,16},{28,20},{32,56},... | collective-permute-start | bytes 147464 | tf_op jit(solution)/shard_map/ppermute | solution.py:31
  56.6 4.8 %collective-permute-start.2 = (bf16[3,18,1,256]{3,2,1,0:T(2,128)(2,1)S(1)}, bf16[3,18,1,256]{3,2,1,0:T(2,128)(2,1)S(1)}, u32[]{:S(2)}, u32[]{:S(2)}) collective-permute-start(bf16[3,18,1,256]{3,2,1,0:T(2,128)(2,1)S(1)} %get-tuple-element.21), channel_id=1, source_target_pairs={{0,1},{1,2},{2,3},{4,5},{5,6},{6,7},{8,9},{9,10},{10,11},{12,13},{... | collective-permute-start | bytes 82952 | tf_op jit(solution)/shard_map/ppermute | solution.py:75
  61.6 3.1 %collective-permute-start.17 = (f32[32,384]{1,0:T(8,128)S(1)}, f32[32,384]{1,0:T(8,128)S(1)}, u32[]{:S(2)}, u32[]{:S(2)}) collective-permute-start(f32[32,384]{1,0:T(8,128)S(1)} %add_add_fusion.1), channel_id=1, source_target_pairs={{0,96},{4,100},{8,104},{12,108},{16,112},{20,116},{24,120},{28,124... | collective-permute-start | bytes 147464 | tf_op jit(solution)/shard_map/ppermute | solution.py:31
  64.8 1.8 %maximum_convert_fusion = f32[3,18,66,256]{3,2,1,0:T(8,128)S(1)} fusion(bf16[3,18,1,256]{3,2,1,0:T(2,128)(2,1)S(1)} %collective-permute-done.3, bf16[3,1,64,256]{3,2,1,0:T(8,128)(2,1)S(1)} %collective-permute-done.1, bf16[3,16,64,256]{3,2,1,0:T(8,128)(2,1)S(1)} %convert_element_type.39, bf16[3,1,64,256]{3,2,1,0:T(8,128)(2,1)} %collective-permute-done, ...), kind=kLoop, calls=%fused_computation.12 | loop fusion | flops 9123840 | bytes 5474304 | tf_op jit(solution)/shard_map/convert_element_type | solution.py:136
  66.8 3.5 %collective-permute-done.15 = f32[32,384]{1,0:T(8,128)S(1)} collective-permute-done((f32[32,384]{1,0:T(8,128)S(1)}, f32[32,384]{1,0:T(8,128)S(1)}, u32[]{:S(2)}, u32[]{:S(2)}) %collective-permute-start.15) | collective-permute-done | bytes 49184 | tf_op jit(solution)/shard_map/ppermute | solution.py:31
  70.4 1.6 %collective-permute-start.19 = (f32[32,384]{1,0:T(8,128)S(1)}, f32[32,384]{1,0:T(8,128)S(1)}, u32[]{:S(2)}, u32[]{:S(2)}) collective-permute-start(f32[32,384]{1,0:T(8,128)S(1)} %add_add_fusion), channel_id=1, source_target_pairs={{0,1},{1,2},{2,3},{3,0},{4,5},{5,6},{6,7},{7,4},{8,9},{9,10},{10,1... | collective-permute-start | bytes 147464 | tf_op jit(solution)/shard_map/ppermute | solution.py:31
  72.0 1.7 %collective-permute-start.20 = (f32[32,384]{1,0:T(8,128)S(1)}, f32[32,384]{1,0:T(8,128)S(1)}, u32[]{:S(2)}, u32[]{:S(2)}) collective-permute-start(f32[32,384]{1,0:T(8,128)S(1)} %add_add_fusion), channel_id=1, source_target_pairs={{0,3},{1,0},{2,1},{3,2},{4,7},{5,4},{6,5},{7,6},{8,11},{9,8},{10,9... | collective-permute-start | bytes 147464 | tf_op jit(solution)/shard_map/ppermute | solution.py:31
  73.7 2.0 %collective-permute-start.18 = (f32[32,384]{1,0:T(8,128)S(1)}, f32[32,384]{1,0:T(8,128)S(1)}, u32[]{:S(2)}, u32[]{:S(2)}) collective-permute-start(f32[32,384]{1,0:T(8,128)S(1)} %add_add_fusion), channel_id=1, source_target_pairs={{0,2},{1,3},{2,0},{3,1},{4,6},{5,7},{6,4},{7,5},{8,10},{9,11},{10,... | collective-permute-start | bytes 147464 | tf_op jit(solution)/shard_map/ppermute | solution.py:31
  75.7 4.9 %multiply_add_fusion = f32[3,16,64,256]{3,2,1,0:T(8,128)} fusion(f32[3,16,64,256]{3,2,1,0:T(8,128)S(1)} %copy-done.2, f32[3,18,66,256]{3,2,1,0:T(8,128)S(1)} %maximum_convert_fusion, f32[16,64,256]{2,1,0:T(8,128)S(1)} %copy-done.6, f32[16,64,256]{2,1,0:T(8,128)S(1)} %copy-done.5, f32[16,64,256]{2,1,0:T(8,128)S(1)} %copy-done.4), kind=kLoop, calls=%fused_computation.10 | loop fusion | flops 14942208 | bytes 22020096 | tf_op jit(solution)/shard_map/add | solution.py:91
  80.9 1.5 %convolution_convert_fusion = bf16[32,4096]{1,0:T(8,128)(2,1)S(1)} fusion(bf16[1024,4096]{1,0:T(8,128)(2,1)S(1)} %bitcast.18, f32[32,1024]{1,0:T(8,128)S(1)} %fusion.4), kind=kOutput, calls=%fused_computation.8 | convolution fusion | flops 268599296 | bytes 8781824 | tf_op jit(solution)/shard_map/dot_general | solution.py:126
  82.6 3.2 %gather_fusion = bf16[1024,128]{1,0:T(8,128)(2,1)S(1)} fusion(bf16[1024,128]{1,0:T(8,128)(2,1)S(1)} %reshape.69, s32[1024]{0:T(1024)S(1)} %fusion.25), kind=kCustom, calls=%fused_computation.3 | custom fusion | bytes 528384 | tf_op jit(solution)/shard_map/gather | solution.py:130
  88.3 2.4 %fusion.5 = f32[3,16,64,256]{3,2,1,0:T(8,128)} fusion(f32[3,16,64,256]{3,2,1,0:T(8,128)} %multiply_add_fusion, f32[1,16,64,256]{3,2,1,0:T(8,128)S(1)} %mul.150), kind=kLoop, calls=%fused_computation.17 | loop fusion | flops 262144 | bytes 3145728 | tf_op jit(solution)/shard_map/scatter-add | solution.py:144
  (93 shorter events, 20.0 us)
Async XLA Ops:
  0.6 80.0 %copy-start = (bf16[384,1024]{1,0:T(8,128)(2,1)S(1)}, bf16[384,1024]{1,0:T(8,128)(2,1)}, u32[]{:S(2)}) copy-start(bf16[384,1024]{1,0:T(8,128)(2,1)} %param.16) | copy-start | bytes 2359300
  3.6 50.8 %collective-permute-start.1 = (bf16[3,1,64,256]{3,2,1,0:T(8,128)(2,1)}, bf16[3,1,64,256]{3,2,1,0:T(8,128)(2,1)S(1)}, u32[]{:S(2)}, u32[]{:S(2)}) collective-permute-start(bf16[3,1,64,256]{3,2,1,0:T(8,128)(2,1)} %get-tuple-element.24), channel_id=1, source_target_pairs={{4,0},{8,4},{12,8},{16,12},{20,16},{24,20},{28,24},{32,28},{36,32}... | collective-permute-start | bytes 294920 | tf_op jit(solution)/shard_map/ppermute | solution.py:77
  4.9 49.5 %collective-permute-start = (bf16[3,1,64,256]{3,2,1,0:T(8,128)(2,1)}, bf16[3,1,64,256]{3,2,1,0:T(8,128)(2,1)}, u32[]{:S(2)}, u32[]{:S(2)}) collective-permute-start(bf16[3,1,64,256]{3,2,1,0:T(8,128)(2,1)} %get-tuple-element.23), channel_id=1, source_target_pairs={{0,4},{4,8},{8,12},{12,16},{16,20},{20,24},{24,28},{28,32},{32,36}... | collective-permute-start | bytes 294920 | tf_op jit(solution)/shard_map/ppermute | solution.py:75
  8.6 21.5 %collective-permute-start.4 = (f32[1,1024]{1,0:T(1,128)}, f32[1,1024]{1,0:T(1,128)}, u32[]{:S(2)}, u32[]{:S(2)}) collective-permute-start(f32[1,1024]{1,0:T(1,128)} %param.19), channel_id=1, source_target_pairs={{0,4},{4,0},{8,12},{12,8},{16,20},{20,16},{24,28},{28,24},{32,36},... | collective-permute-start | bytes 12296 | tf_op jit(solution)/shard_map/ppermute | solution.py:38
  30.8 6.3 %collective-permute-start.5 = (f32[2,1024]{1,0:T(2,128)S(1)}, f32[2,1024]{1,0:T(2,128)S(1)}, u32[]{:S(2)}, u32[]{:S(2)}) collective-permute-start(f32[2,1024]{1,0:T(2,128)S(1)} %pad_maximum_fusion.6), channel_id=1, source_target_pairs={{0,24},{4,28},{8,0},{12,4},{16,8},{20,12},{24,16},{28,20},{32,56},... | collective-permute-start | bytes 24584 | tf_op jit(solution)/shard_map/ppermute | solution.py:38
  35.7 5.2 %collective-permute-start.6 = (f32[2,1024]{1,0:T(2,128)S(1)}, f32[2,1024]{1,0:T(2,128)S(1)}, u32[]{:S(2)}, u32[]{:S(2)}) collective-permute-start(f32[2,1024]{1,0:T(2,128)S(1)} %pad_maximum_fusion.6), channel_id=1, source_target_pairs={{0,16},{4,20},{8,24},{12,28},{16,0},{20,4},{24,8},{28,12},{32,48},... | collective-permute-start | bytes 24584 | tf_op jit(solution)/shard_map/ppermute | solution.py:38
  35.7 5.2 %collective-permute-start.7 = (f32[2,1024]{1,0:T(2,128)S(1)}, f32[2,1024]{1,0:T(2,128)S(1)}, u32[]{:S(2)}, u32[]{:S(2)}) collective-permute-start(f32[2,1024]{1,0:T(2,128)S(1)} %pad_maximum_fusion.6), channel_id=1, source_target_pairs={{0,8},{4,12},{8,16},{12,20},{16,24},{20,28},{24,0},{28,4},{32,40},... | collective-permute-start | bytes 24584 | tf_op jit(solution)/shard_map/ppermute | solution.py:38
  41.0 5.4 %collective-permute-start.8 = (f32[8,1024]{1,0:T(8,128)S(1)}, f32[8,1024]{1,0:T(8,128)S(1)}, u32[]{:S(2)}, u32[]{:S(2)}) collective-permute-start(f32[8,1024]{1,0:T(8,128)S(1)} %pad_maximum_fusion.5), channel_id=1, source_target_pairs={{0,96},{4,100},{8,104},{12,108},{16,112},{20,116},{24,120},{28,124... | collective-permute-start | bytes 98312 | tf_op jit(solution)/shard_map/ppermute | solution.py:38
  43.5 5.4 %collective-permute-start.9 = (f32[8,1024]{1,0:T(8,128)S(1)}, f32[8,1024]{1,0:T(8,128)S(1)}, u32[]{:S(2)}, u32[]{:S(2)}) collective-permute-start(f32[8,1024]{1,0:T(8,128)S(1)} %pad_maximum_fusion.5), channel_id=1, source_target_pairs={{0,64},{4,68},{8,72},{12,76},{16,80},{20,84},{24,88},{28,92},{32,9... | collective-permute-start | bytes 98312 | tf_op jit(solution)/shard_map/ppermute | solution.py:38
  45.0 5.1 %collective-permute-start.10 = (f32[8,1024]{1,0:T(8,128)S(1)}, f32[8,1024]{1,0:T(8,128)S(1)}, u32[]{:S(2)}, u32[]{:S(2)}) collective-permute-start(f32[8,1024]{1,0:T(8,128)S(1)} %pad_maximum_fusion.5), channel_id=1, source_target_pairs={{0,32},{4,36},{8,40},{12,44},{16,48},{20,52},{24,56},{28,60},{32,6... | collective-permute-start | bytes 98312 | tf_op jit(solution)/shard_map/ppermute | solution.py:38
  46.4 3.9 %collective-permute-start.11 = (f32[32,384]{1,0:T(8,128)S(1)}, f32[32,384]{1,0:T(8,128)S(1)}, u32[]{:S(2)}, u32[]{:S(2)}) collective-permute-start(f32[32,384]{1,0:T(8,128)S(1)} %pad_maximum_fusion.4), channel_id=1, source_target_pairs={{0,4},{4,0},{8,12},{12,8},{16,20},{20,16},{24,28},{28,24},{32,36},... | collective-permute-start | bytes 147464 | tf_op jit(solution)/shard_map/ppermute | solution.py:30
  50.3 11.1 %collective-permute-start.13 = (f32[32,384]{1,0:T(8,128)S(1)}, f32[32,384]{1,0:T(8,128)S(1)}, u32[]{:S(2)}, u32[]{:S(2)}) collective-permute-start(f32[32,384]{1,0:T(8,128)S(1)} %fusion.31), channel_id=1, source_target_pairs={{0,8},{4,12},{8,16},{12,20},{16,24},{20,28},{24,0},{28,4},{32,40},... | collective-permute-start | bytes 147464 | tf_op jit(solution)/shard_map/ppermute | solution.py:31
  50.4 11.0 %collective-permute-start.14 = (f32[32,384]{1,0:T(8,128)S(1)}, f32[32,384]{1,0:T(8,128)S(1)}, u32[]{:S(2)}, u32[]{:S(2)}) collective-permute-start(f32[32,384]{1,0:T(8,128)S(1)} %fusion.31), channel_id=1, source_target_pairs={{0,24},{4,28},{8,0},{12,4},{16,8},{20,12},{24,16},{28,20},{32,56},... | collective-permute-start | bytes 147464 | tf_op jit(solution)/shard_map/ppermute | solution.py:31
  53.6 7.8 %collective-permute-start.12 = (f32[32,384]{1,0:T(8,128)S(1)}, f32[32,384]{1,0:T(8,128)S(1)}, u32[]{:S(2)}, u32[]{:S(2)}) collective-permute-start(f32[32,384]{1,0:T(8,128)S(1)} %fusion.31), channel_id=1, source_target_pairs={{0,16},{4,20},{8,24},{12,28},{16,0},{20,4},{24,8},{28,12},{32,48},... | collective-permute-start | bytes 147464 | tf_op jit(solution)/shard_map/ppermute | solution.py:31
  55.2 9.5 %collective-permute-start.3 = (bf16[3,18,1,256]{3,2,1,0:T(2,128)(2,1)S(1)}, bf16[3,18,1,256]{3,2,1,0:T(2,128)(2,1)S(1)}, u32[]{:S(2)}, u32[]{:S(2)}) collective-permute-start(bf16[3,18,1,256]{3,2,1,0:T(2,128)(2,1)S(1)} %get-tuple-element.22), channel_id=1, source_target_pairs={{1,0},{2,1},{3,2},{5,4},{6,5},{7,6},{9,8},{10,9},{11,10},{13,12},{... | collective-permute-start | bytes 82952 | tf_op jit(solution)/shard_map/ppermute | solution.py:77
  56.5 19.1 %copy-start.2 = (f32[3,16,64,256]{3,2,1,0:T(8,128)S(1)}, f32[3,16,64,256]{3,2,1,0:T(8,128)}, u32[]{:S(2)}) copy-start(f32[3,16,64,256]{3,2,1,0:T(8,128)} %param.14) | copy-start | bytes 9437188
  56.5 19.1 %copy-start.4 = (f32[16,64,256]{2,1,0:T(8,128)S(1)}, f32[16,64,256]{2,1,0:T(8,128)}, u32[]{:S(2)}) copy-start(f32[16,64,256]{2,1,0:T(8,128)} %get-tuple-element.18) | copy-start | bytes 3145732
  56.6 8.2 %collective-permute-start.2 = (bf16[3,18,1,256]{3,2,1,0:T(2,128)(2,1)S(1)}, bf16[3,18,1,256]{3,2,1,0:T(2,128)(2,1)S(1)}, u32[]{:S(2)}, u32[]{:S(2)}) collective-permute-start(bf16[3,18,1,256]{3,2,1,0:T(2,128)(2,1)S(1)} %get-tuple-element.21), channel_id=1, source_target_pairs={{0,1},{1,2},{2,3},{4,5},{5,6},{6,7},{8,9},{9,10},{10,11},{12,13},{... | collective-permute-start | bytes 82952 | tf_op jit(solution)/shard_map/ppermute | solution.py:75
  61.4 5.4 %collective-permute-start.16 = (f32[32,384]{1,0:T(8,128)S(1)}, f32[32,384]{1,0:T(8,128)S(1)}, u32[]{:S(2)}, u32[]{:S(2)}) collective-permute-start(f32[32,384]{1,0:T(8,128)S(1)} %add_add_fusion.1), channel_id=1, source_target_pairs={{0,32},{4,36},{8,40},{12,44},{16,48},{20,52},{24,56},{28,60},{32,6... | collective-permute-start | bytes 147464 | tf_op jit(solution)/shard_map/ppermute | solution.py:31
  61.6 5.2 %collective-permute-start.17 = (f32[32,384]{1,0:T(8,128)S(1)}, f32[32,384]{1,0:T(8,128)S(1)}, u32[]{:S(2)}, u32[]{:S(2)}) collective-permute-start(f32[32,384]{1,0:T(8,128)S(1)} %add_add_fusion.1), channel_id=1, source_target_pairs={{0,96},{4,100},{8,104},{12,108},{16,112},{20,116},{24,120},{28,124... | collective-permute-start | bytes 147464 | tf_op jit(solution)/shard_map/ppermute | solution.py:31
  64.7 5.6 %collective-permute-start.15 = (f32[32,384]{1,0:T(8,128)S(1)}, f32[32,384]{1,0:T(8,128)S(1)}, u32[]{:S(2)}, u32[]{:S(2)}) collective-permute-start(f32[32,384]{1,0:T(8,128)S(1)} %add_add_fusion.1), channel_id=1, source_target_pairs={{0,64},{4,68},{8,72},{12,76},{16,80},{20,84},{24,88},{28,92},{32,9... | collective-permute-start | bytes 147464 | tf_op jit(solution)/shard_map/ppermute | solution.py:31
  70.4 10.3 %collective-permute-start.19 = (f32[32,384]{1,0:T(8,128)S(1)}, f32[32,384]{1,0:T(8,128)S(1)}, u32[]{:S(2)}, u32[]{:S(2)}) collective-permute-start(f32[32,384]{1,0:T(8,128)S(1)} %add_add_fusion), channel_id=1, source_target_pairs={{0,1},{1,2},{2,3},{3,0},{4,5},{5,6},{6,7},{7,4},{8,9},{9,10},{10,1... | collective-permute-start | bytes 147464 | tf_op jit(solution)/shard_map/ppermute | solution.py:31
  72.0 8.6 %collective-permute-start.20 = (f32[32,384]{1,0:T(8,128)S(1)}, f32[32,384]{1,0:T(8,128)S(1)}, u32[]{:S(2)}, u32[]{:S(2)}) collective-permute-start(f32[32,384]{1,0:T(8,128)S(1)} %add_add_fusion), channel_id=1, source_target_pairs={{0,3},{1,0},{2,1},{3,2},{4,7},{5,4},{6,5},{7,6},{8,11},{9,8},{10,9... | collective-permute-start | bytes 147464 | tf_op jit(solution)/shard_map/ppermute | solution.py:31
  73.7 7.0 %collective-permute-start.18 = (f32[32,384]{1,0:T(8,128)S(1)}, f32[32,384]{1,0:T(8,128)S(1)}, u32[]{:S(2)}, u32[]{:S(2)}) collective-permute-start(f32[32,384]{1,0:T(8,128)S(1)} %add_add_fusion), channel_id=1, source_target_pairs={{0,2},{1,3},{2,0},{3,1},{4,6},{5,7},{6,4},{7,5},{8,10},{9,11},{10,... | collective-permute-start | bytes 147464 | tf_op jit(solution)/shard_map/ppermute | solution.py:31
  (14 other events, 117.2 us)

commit v2 on v1

--- a/solution.py
+++ b/solution.py
@@ -1,7 +1,11 @@
 import jax
 import jax.numpy as jnp
 from jax import lax
+from jax.experimental import pallas as pl
+from jax.experimental.pallas import tpu as pltpu
 from jax.sharding import PartitionSpec as P
+
+MESH = pl.DeviceIdType.MESH
 
 TILE = 128
 R = 32
@@ -62,6 +66,92 @@
     for axis, stride, n in mesh_rings():
         parts = ring_gather(parts, axis, stride, n)
     return parts
+
+
+def ring_rounds(slab, cross):
+    return [(0, 1, 2), (0, 2, 4), (0, 8, slab // 8), (1, 1, cross)]
+
+
+def partner(me, stride, n, shift):
+    pos = (me // stride) % n
+    return me - pos * stride + ((pos + shift) % n) * stride
+
+
+def reduce_gather_kernel(rounds, per_ref, st_ref, pooled_ref, states_ref, held, sends, recvs, st_sends, st_recvs):
+    here = (lax.axis_index("slab"), lax.axis_index("cross"))
+
+    def device(axis, other):
+        return (other, here[1]) if axis == 0 else (here[0], other)
+
+    barrier = pltpu.get_barrier_semaphore()
+    count = 0
+    for axis, stride, n in rounds:
+        for j in range(1, n):
+            pl.semaphore_signal(barrier, inc=1, device_id=device(axis, partner(here[axis], stride, n, j)), device_id_type=MESH)
+            count += 1
+    pl.semaphore_wait(barrier, count)
+
+    me = here[0]
+    states_ref[pl.ds(me, 1)] = st_ref[...][None]
+    pooled_ref[...] = per_ref[...]
+    for r, (axis, stride, n) in enumerate(rounds):
+        if n == 1:
+            continue
+        copies = []
+        for j in range(1, n):
+            dev = device(axis, partner(here[axis], stride, n, j))
+            copy = pltpu.make_async_remote_copy(
+                src_ref=pooled_ref,
+                dst_ref=held.at[r, j - 1],
+                send_sem=sends.at[r, j - 1],
+                recv_sem=recvs.at[r, j - 1],
+                device_id=dev,
+                device_id_type=MESH,
+            )
+            copy.start()
+            copies.append(copy)
+            if axis == 0:
+                rows = pl.ds(me - me % stride, stride)
+                block = pltpu.make_async_remote_copy(
+                    src_ref=states_ref.at[rows],
+                    dst_ref=states_ref.at[rows],
+                    send_sem=st_sends.at[r, j - 1],
+                    recv_sem=st_recvs.at[r, j - 1],
+                    device_id=dev,
+                    device_id_type=MESH,
+                )
+                block.start()
+                copies.append(block)
+        for copy in copies:
+            copy.wait()
+        if n == 2:
+            total = pooled_ref[...] + held[r, 0]
+        else:
+            total = (pooled_ref[...] + held[r, 1]) + (held[r, 0] + held[r, 2])
+        pooled_ref[...] = total
+
+
+def reduce_gather(per_rotor, rotor_states):
+    slab, cross = lax.axis_size("slab"), lax.axis_size("cross")
+    rounds = ring_rounds(slab, cross)
+    vmem = pl.BlockSpec(memory_space=pltpu.VMEM)
+    return pl.pallas_call(
+        lambda *refs: reduce_gather_kernel(rounds, *refs),
+        out_shape=(
+            jax.ShapeDtypeStruct(per_rotor.shape, jnp.float32),
+            jax.ShapeDtypeStruct((slab,) + rotor_states.shape, jnp.float32),
+        ),
+        in_specs=[vmem, vmem],
+        out_specs=(vmem, vmem),
+        scratch_shapes=[
+            pltpu.VMEM((len(rounds), 3) + per_rotor.shape, jnp.float32),
+            pltpu.SemaphoreType.DMA((len(rounds), 3)),
+            pltpu.SemaphoreType.DMA((len(rounds), 3)),
+            pltpu.SemaphoreType.DMA((len(rounds), 3)),
+            pltpu.SemaphoreType.DMA((len(rounds), 3)),
+        ],
+        compiler_params=pltpu.CompilerParams(collective_id=0, has_side_effects=True),
+    )(per_rotor, rotor_states)
 
 
 def extended(cells, sides, width):
@@ -105,7 +195,6 @@
 ):
     local_x, local_y, local_z = (velocity.shape[1], velocity.shape[2], velocity.shape[3])
     tile_count = local_x * local_y * local_z // TILE
-    all_states = slab_gather(rotor_states)
     rotor_hot = (entry_rotor == jnp.arange(R, dtype=jnp.int32)[None, :]).astype(jnp.int32)
     slots = jnp.sum(rotor_hot * slot_of_rotor[None, :], axis=1)
     sub_range = jnp.arange(NSUB, dtype=jnp.int32)
@@ -119,7 +208,8 @@
         weighted = gains[:, c * TILE:(c + 1) * TILE] * picked
         per_rotor.append(jnp.dot(slot_hot.T, weighted, precision=lax.Precision.HIGHEST))
     per_rotor = jnp.concatenate(per_rotor, axis=1)
-    pooled = all_sum(per_rotor)
+    pooled, all_states = reduce_gather(per_rotor, rotor_states)
+    all_states = all_states.reshape(-1, rotor_states.shape[1])
     pooled_b = (pooled * pool_scale).astype(jnp.bfloat16)
     drive = jnp.dot(pooled_b, w_in, preferred_element_type=jnp.float32)
     all_new = all_states + state_step * (drive - decay[None, :] * all_states)

time: 91 us -> 88.4 us (0.971)
  Pallas kernels: 0 us -> 26.4 us
  starting transfers between devices: 35.7 us -> 11.4 us
  waiting for transfers between devices: 11.7 us -> 0.01 us
  matrix products: 8.67 us -> 14 us
  local copies, waits for them, and re-layouts: 18.5 us -> 22.1 us
  other arithmetic: 14.9 us -> 13 us
    pallas_call x0 -> x1, Pallas kernels: none -> 26.4 us  [reduce_gather(): pl.pallas_call(lambda *refs: reduce_gather_kernel(rounds, *refs), out_sha...]
    ppermute x17 -> x0, starting transfers between devices: 24.6 us -> none  [the longest x9 12.7 us: ring_sum(): lax.ppermute(value, axis, ring_perm(size, stride, n, j))]
    ppermute x17 -> x0, waiting for transfers between devices: 11.7 us -> none  [the longest x7 7.92 us: ring_gather(): lax.ppermute(value, axis, ring_perm(size, stride, n, j))]
    dot_general x1, matrix products: 1.54 us -> 4.93 us  [on_device(): jnp.dot(all_new.astype(jnp.bfloat16), w_out, preferred_element_type=jnp.f...]
    unnamed x34 -> x30, local copies, waits for them, and re-layouts: 0.1 us -> 2.48 us
    scatter-add x1, other arithmetic: 2.35 us -> 0.26 us  [on_device(): advanced.at[0]]
    mul x1, local copies, waits for them, and re-layouts: 0.29 us -> 1.54 us  [on_device(): -force_scale * forcing.reshape(local_x, local_y, local_z)]
    dot_general x1, matrix products: 1.52 us -> 2.5 us  [on_device(): forcing = jnp.dot(tile_hot, rows, preferred_element_type=jnp.float32)]
  transfers between devices with their start and end apart: 21 -> 4, of which waited for: 6 -> 0; matrix products, arithmetic and copies ran while one was open for 32% -> 40% of each run, Pallas kernels for 0% -> 30%
where the time goes in v2:
time: 88.4 us; the launch traced here: 87.9 us
  Pallas kernels  26.4 us (30%)
  local copies, waits for them, and re-layouts  22.1 us (25%)
  matrix products  14 us (16%)
  other arithmetic  13 us (15%)
  starting transfers between devices  11.4 us (13%)
  between operations  0.98 us (1%)
    pallas_call x1, Pallas kernels, reduce_gather(): pl.pallas_call(lambda *refs: reduce_gather_kernel(rounds, *refs), out_sha...  26.4 us
    gather x3, local copies, waits for them, and re-layouts, on_device(): jnp.take(cells, entry_tile, axis=0).astype(jnp.bfloat16).astype(jnp.float32)  10.7 us
    ppermute x2, starting transfers between devices, extended(): lax.ppermute(tail, axis, [(i, (i + 1) % count) for i in range(ends)])  8.84 us
    dot_general x1, matrix products, on_device(): jnp.dot(all_new.astype(jnp.bfloat16), w_out, preferred_element_type=jnp.f...  4.93 us
    add x1, other arithmetic, combine_terms(): return velocity + time_step * (viscosity * laplace - advect)  4.81 us
    dot_general x3, matrix products, on_device(): jnp.dot(slot_hot.T, weighted, precision=lax.Precision.HIGHEST)  3.67 us
    gather x1, local copies, waits for them, and re-layouts, on_device(): rows = all_sources.reshape(R * NSUB, TILE)[slots * NSUB + entry_sub]  3.21 us
    ppermute x2, starting transfers between devices, extended(): lax.ppermute(head, axis, [((i + 1) % count, i) for i in range(ends)])  2.56 us
  transfers between devices with their start and end apart: 4, of which 0 were waited for; matrix products, arithmetic and copies ran while one was open for 40% of the time, Pallas kernels for 30%

profile of v2, /device:TPU:0, one launch (start us, length us, event | category | flops | bytes accessed | tf_op | source)
XLA Modules:
  0.0 87.9 jit_solution(12604856158036851591)
XLA Ops:
  0.7 2.3 %convert_element_type.39 = bf16[3,16,64,256]{3,2,1,0:T(8,128)(2,1)S(1)} convert(f32[3,16,64,256]{3,2,1,0:T(8,128)} %param.14) | non-fusion elementwise | flops 786432 | bytes 4718592 | tf_op jit(solution)/shard_map/convert_element_type | solution.py:226
  3.6 1.3 %collective-permute-start.1 = (bf16[3,1,64,256]{3,2,1,0:T(8,128)(2,1)}, bf16[3,1,64,256]{3,2,1,0:T(8,128)(2,1)S(1)}, u32[]{:S(2)}, u32[]{:S(2)}) collective-permute-start(bf16[3,1,64,256]{3,2,1,0:T(8,128)(2,1)} %get-tuple-element.28), channel_id=1, source_target_pairs={{4,0},{8,4},{12,8},{16,12},{20,16},{24,20},{28,24},{32,28},{36,32}... | collective-permute-start | bytes 294920 | tf_op jit(solution)/shard_map/ppermute | solution.py:167
  4.9 3.7 %collective-permute-start = (bf16[3,1,64,256]{3,2,1,0:T(8,128)(2,1)}, bf16[3,1,64,256]{3,2,1,0:T(8,128)(2,1)}, u32[]{:S(2)}, u32[]{:S(2)}) collective-permute-start(bf16[3,1,64,256]{3,2,1,0:T(8,128)(2,1)} %get-tuple-element.27), channel_id=1, source_target_pairs={{0,4},{4,8},{8,12},{12,16},{16,20},{20,24},{24,28},{28,32},{32,36}... | collective-permute-start | bytes 294920 | tf_op jit(solution)/shard_map/ppermute | solution.py:165
  8.6 1.7 %multiply_bitcast_fusion.2 = (f32[16,64,256]{2,1,0:T(8,128)}, f32[16,64,256]{2,1,0:T(8,128)}, f32[16,64,256]{2,1,0:T(8,128)}) fusion(f32[3,16,64,256]{3,2,1,0:T(8,128)S(1)} %copy-done.1), kind=kLoop, calls=%fused_computation.20 | loop fusion | flops 786432 | bytes 6291456 | tf_op jit(solution)/shard_map/mul | solution.py:177
  10.3 1.2 %fusion.31 = (bf16[1,16,64,256]{3,2,1,0:T(8,128)(2,1)}, bf16[1,16,64,256]{3,2,1,0:T(8,128)(2,1)}, bf16[1,16,64,256]{3,2,1,0:T(8,128)(2,1)S(1)}) fusion(f32[3,16,64,256]{3,2,1,0:T(8,128)S(1)} %copy-done.1), kind=kLoop, calls=%fused_computation.66 | loop fusion | bytes 3145728 | tf_op jit(solution)/shard_map/slice | solution.py:177
  11.7 1.2 %reshape_squeeze.10 = bf16[2048,128]{1,0:T(8,128)(2,1)S(1)} reshape(bf16[1,16,64,256]{3,2,1,0:T(8,128)(2,1)} %get-tuple-element.20) | data formatting | bytes 1048576 | tf_op jit(solution)/shard_map/reshape;squeeze | solution.py:206
  13.0 4.3 %gather_fusion.3 = bf16[1024,128]{1,0:T(8,128)(2,1)} fusion(bf16[2048,128]{1,0:T(8,128)(2,1)S(1)} %reshape_squeeze.11, s32[1024]{0:T(1024)S(1)} %fusion.26), kind=kCustom, calls=%fused_computation.2.clone | custom fusion | bytes 528384 | tf_op jit(solution)/shard_map/jit(_take)/gather | solution.py:207
  17.2 3.2 %gather_fusion.2 = bf16[1024,128]{1,0:T(8,128)(2,1)S(1)} fusion(bf16[2048,128]{1,0:T(8,128)(2,1)S(1)} %reshape_squeeze.10, s32[1024]{0:T(1024)S(1)} %fusion.26), kind=kCustom, calls=%fused_computation.1.clone | custom fusion | bytes 528384 | tf_op jit(solution)/shard_map/jit(_take)/gather | solution.py:207
  20.5 1.7 %fusion.12 = f32[1024,384]{1,0:T(8,128)S(1)} fusion(f32[32,384]{1,0:T(8,128)} %param.15, s32[1024]{0:T(1024)S(1)} %copy-done.9), kind=kOutput, calls=%fused_computation.35 | convolution fusion | flops 151027712 | bytes 1626112 | tf_op jit(solution)/shard_map/dot_general | solution.py:202
  23.2 0.9 %fusion.7 = f32[32,128]{1,0:T(8,128)S(1)} fusion(f32[1024,384]{1,0:T(8,128)S(1)} %fusion.12, bf16[1024,128]{1,0:T(8,128)(2,1)S(1)} %gather_fusion.2, s32[1024]{0:T(1024)S(1)} %select_reduce_fusion, pred[1024]{0:T(1024)(128)(4,1)S(1)} %compare_and_fusion), kind=kOutput, calls=%fused_computation.24 | convolution fusion | flops 50757632 | bytes 807936 | tf_op jit(solution)/shard_map/dot_general | solution.py:209
  24.3 3.2 %gather_fusion.1 = bf16[1024,128]{1,0:T(8,128)(2,1)S(1)} fusion(bf16[2048,128]{1,0:T(8,128)(2,1)S(1)} %reshape_squeeze.9, s32[1024]{0:T(1024)S(1)} %fusion.26), kind=kCustom, calls=%fused_computation.clone | custom fusion | bytes 528384 | tf_op jit(solution)/shard_map/jit(_take)/gather | solution.py:207
  27.5 1.9 %fusion.8 = f32[32,128]{1,0:T(8,128)S(1)} fusion(f32[1024,384]{1,0:T(8,128)} %copy-done.3, bf16[1024,128]{1,0:T(8,128)(2,1)S(1)} %gather_fusion.1, s32[1024]{0:T(1024)S(1)} %select_reduce_fusion, pred[1024]{0:T(1024)(128)(4,1)S(1)} %compare_and_fusion), kind=kOutput, calls=%fused_computation.26 | convolution fusion | flops 50757632 | bytes 807936 | tf_op jit(solution)/shard_map/dot_general | solution.py:209
  30.1 26.4 %shard_map.113 = (f32[32,384]{1,0:T(8,128)}, f32[32,1,1024]{2,1,0:T(1,128)}) custom-call(f32[32,384]{1,0:T(8,128)} %pad_maximum_fusion.3.refs_0_, f32[1,1024]{1,0:T(1,128)} %refs_1_.1), custom_call_target="tpu_custom_call" | custom-call | tf_op jit(solution)/shard_map/pallas_call | solution.py:138
  56.5 1.2 %fusion.4 = f32[32,1024]{1,0:T(8,128)S(1)} fusion(bf16[384,1024]{1,0:T(8,128)(2,1)S(1)} %copy-done, f32[32,1,1024]{2,1,0:T(1,128)} %get-tuple-element.17, f32[1024]{0:T(1024)S(1)} %copy-done.12, f32[32,384]{1,0:T(8,128)} %get-tuple-element.18), kind=kOutput, calls=%fused_computation.15 | convolution fusion | flops 25321472 | bytes 1101824 | tf_op jit(solution)/shard_map/dot_general | solution.py:214
  57.7 4.9 %convolution_convert_fusion = bf16[32,4096]{1,0:T(8,128)(2,1)S(1)} fusion(bf16[1024,4096]{1,0:T(8,128)(2,1)} %param.17, f32[32,1024]{1,0:T(8,128)S(1)} %fusion.4), kind=kOutput, calls=%fused_computation.8 | convolution fusion | flops 268599296 | bytes 8781824 | tf_op jit(solution)/shard_map/dot_general | solution.py:216
  62.7 3.2 %gather_fusion = bf16[1024,128]{1,0:T(8,128)(2,1)S(1)} fusion(bf16[1024,128]{1,0:T(8,128)(2,1)S(1)} %reshape.73, s32[1024]{0:T(1024)S(1)} %fusion.25), kind=kCustom, calls=%fused_computation.3 | custom fusion | bytes 528384 | tf_op jit(solution)/shard_map/gather | solution.py:220
  66.0 2.5 %fusion.2 = f32[2048,128]{1,0:T(8,128)} fusion(bf16[1024,128]{1,0:T(8,128)(2,1)S(1)} %gather_fusion, s32[1024]{0:T(1024)S(1)} %copy-done.11), kind=kOutput, calls=%fused_computation.11 | convolution fusion | flops 539230208 | bytes 1314816 | tf_op jit(solution)/shard_map/dot_general | solution.py:222
  68.5 1.5 %pad_maximum_fusion.2 = (bf16[3,18,1,256]{3,2,1,0:T(2,128)(2,1)}, bf16[3,18,1,256]{3,2,1,0:T(2,128)(2,1)}) fusion(bf16[3,1,64,256]{3,2,1,0:T(8,128)(2,1)S(1)} %collective-permute-done.1, bf16[3,16,64,256]{3,2,1,0:T(8,128)(2,1)S(1)} %convert_element_type.39, bf16[3,1,64,256]{3,2,1,0:T(8,128)(2,1)} %collective-permute-done), kind=kLoop, calls=%fused_computation.52 | loop fusion | flops 165888 | bytes 1824768 | tf_op jit(solution)/shard_map/slice | solution.py:162
  69.9 1.3 %collective-permute-start.3 = (bf16[3,18,1,256]{3,2,1,0:T(2,128)(2,1)}, bf16[3,18,1,256]{3,2,1,0:T(2,128)(2,1)}, u32[]{:S(2)}, u32[]{:S(2)}) collective-permute-start(bf16[3,18,1,256]{3,2,1,0:T(2,128)(2,1)} %get-tuple-element.26), channel_id=1, source_target_pairs={{1,0},{2,1},{3,2},{5,4},{6,5},{7,6},{9,8},{10,9},{11,10},{13,12},{... | collective-permute-start | bytes 82952 | tf_op jit(solution)/shard_map/ppermute | solution.py:167
  71.2 5.2 %collective-permute-start.2 = (bf16[3,18,1,256]{3,2,1,0:T(2,128)(2,1)}, bf16[3,18,1,256]{3,2,1,0:T(2,128)(2,1)}, u32[]{:S(2)}, u32[]{:S(2)}) collective-permute-start(bf16[3,18,1,256]{3,2,1,0:T(2,128)(2,1)} %get-tuple-element.25), channel_id=1, source_target_pairs={{0,1},{1,2},{2,3},{4,5},{5,6},{6,7},{8,9},{9,10},{10,11},{12,13},{... | collective-permute-start | bytes 82952 | tf_op jit(solution)/shard_map/ppermute | solution.py:165
  77.0 1.5 %mul.150 = f32[1,16,64,256]{3,2,1,0:T(8,128)S(1)} reshape(f32[2048,128]{1,0:T(8,128)} %fusion.2) | data formatting | bytes 2097152 | tf_op jit(solution)/shard_map/mul | solution.py:234
  78.6 1.8 %maximum_convert_fusion = f32[3,18,66,256]{3,2,1,0:T(8,128)S(1)} fusion(bf16[3,18,1,256]{3,2,1,0:T(2,128)(2,1)} %collective-permute-done.3, bf16[3,1,64,256]{3,2,1,0:T(8,128)(2,1)S(1)} %collective-permute-done.1, bf16[3,16,64,256]{3,2,1,0:T(8,128)(2,1)S(1)} %convert_element_type.39, bf16[3,1,64,256]{3,2,1,0:T(8,128)(2,1)} %collective-permute-done, ...), kind=kLoop, calls=%fused_computation.12 | loop fusion | flops 9123840 | bytes 5474304 | tf_op jit(solution)/shard_map/convert_element_type | solution.py:226
  81.1 4.8 %multiply_add_fusion = f32[3,16,64,256]{3,2,1,0:T(8,128)S(1)} fusion(f32[3,16,64,256]{3,2,1,0:T(8,128)S(1)} %copy-done.2, f32[3,18,66,256]{3,2,1,0:T(8,128)S(1)} %maximum_convert_fusion, f32[16,64,256]{2,1,0:T(8,128)} %get-tuple-element.24, f32[16,64,256]{2,1,0:T(8,128)S(1)} %copy-done.6, f32[16,64,256]{2,1,0:T(8,128)S(1)} %copy-done.5), kind=kLoop, calls=%fused_computation.10 | loop fusion | flops 14942208 | bytes 22020096 | tf_op jit(solution)/shard_map/add | solution.py:181
  86.2 1.7 %copy-done.4 = f32[3,16,64,256]{3,2,1,0:T(8,128)} copy-done((f32[3,16,64,256]{3,2,1,0:T(8,128)}, f32[3,16,64,256]{3,2,1,0:T(8,128)S(1)}, u32[]{:S(2)}) %copy-start.4) | copy-done | bytes 3145752
  (45 shorter events, 4.5 us)
Async XLA Ops:
  0.6 55.8 %copy-start = (bf16[384,1024]{1,0:T(8,128)(2,1)S(1)}, bf16[384,1024]{1,0:T(8,128)(2,1)}, u32[]{:S(2)}) copy-start(bf16[384,1024]{1,0:T(8,128)(2,1)} %param.16) | copy-start | bytes 2359300
  0.6 7.9 %copy-start.1 = (f32[3,16,64,256]{3,2,1,0:T(8,128)S(1)}, f32[3,16,64,256]{3,2,1,0:T(8,128)}, u32[]{:S(2)}) copy-start(f32[3,16,64,256]{3,2,1,0:T(8,128)} %param.14) | copy-start | bytes 9437188
  3.6 64.9 %collective-permute-start.1 = (bf16[3,1,64,256]{3,2,1,0:T(8,128)(2,1)}, bf16[3,1,64,256]{3,2,1,0:T(8,128)(2,1)S(1)}, u32[]{:S(2)}, u32[]{:S(2)}) collective-permute-start(bf16[3,1,64,256]{3,2,1,0:T(8,128)(2,1)} %get-tuple-element.28), channel_id=1, source_target_pairs={{4,0},{8,4},{12,8},{16,12},{20,16},{24,20},{28,24},{32,28},{36,32}... | collective-permute-start | bytes 294920 | tf_op jit(solution)/shard_map/ppermute | solution.py:167
  4.9 6.6 %copy-start.10 = (s32[1024]{0:T(1024)S(1)}, s32[1024]{0:T(1024)}, u32[]{:S(2)}) copy-start(s32[1024]{0:T(1024)} %param.22) | copy-start | bytes 12292
  4.9 63.6 %collective-permute-start = (bf16[3,1,64,256]{3,2,1,0:T(8,128)(2,1)}, bf16[3,1,64,256]{3,2,1,0:T(8,128)(2,1)}, u32[]{:S(2)}, u32[]{:S(2)}) collective-permute-start(bf16[3,1,64,256]{3,2,1,0:T(8,128)(2,1)} %get-tuple-element.27), channel_id=1, source_target_pairs={{0,4},{4,8},{8,12},{12,16},{16,20},{20,24},{24,28},{28,32},{32,36}... | collective-permute-start | bytes 294920 | tf_op jit(solution)/shard_map/ppermute | solution.py:165
  11.7 8.7 %copy-start.9 = (s32[1024]{0:T(1024)S(1)}, s32[1024]{0:T(1024)}, u32[]{:S(2)}) copy-start(s32[1024]{0:T(1024)} %param.23) | copy-start | bytes 12292
  13.0 9.2 %copy-start.13 = (s32[1024,1]{0,1:T(1,128)S(1)}, s32[1024,1]{0,1:T(1,128)}, u32[]{:S(2)}) copy-start(s32[1024,1]{0,1:T(1,128)} %param.21) | copy-start | bytes 12292
  13.0 9.2 %copy-start.14 = (s32[32]{0:T(128)S(1)}, s32[32]{0:T(128)}, u32[]{:S(2)}) copy-start(s32[32]{0:T(128)} %param.20) | copy-start | bytes 388
  17.2 5.1 %copy-start.8 = (bf16[1024,128]{1,0:T(8,128)(2,1)S(1)}, bf16[1024,128]{1,0:T(8,128)(2,1)}, u32[]{:S(2)}) copy-start(bf16[1024,128]{1,0:T(8,128)(2,1)} %gather_fusion.3) | copy-start | bytes 786436
  20.5 3.6 %copy-start.7 = (bf16[1,16,64,256]{3,2,1,0:T(8,128)(2,1)S(1)}, bf16[1,16,64,256]{3,2,1,0:T(8,128)(2,1)}, u32[]{:S(2)}) copy-start(bf16[1,16,64,256]{3,2,1,0:T(8,128)(2,1)} %get-tuple-element.19) | copy-start | bytes 1572868
  22.2 1.9 %copy-start.3 = (f32[1024,384]{1,0:T(8,128)}, f32[1024,384]{1,0:T(8,128)S(1)}, u32[]{:S(2)}) copy-start(f32[1024,384]{1,0:T(8,128)S(1)} %fusion.12) | copy-start | bytes 4718596
  24.3 32.2 %copy-start.12 = (f32[1024]{0:T(1024)S(1)}, f32[1024]{0:T(1024)}, u32[]{:S(2)}) copy-start(f32[1024]{0:T(1024)} %param.18) | copy-start | bytes 12292
  57.7 8.3 %copy-start.11 = (s32[1024]{0:T(1024)S(1)}, s32[1024]{0:T(1024)}, u32[]{:S(2)}) copy-start(s32[1024]{0:T(1024)} %param.22) | copy-start | bytes 12292
  69.9 8.6 %collective-permute-start.3 = (bf16[3,18,1,256]{3,2,1,0:T(2,128)(2,1)}, bf16[3,18,1,256]{3,2,1,0:T(2,128)(2,1)}, u32[]{:S(2)}, u32[]{:S(2)}) collective-permute-start(bf16[3,18,1,256]{3,2,1,0:T(2,128)(2,1)} %get-tuple-element.26), channel_id=1, source_target_pairs={{1,0},{2,1},{3,2},{5,4},{6,5},{7,6},{9,8},{10,9},{11,10},{13,12},{... | collective-permute-start | bytes 82952 | tf_op jit(solution)/shard_map/ppermute | solution.py:167
  71.2 7.4 %collective-permute-start.2 = (bf16[3,18,1,256]{3,2,1,0:T(2,128)(2,1)}, bf16[3,18,1,256]{3,2,1,0:T(2,128)(2,1)}, u32[]{:S(2)}, u32[]{:S(2)}) collective-permute-start(bf16[3,18,1,256]{3,2,1,0:T(2,128)(2,1)} %get-tuple-element.25), channel_id=1, source_target_pairs={{0,1},{1,2},{2,3},{4,5},{5,6},{6,7},{8,9},{9,10},{10,11},{12,13},{... | collective-permute-start | bytes 82952 | tf_op jit(solution)/shard_map/ppermute | solution.py:165
  78.5 2.0 %copy-start.2 = (f32[3,16,64,256]{3,2,1,0:T(8,128)S(1)}, f32[3,16,64,256]{3,2,1,0:T(8,128)}, u32[]{:S(2)}) copy-start(f32[3,16,64,256]{3,2,1,0:T(8,128)} %param.14) | copy-start | bytes 9437188
  78.5 2.3 %copy-start.5 = (f32[16,64,256]{2,1,0:T(8,128)S(1)}, f32[16,64,256]{2,1,0:T(8,128)}, u32[]{:S(2)}) copy-start(f32[16,64,256]{2,1,0:T(8,128)} %get-tuple-element.22) | copy-start | bytes 3145732
  78.5 2.6 %copy-start.6 = (f32[16,64,256]{2,1,0:T(8,128)S(1)}, f32[16,64,256]{2,1,0:T(8,128)}, u32[]{:S(2)}) copy-start(f32[16,64,256]{2,1,0:T(8,128)} %get-tuple-element.23) | copy-start | bytes 3145732
  86.2 1.7 %copy-start.4 = (f32[3,16,64,256]{3,2,1,0:T(8,128)}, f32[3,16,64,256]{3,2,1,0:T(8,128)S(1)}, u32[]{:S(2)}) copy-start(f32[3,16,64,256]{3,2,1,0:T(8,128)S(1)} %fusion.5) | copy-start | bytes 9437188

commit v3 on v2

--- a/solution.py
+++ b/solution.py
@@ -154,6 +154,66 @@
     )(per_rotor, rotor_states)
 
 
+def stencil_plane(x, planes, vel_ref, xlo_ref, xhi_ref, ylo_ref, yhi_ref):
+    _, _, ny, nz = vel_ref.shape
+    rows = lax.broadcasted_iota(jnp.int32, (ny, nz), 0)
+    lanes = lax.broadcasted_iota(jnp.int32, (ny, nz), 1)
+    here = [vel_ref[c, x] for c in range(3)]
+    results = []
+    for c in range(3):
+        u = here[c]
+        west = jnp.where(x == 0, xlo_ref[c].astype(jnp.float32), vel_ref[c, jnp.maximum(x - 1, 0)])
+        east = jnp.where(x == planes - 1, xhi_ref[c].astype(jnp.float32), vel_ref[c, jnp.minimum(x + 1, planes - 1)])
+        south = jnp.where(rows == 0, ylo_ref[c, x].astype(jnp.float32), pltpu.roll(u, 1, 0))
+        north = jnp.where(rows == ny - 1, yhi_ref[c, x].astype(jnp.float32), pltpu.roll(u, ny - 1, 0))
+        lower = jnp.where(lanes == 0, 0.0, pltpu.roll(u, 1, 1))
+        upper = jnp.where(lanes == nz - 1, 0.0, pltpu.roll(u, nz - 1, 1))
+        laplace = east + west + north + south + upper + lower - 6.0 * u
+        advect = (
+            here[0] * ((east - west) * 0.5)
+            + here[1] * ((north - south) * 0.5)
+            + here[2] * ((upper - lower) * 0.5)
+        )
+        results.append(u + time_step * (viscosity * laplace - advect))
+    return results
+
+
+def stencil_kernel(vel_ref, xlo_ref, xhi_ref, ylo_ref, yhi_ref, force_ref, out_ref):
+    planes = vel_ref.shape[1]
+
+    def body(x, carry):
+        results = stencil_plane(x, planes, vel_ref, xlo_ref, xhi_ref, ylo_ref, yhi_ref)
+        out_ref[0, x] = results[0] - force_scale * force_ref[x]
+        out_ref[1, x] = results[1]
+        out_ref[2, x] = results[2]
+        return carry
+
+    lax.fori_loop(0, planes, body, 0)
+
+
+def stencil(velocity, halos, forcing):
+    vmem = pl.BlockSpec(memory_space=pltpu.VMEM)
+    return pl.pallas_call(
+        stencil_kernel,
+        out_shape=jax.ShapeDtypeStruct(velocity.shape, velocity.dtype),
+        in_specs=[vmem] * 6,
+        out_specs=vmem,
+    )(velocity, *halos, forcing)
+
+
+def halo_faces(velocity):
+    faces = []
+    for axis, dim in (("slab", 1), ("cross", 2)):
+        count = lax.axis_size(axis)
+        size = velocity.shape[dim]
+        head = lax.slice_in_dim(velocity, 0, 1, axis=dim).astype(jnp.bfloat16)
+        tail = lax.slice_in_dim(velocity, size - 1, size, axis=dim).astype(jnp.bfloat16)
+        low = lax.ppermute(tail, axis, [(i, i + 1) for i in range(count - 1)])
+        high = lax.ppermute(head, axis, [(i + 1, i) for i in range(count - 1)])
+        faces += [jnp.squeeze(low, dim), jnp.squeeze(high, dim)] if dim == 1 else [low, high]
+    return faces
+
+
 def extended(cells, sides, width):
     for axis, dim in sides:
         count = lax.axis_size(axis)
@@ -195,6 +255,7 @@
 ):
     local_x, local_y, local_z = (velocity.shape[1], velocity.shape[2], velocity.shape[3])
     tile_count = local_x * local_y * local_z // TILE
+    halos = halo_faces(velocity)
     rotor_hot = (entry_rotor == jnp.arange(R, dtype=jnp.int32)[None, :]).astype(jnp.int32)
     slots = jnp.sum(rotor_hot * slot_of_rotor[None, :], axis=1)
     sub_range = jnp.arange(NSUB, dtype=jnp.int32)
@@ -218,20 +279,21 @@
     ).astype(jnp.bfloat16)
     new_states = lax.dynamic_slice_in_dim(all_new, lax.axis_index("slab"), 1, axis=0)
     rows = all_sources.reshape(R * NSUB, TILE)[slots * NSUB + entry_sub]
-    tile_hot = (jnp.arange(tile_count, dtype=jnp.int32)[:, None] == entry_tile[None, :]).astype(jnp.bfloat16)
-    forcing = jnp.dot(tile_hot, rows, preferred_element_type=jnp.float32)
-    vertical = jnp.pad(velocity, ((0, 0), (0, 0), (0, 0), (1, 1)))
-    upper = vertical[:, :, :, 2:]
-    lower = vertical[:, :, :, :-2]
-    padded = extended(velocity.astype(jnp.bfloat16), (("slab", 1), ("cross", 2)), 1).astype(
-        velocity.dtype
-    )
-    east = padded[:, 2:, 1:-1, :]
-    west = padded[:, :-2, 1:-1, :]
-    north = padded[:, 1:-1, 2:, :]
-    south = padded[:, 1:-1, :-2, :]
-    advanced = combine_terms(velocity, east, west, north, south, upper, lower)
-    advanced = advanced.at[0].add(-force_scale * forcing.reshape(local_x, local_y, local_z))
+    cells_xy = local_x * local_y
+    tile_pos = entry_tile // 2
+    forcing = jnp.concatenate(
+        [
+            jnp.dot(
+                ((jnp.arange(cells_xy, dtype=jnp.int32)[:, None] == tile_pos[None, :])
+                 & (entry_tile % 2 == half)[None, :]).astype(jnp.bfloat16),
+                rows,
+                preferred_element_type=jnp.float32,
+            )
+            for half in range(local_z // TILE)
+        ],
+        axis=1,
+    ).reshape(local_x, local_y, local_z)
+    advanced = stencil(velocity, halos, forcing)
     return (advanced, new_states)
 
 

time: 88.4 us -> 83.8 us (0.948)
  the two profiles are of different devices: /device:TPU:0 before, /device:TPU:1 now
where the time goes in v3:
time: 83.8 us; the launch traced here: 82.2 us
  Pallas kernels  31.3 us (37%)
  local copies, waits for them, and re-layouts  21.2 us (25%)
  starting transfers between devices  12.9 us (15%)
  matrix products  12.8 us (15%)
  other arithmetic  3.11 us (4%)
  between operations  0.91 us (1%)
    pallas_call x1, Pallas kernels, reduce_gather(): pl.pallas_call(lambda *refs: reduce_gather_kernel(rounds, *refs), out_sha...  23.2 us
    gather x3, local copies, waits for them, and re-layouts, on_device(): jnp.take(cells, entry_tile, axis=0).astype(jnp.bfloat16).astype(jnp.float32)  10.7 us
    ppermute x2, starting transfers between devices, halo_faces(): low = lax.ppermute(tail, axis, [(i, i + 1) for i in range(count - 1)])  8.38 us
    pallas_call x1, Pallas kernels, stencil(): pl.pallas_call(stencil_kernel, out_shape=jax.ShapeDtypeStruct(velocity.sh...  8.15 us
    dot_general x1, matrix products, on_device(): jnp.dot(all_new.astype(jnp.bfloat16), w_out, preferred_element_type=jnp.f...  4.92 us
    ppermute x2, starting transfers between devices, halo_faces(): high = lax.ppermute(head, axis, [(i + 1, i) for i in range(count - 1)])  4.49 us
    dot_general x3, matrix products, on_device(): jnp.dot(slot_hot.T, weighted, precision=lax.Precision.HIGHEST)  3.58 us
    gather x1, local copies, waits for them, and re-layouts, on_device(): rows = all_sources.reshape(R * NSUB, TILE)[slots * NSUB + entry_sub]  3.21 us
  transfers between devices with their start and end apart: 4, of which 0 were waited for; matrix products, arithmetic and copies ran while one was open for 42% of the time, Pallas kernels for 28%

profile of v3, /device:TPU:1, one launch (start us, length us, event | category | flops | bytes accessed | tf_op | source)
XLA Modules:
  0.0 82.2 jit_solution(9821472034588609843)
XLA Ops:
  0.7 2.3 %convert.6 = bf16[3,16,64,256]{3,2,1,0:T(8,128)(2,1)S(1)} convert(f32[3,16,64,256]{3,2,1,0:T(8,128)} %vel_ref.1) | non-fusion elementwise | flops 786432 | bytes 4718592 | tf_op jit(solution)/shard_map/convert.3
  3.0 0.7 fusion.40
  3.7 1.3 %collective-permute-start.3 = (bf16[3,16,1,256]{3,2,1,0:T(2,128)(2,1)}, bf16[3,16,1,256]{3,2,1,0:T(2,128)(2,1)}, u32[]{:S(2)}, u32[]{:S(2)}) collective-permute-start(bf16[3,16,1,256]{3,2,1,0:T(2,128)(2,1)} %get-tuple-element.10), channel_id=1, source_target_pairs={{1,0},{2,1},{3,2},{5,4},{6,5},{7,6},{9,8},{10,9},{11,10},{13,12},{... | collective-permute-start | bytes 73736 | tf_op jit(solution)/shard_map/ppermute | solution.py:212
  5.0 5.3 %collective-permute-start.2 = (bf16[3,16,1,256]{3,2,1,0:T(2,128)(2,1)}, bf16[3,16,1,256]{3,2,1,0:T(2,128)(2,1)}, u32[]{:S(2)}, u32[]{:S(2)}) collective-permute-start(bf16[3,16,1,256]{3,2,1,0:T(2,128)(2,1)} %get-tuple-element.11), channel_id=1, source_target_pairs={{0,1},{1,2},{2,3},{4,5},{5,6},{6,7},{8,9},{9,10},{10,11},{12,13},{... | collective-permute-start | bytes 73736 | tf_op jit(solution)/shard_map/ppermute | solution.py:211
  10.9 3.2 %collective-permute-start.1 = (bf16[3,1,64,256]{3,2,1,0:T(8,128)(2,1)}, bf16[3,1,64,256]{3,2,1,0:T(8,128)(2,1)}, u32[]{:S(2)}, u32[]{:S(2)}) collective-permute-start(bf16[3,1,64,256]{3,2,1,0:T(8,128)(2,1)} %get-tuple-element.12), channel_id=1, source_target_pairs={{4,0},{8,4},{12,8},{16,12},{20,16},{24,20},{28,24},{32,28},{36,32}... | collective-permute-start | bytes 294920 | tf_op jit(solution)/shard_map/ppermute | solution.py:212
  14.1 3.1 %collective-permute-start = (bf16[3,1,64,256]{3,2,1,0:T(8,128)(2,1)S(1)}, bf16[3,1,64,256]{3,2,1,0:T(8,128)(2,1)}, u32[]{:S(2)}, u32[]{:S(2)}) collective-permute-start(bf16[3,1,64,256]{3,2,1,0:T(8,128)(2,1)S(1)} %get-tuple-element.13), channel_id=1, source_target_pairs={{0,4},{4,8},{8,12},{12,16},{16,20},{20,24},{24,28},{28,32},{32,36}... | collective-permute-start | bytes 294920 | tf_op jit(solution)/shard_map/ppermute | solution.py:211
  17.3 1.2 %fusion.39 = (bf16[1,16,64,256]{3,2,1,0:T(8,128)(2,1)S(1)}, bf16[1,16,64,256]{3,2,1,0:T(8,128)(2,1)}, bf16[1,16,64,256]{3,2,1,0:T(8,128)(2,1)}) fusion(f32[3,16,64,256]{3,2,1,0:T(8,128)S(1)} %copy-done.1), kind=kLoop, calls=%fused_computation.70 | loop fusion | bytes 3145728 | tf_op jit(solution)/shard_map/slice | solution.py:267
  18.6 0.8 %fusion.18 = f32[1024,384]{1,0:T(8,128)S(1)} fusion(f32[32,384]{1,0:T(8,128)S(1)} %copy-done.2, s32[1024]{0:T(1024)S(1)} %copy-done.3), kind=kOutput, calls=%fused_computation.32 | convolution fusion | flops 151027712 | bytes 1626112 | tf_op jit(solution)/shard_map/dot_general | solution.py:263
  19.6 1.2 %reshape_squeeze.10 = bf16[2048,128]{1,0:T(8,128)(2,1)S(1)} reshape(bf16[1,16,64,256]{3,2,1,0:T(8,128)(2,1)} %get-tuple-element.8) | data formatting | bytes 1048576 | tf_op jit(solution)/shard_map/reshape;squeeze | solution.py:267
  20.8 4.3 %gather_fusion.1 = bf16[1024,128]{1,0:T(8,128)(2,1)} fusion(bf16[2048,128]{1,0:T(8,128)(2,1)S(1)} %reshape_squeeze.9, s32[1024]{0:T(1024)S(1)} %get-tuple-element.18), kind=kCustom, calls=%fused_computation.clone | custom fusion | bytes 528384 | tf_op jit(solution)/shard_map/jit(_take)/gather | solution.py:268
  25.1 3.2 %gather_fusion.2 = bf16[1024,128]{1,0:T(8,128)(2,1)S(1)} fusion(bf16[2048,128]{1,0:T(8,128)(2,1)S(1)} %reshape_squeeze.10, s32[1024]{0:T(1024)S(1)} %get-tuple-element.18), kind=kCustom, calls=%fused_computation.1.clone | custom fusion | bytes 528384 | tf_op jit(solution)/shard_map/jit(_take)/gather | solution.py:268
  28.4 1.8 %fusion.14 = f32[32,128]{1,0:T(8,128)S(1)} fusion(f32[1024,384]{1,0:T(8,128)S(1)} %fusion.18, bf16[1024,128]{1,0:T(8,128)(2,1)} %gather_fusion.1, s32[1024]{0:T(1024)S(1)} %select_reduce_fusion, pred[1024]{0:T(1024)(128)(4,1)S(1)} %get-tuple-element.16), kind=kOutput, calls=%fused_computation.23 | convolution fusion | flops 50757632 | bytes 807936 | tf_op jit(solution)/shard_map/dot_general | solution.py:270
  30.2 0.9 %fusion.13 = f32[32,128]{1,0:T(8,128)S(1)} fusion(f32[1024,384]{1,0:T(8,128)S(1)} %fusion.18, bf16[1024,128]{1,0:T(8,128)(2,1)S(1)} %gather_fusion.2, s32[1024]{0:T(1024)S(1)} %select_reduce_fusion, pred[1024]{0:T(1024)(128)(4,1)S(1)} %get-tuple-element.16), kind=kOutput, calls=%fused_computation.21 | convolution fusion | flops 50757632 | bytes 807936 | tf_op jit(solution)/shard_map/dot_general | solution.py:270
  31.1 1.2 %reshape_squeeze.11 = bf16[2048,128]{1,0:T(8,128)(2,1)S(1)} reshape(bf16[1,16,64,256]{3,2,1,0:T(8,128)(2,1)} %get-tuple-element.9) | data formatting | bytes 1048576 | tf_op jit(solution)/shard_map/reshape;squeeze | solution.py:267
  32.3 3.2 %gather_fusion.3 = bf16[1024,128]{1,0:T(8,128)(2,1)S(1)} fusion(bf16[2048,128]{1,0:T(8,128)(2,1)S(1)} %reshape_squeeze.11, s32[1024]{0:T(1024)S(1)} %get-tuple-element.18), kind=kCustom, calls=%fused_computation.2.clone | custom fusion | bytes 528384 | tf_op jit(solution)/shard_map/jit(_take)/gather | solution.py:268
  35.5 0.9 %fusion.12 = f32[32,128]{1,0:T(8,128)S(1)} fusion(f32[1024,384]{1,0:T(8,128)S(1)} %fusion.18, bf16[1024,128]{1,0:T(8,128)(2,1)S(1)} %gather_fusion.3, s32[1024]{0:T(1024)S(1)} %select_reduce_fusion, pred[1024]{0:T(1024)(128)(4,1)S(1)} %get-tuple-element.16), kind=kOutput, calls=%fused_computation.19 | convolution fusion | flops 50757632 | bytes 807936 | tf_op jit(solution)/shard_map/dot_general | solution.py:270
  37.0 23.2 %shard_map.113 = (f32[32,384]{1,0:T(8,128)}, f32[32,1,1024]{2,1,0:T(1,128)}) custom-call(f32[32,384]{1,0:T(8,128)} %pad_maximum_fusion.1.refs_0_, f32[1,1024]{1,0:T(1,128)} %refs_1_.1), custom_call_target="tpu_custom_call" | custom-call | tf_op jit(solution)/shard_map/pallas_call | solution.py:138
  60.2 1.2 %fusion.11 = f32[32,1024]{1,0:T(8,128)S(1)} fusion(bf16[384,1024]{1,0:T(8,128)(2,1)S(1)} %copy-done, f32[32,1,1024]{2,1,0:T(1,128)} %get-tuple-element.5, f32[1024]{0:T(1024)S(1)} %copy-done.5, f32[32,384]{1,0:T(8,128)} %get-tuple-element.6), kind=kOutput, calls=%fused_computation.16 | convolution fusion | flops 25321472 | bytes 1101824 | tf_op jit(solution)/shard_map/dot_general | solution.py:275
  61.4 4.9 %convolution_convert_fusion = bf16[32,4096]{1,0:T(8,128)(2,1)S(1)} fusion(bf16[1024,4096]{1,0:T(8,128)(2,1)} %param.15, f32[32,1024]{1,0:T(8,128)S(1)} %fusion.11), kind=kOutput, calls=%fused_computation.4 | convolution fusion | flops 268599296 | bytes 8781824 | tf_op jit(solution)/shard_map/dot_general | solution.py:277
  66.5 3.2 %gather_fusion = bf16[1024,128]{1,0:T(8,128)(2,1)S(1)} fusion(bf16[1024,128]{1,0:T(8,128)(2,1)S(1)} %reshape.26, s32[1024]{0:T(1024)S(1)} %fusion.31), kind=kCustom, calls=%fused_computation.3 | custom fusion | bytes 528384 | tf_op jit(solution)/shard_map/gather | solution.py:281
  69.7 1.2 %fusion.2 = f32[1024,128]{0,1:T(8,128)S(1)} fusion(bf16[1024,128]{1,0:T(8,128)(2,1)S(1)} %gather_fusion, s32[1024]{0:T(1024)S(1)} %get-tuple-element.17, pred[1024]{0:T(1024)(128)(4,1)S(1)} %get-tuple-element.14), kind=kOutput, calls=%fused_computation.8 | convolution fusion | flops 270532608 | bytes 791552 | tf_op jit(solution)/shard_map/dot_general | solution.py:286
  70.9 1.2 %fusion.4 = f32[1024,128]{0,1:T(8,128)S(1)} fusion(bf16[1024,128]{1,0:T(8,128)(2,1)S(1)} %gather_fusion, s32[1024]{0:T(1024)S(1)} %get-tuple-element.17, pred[1024]{0:T(1024)(128)(4,1)S(1)} %get-tuple-element.15), kind=kOutput, calls=%fused_computation.9 | convolution fusion | flops 270532608 | bytes 791552 | tf_op jit(solution)/shard_map/dot_general | solution.py:286
  72.7 1.3 %copy.13 = f32[1024,256]{1,0:T(8,128)} copy(f32[1024,256]{0,1:T(8,128)S(1)} %pad_maximum_fusion) | data formatting | bytes 2097152 | tf_op jit(solution)/shard_map/concatenate | solution.py:284
  74.1 8.1 %shard_map.114 = f32[3,16,64,256]{3,2,1,0:T(8,128)} custom-call(f32[3,16,64,256]{3,2,1,0:T(8,128)} %vel_ref.1, bf16[3,64,256]{2,1,0:T(8,128)(2,1)} %bitcast.xlo_ref, bf16[3,64,256]{2,1,0:T(8,128)(2,1)} %bitcast.1.xhi_ref, bf16[3,16,1,256]{3,2,1,0:T(2,128)(2,1)} %collective-permute-done.2.ylo_ref, bf16[3,16,1,256]{3,2,1,0:T(2,128)(2,1)} %collective-permute-done.3.yhi_ref, ...), custom_call_target="tpu_custom_call" | custom-call | tf_op jit(solution)/shard_map/pallas_call | solution.py:196
  (30 shorter events, 2.5 us)
Async XLA Ops:
  0.6 59.6 %copy-start = (bf16[384,1024]{1,0:T(8,128)(2,1)S(1)}, bf16[384,1024]{1,0:T(8,128)(2,1)}, u32[]{:S(2)}) copy-start(bf16[384,1024]{1,0:T(8,128)(2,1)} %param.14) | copy-start | bytes 2359300
  0.6 16.6 %copy-start.1 = (f32[3,16,64,256]{3,2,1,0:T(8,128)S(1)}, f32[3,16,64,256]{3,2,1,0:T(8,128)}, u32[]{:S(2)}) copy-start(f32[3,16,64,256]{3,2,1,0:T(8,128)} %vel_ref.1) | copy-start | bytes 9437188
  0.7 16.6 %copy-start.4 = (s32[1024]{0:T(1024)S(1)}, s32[1024]{0:T(1024)}, u32[]{:S(2)}) copy-start(s32[1024]{0:T(1024)} %param.20) | copy-start | bytes 12292
  0.7 17.8 %copy-start.6 = (s32[1024,1]{0,1:T(1,128)S(1)}, s32[1024,1]{0,1:T(1,128)}, u32[]{:S(2)}) copy-start(s32[1024,1]{0,1:T(1,128)} %param.19) | copy-start | bytes 12292
  0.7 17.8 %copy-start.7 = (s32[32]{0:T(128)S(1)}, s32[32]{0:T(128)}, u32[]{:S(2)}) copy-start(s32[32]{0:T(128)} %param.18) | copy-start | bytes 388
  0.7 17.9 %copy-start.3 = (s32[1024]{0:T(1024)S(1)}, s32[1024]{0:T(1024)}, u32[]{:S(2)}) copy-start(s32[1024]{0:T(1024)} %param.21) | copy-start | bytes 12292
  0.7 17.9 %copy-start.2 = (f32[32,384]{1,0:T(8,128)S(1)}, f32[32,384]{1,0:T(8,128)}, u32[]{:S(2)}) copy-start(f32[32,384]{1,0:T(8,128)} %param.13) | copy-start | bytes 147460
  3.7 70.4 %collective-permute-start.3 = (bf16[3,16,1,256]{3,2,1,0:T(2,128)(2,1)}, bf16[3,16,1,256]{3,2,1,0:T(2,128)(2,1)}, u32[]{:S(2)}, u32[]{:S(2)}) collective-permute-start(bf16[3,16,1,256]{3,2,1,0:T(2,128)(2,1)} %get-tuple-element.10), channel_id=1, source_target_pairs={{1,0},{2,1},{3,2},{5,4},{6,5},{7,6},{9,8},{10,9},{11,10},{13,12},{... | collective-permute-start | bytes 73736 | tf_op jit(solution)/shard_map/ppermute | solution.py:212
  5.0 69.1 %collective-permute-start.2 = (bf16[3,16,1,256]{3,2,1,0:T(2,128)(2,1)}, bf16[3,16,1,256]{3,2,1,0:T(2,128)(2,1)}, u32[]{:S(2)}, u32[]{:S(2)}) collective-permute-start(bf16[3,16,1,256]{3,2,1,0:T(2,128)(2,1)} %get-tuple-element.11), channel_id=1, source_target_pairs={{0,1},{1,2},{2,3},{4,5},{5,6},{6,7},{8,9},{9,10},{10,11},{12,13},{... | collective-permute-start | bytes 73736 | tf_op jit(solution)/shard_map/ppermute | solution.py:211
  10.9 63.2 %collective-permute-start.1 = (bf16[3,1,64,256]{3,2,1,0:T(8,128)(2,1)}, bf16[3,1,64,256]{3,2,1,0:T(8,128)(2,1)}, u32[]{:S(2)}, u32[]{:S(2)}) collective-permute-start(bf16[3,1,64,256]{3,2,1,0:T(8,128)(2,1)} %get-tuple-element.12), channel_id=1, source_target_pairs={{4,0},{8,4},{12,8},{16,12},{20,16},{24,20},{28,24},{32,28},{36,32}... | collective-permute-start | bytes 294920 | tf_op jit(solution)/shard_map/ppermute | solution.py:212
  14.1 60.0 %collective-permute-start = (bf16[3,1,64,256]{3,2,1,0:T(8,128)(2,1)S(1)}, bf16[3,1,64,256]{3,2,1,0:T(8,128)(2,1)}, u32[]{:S(2)}, u32[]{:S(2)}) collective-permute-start(bf16[3,1,64,256]{3,2,1,0:T(8,128)(2,1)S(1)} %get-tuple-element.13), channel_id=1, source_target_pairs={{0,4},{4,8},{8,12},{12,16},{16,20},{20,24},{24,28},{28,32},{32,36}... | collective-permute-start | bytes 294920 | tf_op jit(solution)/shard_map/ppermute | solution.py:211
  28.3 31.9 %copy-start.5 = (f32[1024]{0:T(1024)S(1)}, f32[1024]{0:T(1024)}, u32[]{:S(2)}) copy-start(f32[1024]{0:T(1024)} %param.16) | copy-start | bytes 12292

commit v4 on v3

--- a/solution.py
+++ b/solution.py
@@ -263,9 +263,10 @@
     gains = jnp.dot(sub_hot, shape_weight, precision=lax.Precision.HIGHEST)
     slot_hot = (slots[:, None] == jnp.arange(R, dtype=jnp.int32)[None, :]).astype(jnp.float32)
     per_rotor = []
+    pick_hot = (entry_tile[:, None] == jnp.arange(tile_count, dtype=jnp.int32)[None, :]).astype(jnp.bfloat16)
     for c in range(3):
-        cells = velocity[c].reshape(tile_count, TILE)
-        picked = jnp.take(cells, entry_tile, axis=0).astype(jnp.bfloat16).astype(jnp.float32)
+        cells = velocity[c].reshape(tile_count, TILE).astype(jnp.bfloat16)
+        picked = jnp.dot(pick_hot, cells, preferred_element_type=jnp.float32)
         weighted = gains[:, c * TILE:(c + 1) * TILE] * picked
         per_rotor.append(jnp.dot(slot_hot.T, weighted, precision=lax.Precision.HIGHEST))
     per_rotor = jnp.concatenate(per_rotor, axis=1)
@@ -280,19 +281,11 @@
     new_states = lax.dynamic_slice_in_dim(all_new, lax.axis_index("slab"), 1, axis=0)
     rows = all_sources.reshape(R * NSUB, TILE)[slots * NSUB + entry_sub]
     cells_xy = local_x * local_y
-    tile_pos = entry_tile // 2
-    forcing = jnp.concatenate(
-        [
-            jnp.dot(
-                ((jnp.arange(cells_xy, dtype=jnp.int32)[:, None] == tile_pos[None, :])
-                 & (entry_tile % 2 == half)[None, :]).astype(jnp.bfloat16),
-                rows,
-                preferred_element_type=jnp.float32,
-            )
-            for half in range(local_z // TILE)
-        ],
-        axis=1,
-    ).reshape(local_x, local_y, local_z)
+    halves = local_z // TILE
+    half = (entry_tile % halves)[:, None]
+    wide = jnp.concatenate([jnp.where(half == h, rows, jnp.zeros_like(rows)) for h in range(halves)], axis=1)
+    place_hot = (jnp.arange(cells_xy, dtype=jnp.int32)[:, None] == (entry_tile // halves)[None, :]).astype(jnp.bfloat16)
+    forcing = jnp.dot(place_hot, wide, preferred_element_type=jnp.float32).reshape(local_x, local_y, local_z)
     advanced = stencil(velocity, halos, forcing)
     return (advanced, new_states)
 

time: 83.8 us -> 77.7 us (0.927)
  the two profiles are of different devices: /device:TPU:1 before, /device:TPU:0 now
where the time goes in v4:
time: 77.7 us; the launch traced here: 77.3 us
  Pallas kernels  36.9 us (47%)
  matrix products  18.2 us (23%)
  starting transfers between devices  9.23 us (12%)
  local copies, waits for them, and re-layouts  7.56 us (10%)
  other arithmetic  4.44 us (6%)
  between operations  0.87 us (1%)
    pallas_call x1, Pallas kernels, reduce_gather(): pl.pallas_call(lambda *refs: reduce_gather_kernel(rounds, *refs), out_sha...  28.8 us
    pallas_call x1, Pallas kernels, stencil(): pl.pallas_call(stencil_kernel, out_shape=jax.ShapeDtypeStruct(velocity.sh...  8.15 us
    ppermute x2, starting transfers between devices, halo_faces(): low = lax.ppermute(tail, axis, [(i, i + 1) for i in range(count - 1)])  6.54 us
    dot_general x3, matrix products, on_device(): picked = jnp.dot(pick_hot, cells, preferred_element_type=jnp.float32)  6.5 us
    dot_general x1, matrix products, on_device(): jnp.dot(all_new.astype(jnp.bfloat16), w_out, preferred_element_type=jnp.f...  4.92 us
    gather x1, local copies, waits for them, and re-layouts, on_device(): rows = all_sources.reshape(R * NSUB, TILE)[slots * NSUB + entry_sub]  3.21 us
    ppermute x2, starting transfers between devices, halo_faces(): high = lax.ppermute(head, axis, [(i + 1, i) for i in range(count - 1)])  2.69 us
    dot_general x3, matrix products, on_device(): jnp.dot(slot_hot.T, weighted, precision=lax.Precision.HIGHEST)  2.2 us
  transfers between devices with their start and end apart: 4, of which 0 were waited for; matrix products, arithmetic and copies ran while one was open for 35% of the time, Pallas kernels for 37%

profile of v4, /device:TPU:0, one launch (start us, length us, event | category | flops | bytes accessed | tf_op | source)
XLA Modules:
  0.0 77.3 jit_solution(13262013115010066432)
XLA Ops:
  0.6 2.2 %convert.9 = bf16[3,16,64,256]{3,2,1,0:T(8,128)(2,1)S(1)} convert(f32[3,16,64,256]{3,2,1,0:T(8,128)} %vel_ref.1) | non-fusion elementwise | flops 786432 | bytes 4718592 | tf_op jit(solution)/shard_map/convert.6
  2.8 0.6 fusion.33
  3.5 1.9 %collective-permute-start = (bf16[3,1,64,256]{3,2,1,0:T(8,128)(2,1)}, bf16[3,1,64,256]{3,2,1,0:T(8,128)(2,1)}, u32[]{:S(2)}, u32[]{:S(2)}) collective-permute-start(bf16[3,1,64,256]{3,2,1,0:T(8,128)(2,1)} %get-tuple-element.12), channel_id=1, source_target_pairs={{0,4},{4,8},{8,12},{12,16},{16,20},{20,24},{24,28},{28,32},{32,36}... | collective-permute-start | bytes 294920 | tf_op jit(solution)/shard_map/ppermute | solution.py:211
  5.4 1.3 %collective-permute-start.1 = (bf16[3,1,64,256]{3,2,1,0:T(8,128)(2,1)S(1)}, bf16[3,1,64,256]{3,2,1,0:T(8,128)(2,1)}, u32[]{:S(2)}, u32[]{:S(2)}) collective-permute-start(bf16[3,1,64,256]{3,2,1,0:T(8,128)(2,1)S(1)} %get-tuple-element.11), channel_id=1, source_target_pairs={{4,0},{8,4},{12,8},{16,12},{20,16},{24,20},{28,24},{32,28},{36,32}... | collective-permute-start | bytes 294920 | tf_op jit(solution)/shard_map/ppermute | solution.py:212
  6.7 0.7 fusion.32
  7.4 4.6 %collective-permute-start.2 = (bf16[3,16,1,256]{3,2,1,0:T(2,128)(2,1)}, bf16[3,16,1,256]{3,2,1,0:T(2,128)(2,1)}, u32[]{:S(2)}, u32[]{:S(2)}) collective-permute-start(bf16[3,16,1,256]{3,2,1,0:T(2,128)(2,1)} %get-tuple-element.10), channel_id=1, source_target_pairs={{0,1},{1,2},{2,3},{4,5},{5,6},{6,7},{8,9},{9,10},{10,11},{12,13},{... | collective-permute-start | bytes 73736 | tf_op jit(solution)/shard_map/ppermute | solution.py:211
  12.0 1.4 %collective-permute-start.3 = (bf16[3,16,1,256]{3,2,1,0:T(2,128)(2,1)}, bf16[3,16,1,256]{3,2,1,0:T(2,128)(2,1)}, u32[]{:S(2)}, u32[]{:S(2)}) collective-permute-start(bf16[3,16,1,256]{3,2,1,0:T(2,128)(2,1)} %get-tuple-element.9), channel_id=1, source_target_pairs={{1,0},{2,1},{3,2},{5,4},{6,5},{7,6},{9,8},{10,9},{11,10},{13,12},{... | collective-permute-start | bytes 73736 | tf_op jit(solution)/shard_map/ppermute | solution.py:212
  13.6 0.6 add_select_fusion.1
  14.8 1.0 %convert_element_type.32 = bf16[2048,128]{1,0:T(8,128)(2,1)} reshape(bf16[1,16,64,256]{3,2,1,0:T(8,128)(2,1)S(1)} %get-tuple-element.7) | data formatting | bytes 1048576 | tf_op jit(solution)/shard_map/convert_element_type | solution.py:268
  15.7 1.6 %fusion.19 = f32[1024,384]{1,0:T(8,128)S(1)} fusion(f32[32,384]{1,0:T(8,128)} %param.11, s32[1024]{0:T(1024)S(1)} %copy-done.1), kind=kOutput, calls=%fused_computation.26 | convolution fusion | flops 151027712 | bytes 1626112 | tf_op jit(solution)/shard_map/dot_general | solution.py:263
  17.5 2.5 %fusion.10 = f32[1024,128]{1,0:T(8,128)S(1)} fusion(bf16[2048,128]{1,0:T(8,128)(2,1)} %convert_element_type.32, s32[1024]{0:T(1024)S(1)} %copy-done.2, f32[1024,384]{1,0:T(8,128)S(1)} %fusion.19), kind=kOutput, calls=%fused_computation.14 | convolution fusion | flops 539099136 | bytes 1576960 | tf_op jit(solution)/shard_map/dot_general | solution.py:269
  20.0 0.7 fusion.16
  20.8 1.0 %convert_element_type.31 = bf16[2048,128]{1,0:T(8,128)(2,1)} reshape(bf16[1,16,64,256]{3,2,1,0:T(8,128)(2,1)S(1)} %get-tuple-element.8) | data formatting | bytes 1048576 | tf_op jit(solution)/shard_map/convert_element_type | solution.py:268
  21.7 2.5 %fusion.9 = f32[1024,128]{1,0:T(8,128)S(1)} fusion(bf16[2048,128]{1,0:T(8,128)(2,1)} %convert_element_type.31, s32[1024]{0:T(1024)S(1)} %copy-done.2, f32[1024,384]{1,0:T(8,128)S(1)} %fusion.19), kind=kOutput, calls=%fused_computation.13 | convolution fusion | flops 539099136 | bytes 1576960 | tf_op jit(solution)/shard_map/dot_general | solution.py:269
  24.3 0.7 fusion.17
  25.2 1.5 %fusion.8 = f32[1024,128]{1,0:T(8,128)S(1)} fusion(bf16[2048,128]{1,0:T(8,128)(2,1)S(1)} %convert_element_type.30, s32[1024]{0:T(1024)S(1)} %copy-done.2, f32[1024,384]{1,0:T(8,128)S(1)} %fusion.19), kind=kOutput, calls=%fused_computation.12 | convolution fusion | flops 539099136 | bytes 1576960 | tf_op jit(solution)/shard_map/dot_general | solution.py:269
  26.7 0.7 fusion.18
  27.4 0.6 pad_maximum_fusion.refs_0_
  28.0 28.8 %shard_map.113 = (f32[32,384]{1,0:T(8,128)}, f32[32,1,1024]{2,1,0:T(1,128)}) custom-call(f32[32,384]{1,0:T(8,128)} %pad_maximum_fusion.refs_0_, f32[1,1024]{1,0:T(1,128)} %refs_1_.1), custom_call_target="tpu_custom_call" | custom-call | tf_op jit(solution)/shard_map/pallas_call | solution.py:138
  56.8 1.2 %fusion.12 = f32[32,1024]{1,0:T(8,128)S(1)} fusion(bf16[384,1024]{1,0:T(8,128)(2,1)S(1)} %copy-done, f32[32,1,1024]{2,1,0:T(1,128)} %get-tuple-element.4, f32[1024]{0:T(1024)S(1)} %copy-done.3, f32[32,384]{1,0:T(8,128)} %get-tuple-element.5), kind=kOutput, calls=%fused_computation.17 | convolution fusion | flops 25321472 | bytes 1101824 | tf_op jit(solution)/shard_map/dot_general | solution.py:276
  58.0 4.9 %convolution_convert_fusion = bf16[32,4096]{1,0:T(8,128)(2,1)S(1)} fusion(bf16[1024,4096]{1,0:T(8,128)(2,1)} %param.13, f32[32,1024]{1,0:T(8,128)S(1)} %fusion.12), kind=kOutput, calls=%fused_computation.5 | convolution fusion | flops 268599296 | bytes 8781824 | tf_op jit(solution)/shard_map/dot_general | solution.py:278
  63.1 3.2 %gather_fusion = bf16[1024,128]{1,0:T(8,128)(2,1)S(1)} fusion(bf16[1024,128]{1,0:T(8,128)(2,1)S(1)} %reshape.27, s32[1024]{0:T(1024)S(1)} %fusion.26), kind=kCustom, calls=%fused_computation | custom fusion | bytes 528384 | tf_op jit(solution)/shard_map/gather | solution.py:282
  66.7 1.8 %fusion.6 = f32[1024,256]{1,0:T(8,128)} fusion(s32[1024]{0:T(1024)S(1)} %copy-done.6, bf16[1024,128]{1,0:T(8,128)(2,1)S(1)} %get-tuple-element.14, bf16[1024,128]{1,0:T(8,128)(2,1)S(1)} %get-tuple-element.13), kind=kOutput, calls=%fused_computation.10 | convolution fusion | flops 538968064 | bytes 1576960 | tf_op jit(solution)/shard_map/dot_general | solution.py:288
  69.1 8.1 %shard_map.114 = f32[3,16,64,256]{3,2,1,0:T(8,128)} custom-call(f32[3,16,64,256]{3,2,1,0:T(8,128)} %vel_ref.1, bf16[3,64,256]{2,1,0:T(8,128)(2,1)} %bitcast.xlo_ref, bf16[3,64,256]{2,1,0:T(8,128)(2,1)} %bitcast.1.xhi_ref, bf16[3,16,1,256]{3,2,1,0:T(2,128)(2,1)} %collective-permute-done.2.ylo_ref, bf16[3,16,1,256]{3,2,1,0:T(2,128)(2,1)} %collective-permute-done.3.yhi_ref, ...), custom_call_target="tpu_custom_call" | custom-call | tf_op jit(solution)/shard_map/pallas_call | solution.py:196
  (28 shorter events, 2.1 us)
Async XLA Ops:
  0.6 56.2 %copy-start = (bf16[384,1024]{1,0:T(8,128)(2,1)S(1)}, bf16[384,1024]{1,0:T(8,128)(2,1)}, u32[]{:S(2)}) copy-start(bf16[384,1024]{1,0:T(8,128)(2,1)} %param.12) | copy-start | bytes 2359300
  2.8 10.7 %copy-start.2 = (s32[1024]{0:T(1024)S(1)}, s32[1024]{0:T(1024)}, u32[]{:S(2)}) copy-start(s32[1024]{0:T(1024)} %param.18) | copy-start | bytes 12292
  3.5 65.6 %collective-permute-start = (bf16[3,1,64,256]{3,2,1,0:T(8,128)(2,1)}, bf16[3,1,64,256]{3,2,1,0:T(8,128)(2,1)}, u32[]{:S(2)}, u32[]{:S(2)}) collective-permute-start(bf16[3,1,64,256]{3,2,1,0:T(8,128)(2,1)} %get-tuple-element.12), channel_id=1, source_target_pairs={{0,4},{4,8},{8,12},{12,16},{16,20},{20,24},{24,28},{28,32},{32,36}... | collective-permute-start | bytes 294920 | tf_op jit(solution)/shard_map/ppermute | solution.py:211
  5.4 63.7 %collective-permute-start.1 = (bf16[3,1,64,256]{3,2,1,0:T(8,128)(2,1)S(1)}, bf16[3,1,64,256]{3,2,1,0:T(8,128)(2,1)}, u32[]{:S(2)}, u32[]{:S(2)}) collective-permute-start(bf16[3,1,64,256]{3,2,1,0:T(8,128)(2,1)S(1)} %get-tuple-element.11), channel_id=1, source_target_pairs={{4,0},{8,4},{12,8},{16,12},{20,16},{24,20},{28,24},{32,28},{36,32}... | collective-permute-start | bytes 294920 | tf_op jit(solution)/shard_map/ppermute | solution.py:212
  7.4 61.7 %collective-permute-start.2 = (bf16[3,16,1,256]{3,2,1,0:T(2,128)(2,1)}, bf16[3,16,1,256]{3,2,1,0:T(2,128)(2,1)}, u32[]{:S(2)}, u32[]{:S(2)}) collective-permute-start(bf16[3,16,1,256]{3,2,1,0:T(2,128)(2,1)} %get-tuple-element.10), channel_id=1, source_target_pairs={{0,1},{1,2},{2,3},{4,5},{5,6},{6,7},{8,9},{9,10},{10,11},{12,13},{... | collective-permute-start | bytes 73736 | tf_op jit(solution)/shard_map/ppermute | solution.py:211
  12.0 3.7 %copy-start.1 = (s32[1024]{0:T(1024)S(1)}, s32[1024]{0:T(1024)}, u32[]{:S(2)}) copy-start(s32[1024]{0:T(1024)} %param.19) | copy-start | bytes 12292
  12.0 57.1 %collective-permute-start.3 = (bf16[3,16,1,256]{3,2,1,0:T(2,128)(2,1)}, bf16[3,16,1,256]{3,2,1,0:T(2,128)(2,1)}, u32[]{:S(2)}, u32[]{:S(2)}) collective-permute-start(bf16[3,16,1,256]{3,2,1,0:T(2,128)(2,1)} %get-tuple-element.9), channel_id=1, source_target_pairs={{1,0},{2,1},{3,2},{5,4},{6,5},{7,6},{9,8},{10,9},{11,10},{13,12},{... | collective-permute-start | bytes 73736 | tf_op jit(solution)/shard_map/ppermute | solution.py:212
  13.6 3.8 %copy-start.5 = (s32[1024,1]{0,1:T(1,128)S(1)}, s32[1024,1]{0,1:T(1,128)}, u32[]{:S(2)}) copy-start(s32[1024,1]{0,1:T(1,128)} %param.17) | copy-start | bytes 12292
  13.6 3.8 %copy-start.7 = (s32[32]{0:T(128)S(1)}, s32[32]{0:T(128)}, u32[]{:S(2)}) copy-start(s32[32]{0:T(128)} %param.16) | copy-start | bytes 388
  25.2 31.7 %copy-start.3 = (f32[1024]{0:T(1024)S(1)}, f32[1024]{0:T(1024)}, u32[]{:S(2)}) copy-start(f32[1024]{0:T(1024)} %param.14) | copy-start | bytes 12292
  63.0 3.4 %copy-start.4 = (pred[1024]{0:T(1024)(128)(4,1)S(1)}, pred[1024]{0:T(1024)(128)(4,1)}, u32[]{:S(2)}) copy-start(pred[1024]{0:T(1024)(128)(4,1)} %get-tuple-element.16) | copy-start | bytes 3076
  63.0 3.7 %copy-start.6 = (s32[1024]{0:T(1024)S(1)}, s32[1024]{0:T(1024)}, u32[]{:S(2)}) copy-start(s32[1024]{0:T(1024)} %add_select_fusion.1) | copy-start | bytes 12292

commit v5 on v4

--- a/solution.py
+++ b/solution.py
@@ -77,26 +77,54 @@
     return me - pos * stride + ((pos + shift) % n) * stride
 
 
-def reduce_gather_kernel(rounds, per_ref, st_ref, pooled_ref, states_ref, held, sends, recvs, st_sends, st_recvs):
+def step_kernel(rounds, per_ref, st_ref, vel_ref, pooled_ref, states_ref, adv_ref, held, sends, recvs,
+                st_sends, st_recvs, xlo, xhi, ylo, yhi, face_sends, face_recvs):
     here = (lax.axis_index("slab"), lax.axis_index("cross"))
+    slab, cross = lax.axis_size("slab"), lax.axis_size("cross")
+    planes = vel_ref.shape[1]
+    ny = vel_ref.shape[2]
+    s, c = here
 
     def device(axis, other):
         return (other, here[1]) if axis == 0 else (here[0], other)
 
+    extra = s - 1 + 2 * (s % 2)
     barrier = pltpu.get_barrier_semaphore()
     count = 0
     for axis, stride, n in rounds:
         for j in range(1, n):
             pl.semaphore_signal(barrier, inc=1, device_id=device(axis, partner(here[axis], stride, n, j)), device_id_type=MESH)
             count += 1
-    pl.semaphore_wait(barrier, count)
-
-    me = here[0]
-    states_ref[pl.ds(me, 1)] = st_ref[...][None]
+    pl.semaphore_signal(barrier, inc=1, device_id=((extra + slab) % slab, c), device_id_type=MESH)
+    pl.semaphore_wait(barrier, count + 1)
+
+    faces = [
+        (s > 0, s < slab - 1, vel_ref.at[:, 0], xhi, ((s + slab - 1) % slab, c)),
+        (s < slab - 1, s > 0, vel_ref.at[:, planes - 1], xlo, ((s + 1) % slab, c)),
+        (c > 0, c < cross - 1, vel_ref.at[:, :, pl.ds(0, 1)], yhi, (s, (c + cross - 1) % cross)),
+        (c < cross - 1, c > 0, vel_ref.at[:, :, pl.ds(ny - 1, 1)], ylo, (s, (c + 1) % cross)),
+    ]
+    face_copies = []
+    for k, (send_if, recv_if, src, dst, dev) in enumerate(faces):
+        copy = pltpu.make_async_remote_copy(
+            src_ref=src, dst_ref=dst, send_sem=face_sends.at[k], recv_sem=face_recvs.at[k],
+            device_id=dev, device_id_type=MESH,
+        )
+
+        @pl.when(send_if)
+        def _():
+            copy.start()
+
+        @pl.when(jnp.logical_not(recv_if))
+        def _():
+            dst[...] = jnp.zeros(dst.shape, dst.dtype)
+
+        face_copies.append((send_if, recv_if, copy))
+
+    states_ref[pl.ds(s, 1)] = st_ref[...][None]
     pooled_ref[...] = per_ref[...]
+    chunks = [None, (0, 6), (6, 11), (11, planes)]
     for r, (axis, stride, n) in enumerate(rounds):
-        if n == 1:
-            continue
         copies = []
         for j in range(1, n):
             dev = device(axis, partner(here[axis], stride, n, j))
@@ -111,7 +139,7 @@
             copy.start()
             copies.append(copy)
             if axis == 0:
-                rows = pl.ds(me - me % stride, stride)
+                rows = pl.ds(s - s % stride, stride)
                 block = pltpu.make_async_remote_copy(
                     src_ref=states_ref.at[rows],
                     dst_ref=states_ref.at[rows],
@@ -122,6 +150,16 @@
                 )
                 block.start()
                 copies.append(block)
+        if chunks[r] is not None:
+            first, last = chunks[r]
+
+            def body(x, carry):
+                results = stencil_plane(x, planes, vel_ref, xlo, xhi, ylo, yhi)
+                for k in range(3):
+                    adv_ref[k, x] = results[k]
+                return carry
+
+            lax.fori_loop(first, last, body, 0)
         for copy in copies:
             copy.wait()
         if n == 2:
@@ -129,29 +167,47 @@
         else:
             total = (pooled_ref[...] + held[r, 1]) + (held[r, 0] + held[r, 2])
         pooled_ref[...] = total
-
-
-def reduce_gather(per_rotor, rotor_states):
+        if r == 0:
+            for send_if, recv_if, copy in face_copies:
+
+                @pl.when(send_if)
+                def _():
+                    copy.wait_send()
+
+                @pl.when(recv_if)
+                def _():
+                    copy.wait_recv()
+
+
+def reduce_step(per_rotor, rotor_states, velocity):
     slab, cross = lax.axis_size("slab"), lax.axis_size("cross")
     rounds = ring_rounds(slab, cross)
     vmem = pl.BlockSpec(memory_space=pltpu.VMEM)
+    _, planes, ny, nz = velocity.shape
     return pl.pallas_call(
-        lambda *refs: reduce_gather_kernel(rounds, *refs),
+        lambda *refs: step_kernel(rounds, *refs),
         out_shape=(
             jax.ShapeDtypeStruct(per_rotor.shape, jnp.float32),
             jax.ShapeDtypeStruct((slab,) + rotor_states.shape, jnp.float32),
+            jax.ShapeDtypeStruct(velocity.shape, jnp.float32),
         ),
-        in_specs=[vmem, vmem],
-        out_specs=(vmem, vmem),
+        in_specs=[vmem, vmem, vmem],
+        out_specs=(vmem, vmem, vmem),
         scratch_shapes=[
             pltpu.VMEM((len(rounds), 3) + per_rotor.shape, jnp.float32),
             pltpu.SemaphoreType.DMA((len(rounds), 3)),
             pltpu.SemaphoreType.DMA((len(rounds), 3)),
             pltpu.SemaphoreType.DMA((len(rounds), 3)),
             pltpu.SemaphoreType.DMA((len(rounds), 3)),
+            pltpu.VMEM((3, ny, nz), jnp.float32),
+            pltpu.VMEM((3, ny, nz), jnp.float32),
+            pltpu.VMEM((3, planes, 1, nz), jnp.float32),
+            pltpu.VMEM((3, planes, 1, nz), jnp.float32),
+            pltpu.SemaphoreType.DMA((4,)),
+            pltpu.SemaphoreType.DMA((4,)),
         ],
         compiler_params=pltpu.CompilerParams(collective_id=0, has_side_effects=True),
-    )(per_rotor, rotor_states)
+    )(per_rotor, rotor_states, velocity)
 
 
 def stencil_plane(x, planes, vel_ref, xlo_ref, xhi_ref, ylo_ref, yhi_ref):
@@ -255,7 +311,6 @@
 ):
     local_x, local_y, local_z = (velocity.shape[1], velocity.shape[2], velocity.shape[3])
     tile_count = local_x * local_y * local_z // TILE
-    halos = halo_faces(velocity)
     rotor_hot = (entry_rotor == jnp.arange(R, dtype=jnp.int32)[None, :]).astype(jnp.int32)
     slots = jnp.sum(rotor_hot * slot_of_rotor[None, :], axis=1)
     sub_range = jnp.arange(NSUB, dtype=jnp.int32)
@@ -270,7 +325,7 @@
         weighted = gains[:, c * TILE:(c + 1) * TILE] * picked
         per_rotor.append(jnp.dot(slot_hot.T, weighted, precision=lax.Precision.HIGHEST))
     per_rotor = jnp.concatenate(per_rotor, axis=1)
-    pooled, all_states = reduce_gather(per_rotor, rotor_states)
+    pooled, all_states, advanced = reduce_step(per_rotor, rotor_states, velocity)
     all_states = all_states.reshape(-1, rotor_states.shape[1])
     pooled_b = (pooled * pool_scale).astype(jnp.bfloat16)
     drive = jnp.dot(pooled_b, w_in, preferred_element_type=jnp.float32)
@@ -286,7 +341,7 @@
     wide = jnp.concatenate([jnp.where(half == h, rows, jnp.zeros_like(rows)) for h in range(halves)], axis=1)
     place_hot = (jnp.arange(cells_xy, dtype=jnp.int32)[:, None] == (entry_tile // halves)[None, :]).astype(jnp.bfloat16)
     forcing = jnp.dot(place_hot, wide, preferred_element_type=jnp.float32).reshape(local_x, local_y, local_z)
-    advanced = stencil(velocity, halos, forcing)
+    advanced = advanced.at[0].add(-force_scale * forcing)
     return (advanced, new_states)
 
 

time: 77.7 us -> 66.9 us (0.86)
  the two profiles are of different devices: /device:TPU:0 before, /device:TPU:1 now
where the time goes in v5:
time: 66.9 us; the launch traced here: 66.5 us
  Pallas kernels  31.8 us (48%)
  matrix products  18.7 us (28%)
  local copies, waits for them, and re-layouts  8.93 us (13%)
  other arithmetic  6.31 us (9%)
  between operations  0.78 us (1%)
    pallas_call x1, Pallas kernels, reduce_step(): pl.pallas_call(lambda *refs: step_kernel(rounds, *refs), out_shape=(jax.S...  31.8 us
    dot_general x3, matrix products, on_device(): picked = jnp.dot(pick_hot, cells, preferred_element_type=jnp.float32)  6.77 us
    dot_general x1, matrix products, on_device(): jnp.dot(all_new.astype(jnp.bfloat16), w_out, preferred_element_type=jnp.f...  4.93 us
    gather x1, local copies, waits for them, and re-layouts, on_device(): rows = all_sources.reshape(R * NSUB, TILE)[slots * NSUB + entry_sub]  3.21 us
    dot_general x1, matrix products, on_device(): gains = jnp.dot(sub_hot, shape_weight, precision=lax.Precision.HIGHEST)  2.79 us
    unnamed x11, local copies, waits for them, and re-layouts  2.76 us
    dot_general x3, matrix products, on_device(): jnp.dot(slot_hot.T, weighted, precision=lax.Precision.HIGHEST)  2.2 us
    convert_element_type x3, local copies, waits for them, and re-layouts, on_device(): cells = velocity[c].reshape(tile_count, TILE).astype(jnp.bfloat16)  2.12 us

profile of v5, /device:TPU:1, one launch (start us, length us, event | category | flops | bytes accessed | tf_op | source)
XLA Modules:
  0.0 66.5 jit_solution(7711321376198099969)
XLA Ops:
  0.6 0.8 %broadcast_compare_fusion = (pred[1024]{0:T(1024)(128)(4,1)S(1)}, pred[1024]{0:T(1024)(128)(4,1)S(1)}) fusion(s32[1024]{0:T(1024)} %param.20), kind=kLoop, calls=%fused_computation.52 | loop fusion | flops 13312 | bytes 6144 | tf_op jit(solution)/shard_map/eq | solution.py:341
  1.4 0.8 %select_reduce_fusion = s32[1024]{0:T(1024)S(1)} fusion(s32[32]{0:T(128)} %param.18, s32[1024]{0:T(1024)} %bitcast.23), kind=kLoop, calls=%fused_computation.36 | loop fusion | flops 97280 | bytes 8320 | tf_op jit(solution)/shard_map/reduce_sum | solution.py:315
  2.2 0.7 %fusion.27 = s32[1024]{0:T(1024)S(1)} fusion(s32[1024]{0:T(1024)} %param.21, s32[1024]{0:T(1024)S(1)} %select_reduce_fusion), kind=kLoop, calls=%fused_computation.48 | loop fusion | flops 6144 | bytes 12288 | tf_op jit(solution)/shard_map/gather | solution.py:337
  2.9 0.7 %add_select_fusion.1 = s32[1024]{0:T(1024)S(1)} fusion(s32[1024]{0:T(1024)} %param.20), kind=kLoop, calls=%fused_computation.44 | loop fusion | flops 15360 | bytes 8192 | tf_op jit(solution)/shard_map/jit(floor_divide)/jit(_where)/select_n | solution.py:342
  3.6 2.8 %fusion.20 = f32[1024,384]{1,0:T(8,128)} fusion(f32[32,384]{1,0:T(8,128)} %param.13, s32[1024]{0:T(1024)} %param.21), kind=kOutput, calls=%fused_computation.28 | convolution fusion | flops 151027712 | bytes 1626112 | tf_op jit(solution)/shard_map/dot_general | solution.py:318
  6.4 2.1 %convert.5 = bf16[3,16,64,256]{3,2,1,0:T(8,128)(2,1)S(1)} convert(f32[3,16,64,256]{3,2,1,0:T(8,128)} %refs_2_.1) | non-fusion elementwise | flops 786432 | bytes 4718592 | tf_op jit(solution)/shard_map/convert.2
  8.6 1.0 %convert_element_type.26 = bf16[2048,128]{1,0:T(8,128)(2,1)} reshape(bf16[1,16,64,256]{3,2,1,0:T(8,128)(2,1)S(1)} %get-tuple-element.20) | data formatting | bytes 1048576 | tf_op jit(solution)/shard_map/convert_element_type | solution.py:323
  9.6 2.8 %fusion.9 = f32[1024,128]{1,0:T(8,128)S(1)} fusion(bf16[2048,128]{1,0:T(8,128)(2,1)} %convert_element_type.26, s32[1024]{0:T(1024)S(1)} %copy-done.3, f32[1024,384]{1,0:T(8,128)} %fusion.20), kind=kOutput, calls=%fused_computation.13 | convolution fusion | flops 539099136 | bytes 1576960 | tf_op jit(solution)/shard_map/dot_general | solution.py:324
  12.4 0.7 %fusion.19 = f32[32,128]{1,0:T(8,128)S(1)} fusion(f32[1024,128]{1,0:T(8,128)S(1)} %fusion.9, s32[1024]{0:T(1024)S(1)} %select_reduce_fusion), kind=kOutput, calls=%fused_computation.27 | convolution fusion | flops 50364416 | bytes 544768 | tf_op jit(solution)/shard_map/dot_general | solution.py:326
  13.1 1.0 %convert_element_type.28 = bf16[2048,128]{1,0:T(8,128)(2,1)} reshape(bf16[1,16,64,256]{3,2,1,0:T(8,128)(2,1)S(1)} %get-tuple-element.21) | data formatting | bytes 1048576 | tf_op jit(solution)/shard_map/convert_element_type | solution.py:323
  14.1 2.5 %fusion.11 = f32[1024,128]{1,0:T(8,128)S(1)} fusion(bf16[2048,128]{1,0:T(8,128)(2,1)} %convert_element_type.28, s32[1024]{0:T(1024)S(1)} %copy-done.3, f32[1024,384]{1,0:T(8,128)S(1)} %copy-done.2), kind=kOutput, calls=%fused_computation.15 | convolution fusion | flops 539099136 | bytes 1576960 | tf_op jit(solution)/shard_map/dot_general | solution.py:324
  16.6 0.7 %fusion.17 = f32[32,128]{1,0:T(8,128)S(1)} fusion(f32[1024,128]{1,0:T(8,128)S(1)} %fusion.11, s32[1024]{0:T(1024)S(1)} %select_reduce_fusion), kind=kOutput, calls=%fused_computation.25 | convolution fusion | flops 50364416 | bytes 544768 | tf_op jit(solution)/shard_map/dot_general | solution.py:326
  17.5 1.5 %fusion.10 = f32[1024,128]{1,0:T(8,128)S(1)} fusion(bf16[2048,128]{1,0:T(8,128)(2,1)S(1)} %convert_element_type.27, s32[1024]{0:T(1024)S(1)} %copy-done.3, f32[1024,384]{1,0:T(8,128)S(1)} %copy-done.2), kind=kOutput, calls=%fused_computation.14 | convolution fusion | flops 539099136 | bytes 1576960 | tf_op jit(solution)/shard_map/dot_general | solution.py:324
  19.0 0.7 %fusion.18 = f32[32,128]{1,0:T(8,128)S(1)} fusion(f32[1024,128]{1,0:T(8,128)S(1)} %fusion.10, s32[1024]{0:T(1024)S(1)} %select_reduce_fusion), kind=kOutput, calls=%fused_computation.26 | convolution fusion | flops 50364416 | bytes 544768 | tf_op jit(solution)/shard_map/dot_general | solution.py:326
  19.8 0.6 pad_maximum_fusion.refs_0_
  20.4 31.8 %shard_map.113 = (f32[32,384]{1,0:T(8,128)}, f32[32,1,1024]{2,1,0:T(1,128)}, f32[3,16,64,256]{3,2,1,0:T(8,128)}) custom-call(f32[32,384]{1,0:T(8,128)} %pad_maximum_fusion.refs_0_, f32[1,1024]{1,0:T(1,128)} %refs_1_.1, f32[3,16,64,256]{3,2,1,0:T(8,128)} %refs_2_.1), custom_call_target="tpu_custom_call" | custom-call | tf_op jit(solution)/shard_map/pallas_call | solution.py:187
  52.2 1.2 %fusion.13 = f32[32,1024]{1,0:T(8,128)S(1)} fusion(bf16[384,1024]{1,0:T(8,128)(2,1)S(1)} %copy-done, f32[32,1,1024]{2,1,0:T(1,128)} %get-tuple-element.18, f32[1024]{0:T(1024)S(1)} %copy-done.4, f32[32,384]{1,0:T(8,128)} %get-tuple-element.19), kind=kOutput, calls=%fused_computation.18 | convolution fusion | flops 25321472 | bytes 1101824 | tf_op jit(solution)/shard_map/dot_general | solution.py:331
  53.4 0.6 constant_dynamic-slice_fusion
  54.0 4.9 %convolution_convert_fusion = bf16[32,4096]{1,0:T(8,128)(2,1)S(1)} fusion(bf16[1024,4096]{1,0:T(8,128)(2,1)} %param.15, f32[32,1024]{1,0:T(8,128)S(1)} %fusion.13), kind=kOutput, calls=%fused_computation.5 | convolution fusion | flops 268599296 | bytes 8781824 | tf_op jit(solution)/shard_map/dot_general | solution.py:333
  59.0 3.2 %gather_fusion = bf16[1024,128]{1,0:T(8,128)(2,1)S(1)} fusion(bf16[1024,128]{1,0:T(8,128)(2,1)S(1)} %reshape.70, s32[1024]{0:T(1024)S(1)} %fusion.27), kind=kCustom, calls=%fused_computation | custom fusion | bytes 528384 | tf_op jit(solution)/shard_map/gather | solution.py:337
  62.3 0.3 broadcast_select_fusion.1
  62.6 0.8 %fusion.8 = f32[1024,256]{1,0:T(8,128)S(1)} fusion(s32[1024]{0:T(1024)S(1)} %add_select_fusion.1, bf16[1024,128]{1,0:T(8,128)(2,1)S(1)} %get-tuple-element.24, bf16[1024,128]{1,0:T(8,128)(2,1)S(1)} %get-tuple-element.23), kind=kOutput, calls=%fused_computation.12 | convolution fusion | flops 539230208 | bytes 1576960 | tf_op jit(solution)/shard_map/dot_general | solution.py:343
  63.4 1.1 %copy-done.1 = f32[3,16,64,256]{3,2,1,0:T(8,128)S(1)} copy-done((f32[3,16,64,256]{3,2,1,0:T(8,128)S(1)}, f32[3,16,64,256]{3,2,1,0:T(8,128)}, u32[]{:S(2)}) %copy-start.1) | copy-done | bytes 3145752
  64.8 1.7 %copy.16 = f32[3,16,64,256]{3,2,1,0:T(8,128)} copy(f32[3,16,64,256]{3,2,1,0:T(8,128)S(1)} %add_dynamic-update-slice_fusion) | data formatting | bytes 6291456
  (13 shorter events, 0.7 us)
Async XLA Ops:
  0.6 51.5 %copy-start = (bf16[384,1024]{1,0:T(8,128)(2,1)S(1)}, bf16[384,1024]{1,0:T(8,128)(2,1)}, u32[]{:S(2)}) copy-start(bf16[384,1024]{1,0:T(8,128)(2,1)} %param.14) | copy-start | bytes 2359300
  8.5 1.1 %copy-start.3 = (s32[1024]{0:T(1024)S(1)}, s32[1024]{0:T(1024)}, u32[]{:S(2)}) copy-start(s32[1024]{0:T(1024)} %param.20) | copy-start | bytes 12292
  9.6 4.5 %copy-start.2 = (f32[1024,384]{1,0:T(8,128)S(1)}, f32[1024,384]{1,0:T(8,128)}, u32[]{:S(2)}) copy-start(f32[1024,384]{1,0:T(8,128)} %fusion.20) | copy-start | bytes 4718596
  19.0 33.2 %copy-start.4 = (f32[1024]{0:T(1024)S(1)}, f32[1024]{0:T(1024)}, u32[]{:S(2)}) copy-start(f32[1024]{0:T(1024)} %param.16) | copy-start | bytes 12292
  62.6 1.9 %copy-start.1 = (f32[3,16,64,256]{3,2,1,0:T(8,128)S(1)}, f32[3,16,64,256]{3,2,1,0:T(8,128)}, u32[]{:S(2)}) copy-start(f32[3,16,64,256]{3,2,1,0:T(8,128)} %get-tuple-element.17) | copy-start | bytes 9437188

commit v6 on v5

--- a/solution.py
+++ b/solution.py
@@ -314,14 +314,25 @@
     rotor_hot = (entry_rotor == jnp.arange(R, dtype=jnp.int32)[None, :]).astype(jnp.int32)
     slots = jnp.sum(rotor_hot * slot_of_rotor[None, :], axis=1)
     sub_range = jnp.arange(NSUB, dtype=jnp.int32)
-    sub_hot = (entry_sub[:, None] == sub_range[None, :]).astype(jnp.float32)
-    gains = jnp.dot(sub_hot, shape_weight, precision=lax.Precision.HIGHEST)
+    sub_hot = (entry_sub[:, None] == sub_range[None, :]).astype(jnp.bfloat16)
+    high = shape_weight.astype(jnp.bfloat16)
+    rest = shape_weight - high.astype(jnp.float32)
+    middle = rest.astype(jnp.bfloat16)
+    low = (rest - middle.astype(jnp.float32)).astype(jnp.bfloat16)
+    gains = [jnp.dot(sub_hot, part, preferred_element_type=jnp.float32) for part in (high, middle, low)]
+    gains = (gains[0] + gains[1]) + gains[2]
     slot_hot = (slots[:, None] == jnp.arange(R, dtype=jnp.int32)[None, :]).astype(jnp.float32)
+    cells_xy = local_x * local_y
+    halves = local_z // TILE
+    half = (entry_tile % halves)[:, None]
+    place_hot = (jnp.arange(cells_xy, dtype=jnp.int32)[:, None] == (entry_tile // halves)[None, :]).astype(jnp.bfloat16)
     per_rotor = []
-    pick_hot = (entry_tile[:, None] == jnp.arange(tile_count, dtype=jnp.int32)[None, :]).astype(jnp.bfloat16)
     for c in range(3):
-        cells = velocity[c].reshape(tile_count, TILE).astype(jnp.bfloat16)
-        picked = jnp.dot(pick_hot, cells, preferred_element_type=jnp.float32)
+        cells = velocity[c].reshape(cells_xy, local_z).astype(jnp.bfloat16)
+        both = jnp.dot(place_hot.T, cells, preferred_element_type=jnp.float32)
+        picked = both[:, :TILE]
+        for h in range(1, halves):
+            picked = jnp.where(half == h, both[:, h * TILE:(h + 1) * TILE], picked)
         weighted = gains[:, c * TILE:(c + 1) * TILE] * picked
         per_rotor.append(jnp.dot(slot_hot.T, weighted, precision=lax.Precision.HIGHEST))
     per_rotor = jnp.concatenate(per_rotor, axis=1)
@@ -334,12 +345,10 @@
         all_new.astype(jnp.bfloat16), w_out, preferred_element_type=jnp.float32
     ).astype(jnp.bfloat16)
     new_states = lax.dynamic_slice_in_dim(all_new, lax.axis_index("slab"), 1, axis=0)
-    rows = all_sources.reshape(R * NSUB, TILE)[slots * NSUB + entry_sub]
-    cells_xy = local_x * local_y
-    halves = local_z // TILE
-    half = (entry_tile % halves)[:, None]
+    flat = all_sources.reshape(R * NSUB, TILE)
+    row_hot = ((slots * NSUB + entry_sub)[:, None] == jnp.arange(R * NSUB, dtype=jnp.int32)[None, :]).astype(jnp.bfloat16)
+    rows = jnp.dot(row_hot, flat, preferred_element_type=jnp.float32).astype(jnp.bfloat16)
     wide = jnp.concatenate([jnp.where(half == h, rows, jnp.zeros_like(rows)) for h in range(halves)], axis=1)
-    place_hot = (jnp.arange(cells_xy, dtype=jnp.int32)[:, None] == (entry_tile // halves)[None, :]).astype(jnp.bfloat16)
     forcing = jnp.dot(place_hot, wide, preferred_element_type=jnp.float32).reshape(local_x, local_y, local_z)
     advanced = advanced.at[0].add(-force_scale * forcing)
     return (advanced, new_states)

time: 66.9 us -> 58.6 us (0.88)
  local copies, waits for them, and re-layouts: 8.93 us -> 3.6 us
  matrix products: 18.7 us -> 16.1 us
    gather x1 -> x0, local copies, waits for them, and re-layouts: 3.21 us -> none  [on_device(): rows = all_sources.reshape(R * NSUB, TILE)[slots * NSUB + entry_sub]]
    dot_general x4 -> x7, matrix products: 9.56 us -> 6.57 us  [the longest x3 3.82 us: on_device(): both = jnp.dot(place_hot.T, cells, preferred_element_type=jnp.float32)]
    convert_element_type x3 -> x0, local copies, waits for them, and re-layouts: 2.12 us -> none  [on_device(): cells = velocity[c].reshape(tile_count, TILE).astype(jnp.bfloat16)]
    gather x1 -> x0, other arithmetic: 0.7 us -> none  [on_device(): rows = all_sources.reshape(R * NSUB, TILE)[slots * NSUB + entry_sub]]
    add x0 -> x1, other arithmetic: none -> 0.69 us  [on_device(): slots * NSUB + entry_sub]
where the time goes in v6:
time: 58.6 us; the launch traced here: 58.2 us
  Pallas kernels  31.8 us (54%)
  matrix products  16.1 us (27%)
  other arithmetic  5.97 us (10%)
  local copies, waits for them, and re-layouts  3.6 us (6%)
  between operations  0.81 us (1%)
    pallas_call x1, Pallas kernels, reduce_step(): pl.pallas_call(lambda *refs: step_kernel(rounds, *refs), out_shape=(jax.S...  31.8 us
    dot_general x1, matrix products, on_device(): jnp.dot(all_new.astype(jnp.bfloat16), w_out, preferred_element_type=jnp.f...  4.93 us
    dot_general x3, matrix products, on_device(): both = jnp.dot(place_hot.T, cells, preferred_element_type=jnp.float32)  3.82 us
    unnamed x11, local copies, waits for them, and re-layouts  2.76 us
    dot_general x3, matrix products, on_device(): jnp.dot(slot_hot.T, weighted, precision=lax.Precision.HIGHEST)  2.62 us
    another operation x1, other arithmetic  2.1 us
    dot_general x1, matrix products, on_device(): jnp.dot(row_hot, flat, preferred_element_type=jnp.float32)  1.49 us
    dot_general x3, matrix products, on_device(): jnp.dot(sub_hot, part, preferred_element_type=jnp.float32)  1.26 us

profile of v6, /device:TPU:1, one launch (start us, length us, event | category | flops | bytes accessed | tf_op | source)
XLA Modules:
  0.0 58.2 jit_solution(13531255612594675586)
XLA Ops:
  0.6 0.8 %broadcast_compare_fusion.1 = (pred[1024]{0:T(1024)(128)(4,1)S(1)}, pred[1024]{0:T(1024)(128)(4,1)S(1)}) fusion(s32[1024]{0:T(1024)} %param.20), kind=kLoop, calls=%fused_computation.74 | loop fusion | flops 13312 | bytes 6144 | tf_op jit(solution)/shard_map/eq | solution.py:351
  1.4 0.8 %select_reduce_fusion = s32[1024]{0:T(1024)S(1)} fusion(s32[32]{0:T(128)} %param.18, s32[1024]{0:T(1024)} %bitcast.20), kind=kLoop, calls=%fused_computation.54 | loop fusion | flops 97280 | bytes 8320 | tf_op jit(solution)/shard_map/reduce_sum | solution.py:315
  2.2 0.7 %add_select_fusion = s32[1024]{0:T(1024)S(1)} fusion(s32[1024]{0:T(1024)} %param.20), kind=kLoop, calls=%fused_computation.64 | loop fusion | flops 15360 | bytes 8192 | tf_op jit(solution)/shard_map/jit(floor_divide)/jit(_where)/select_n | solution.py:328
  2.9 0.7 %multiply_add_fusion = s32[1024]{0:T(1024)S(1)} fusion(s32[1024]{0:T(1024)} %param.21, s32[1024]{0:T(1024)S(1)} %select_reduce_fusion), kind=kLoop, calls=%fused_computation.69 | loop fusion | flops 2048 | bytes 12288 | tf_op jit(solution)/shard_map/add | solution.py:349
  3.6 2.1 %convert.5 = bf16[3,16,64,256]{3,2,1,0:T(8,128)(2,1)S(1)} convert(f32[3,16,64,256]{3,2,1,0:T(8,128)} %refs_2_.1) | non-fusion elementwise | flops 786432 | bytes 4718592 | tf_op jit(solution)/shard_map/convert.2
  5.8 1.3 %fusion.1 = f32[1024,256]{1,0:T(8,128)S(1)} fusion(bf16[1024,256]{1,0:T(8,128)(2,1)S(1)} %bitcast.19, s32[1024]{0:T(1024)S(1)} %add_select_fusion), kind=kOutput, calls=%fused_computation.4 | convolution fusion | flops 537919488 | bytes 1576960 | tf_op jit(solution)/shard_map/dot_general | solution.py:332
  7.1 1.3 %fusion.3 = f32[1024,256]{1,0:T(8,128)S(1)} fusion(bf16[1024,256]{1,0:T(8,128)(2,1)S(1)} %bitcast.18, s32[1024]{0:T(1024)S(1)} %add_select_fusion), kind=kOutput, calls=%fused_computation.6 | convolution fusion | flops 537919488 | bytes 1576960 | tf_op jit(solution)/shard_map/dot_general | solution.py:332
  8.4 1.3 %fusion.2 = f32[1024,256]{1,0:T(8,128)S(1)} fusion(bf16[1024,256]{1,0:T(8,128)(2,1)S(1)} %bitcast.17, s32[1024]{0:T(1024)S(1)} %add_select_fusion), kind=kOutput, calls=%fused_computation.5 | convolution fusion | flops 537919488 | bytes 1576960 | tf_op jit(solution)/shard_map/dot_general | solution.py:332
  9.7 0.4 fusion.32
  10.1 0.4 fusion.33
  10.6 0.4 add_add_fusion
  11.0 0.9 %fusion.15 = f32[32,128]{1,0:T(8,128)S(1)} fusion(f32[1024,256]{1,0:T(8,128)S(1)} %fusion.1, f32[1024,384]{1,0:T(8,128)S(1)} %add_add_fusion, s32[1024]{0:T(1024)S(1)} %select_reduce_fusion, pred[1024]{0:T(1024)(128)(4,1)S(1)} %get-tuple-element.26), kind=kOutput, calls=%fused_computation.22 | convolution fusion | flops 50626560 | bytes 1594368 | tf_op jit(solution)/shard_map/dot_general | solution.py:337
  11.9 0.9 %fusion.20 = f32[32,128]{1,0:T(8,128)S(1)} fusion(f32[1024,256]{1,0:T(8,128)S(1)} %fusion.2, f32[1024,384]{1,0:T(8,128)S(1)} %add_add_fusion, s32[1024]{0:T(1024)S(1)} %select_reduce_fusion, pred[1024]{0:T(1024)(128)(4,1)S(1)} %get-tuple-element.26), kind=kOutput, calls=%fused_computation.27 | convolution fusion | flops 50626560 | bytes 1594368 | tf_op jit(solution)/shard_map/dot_general | solution.py:337
  12.7 0.9 %fusion.25 = f32[32,128]{1,0:T(8,128)S(1)} fusion(f32[1024,256]{1,0:T(8,128)S(1)} %fusion.3, f32[1024,384]{1,0:T(8,128)S(1)} %add_add_fusion, s32[1024]{0:T(1024)S(1)} %select_reduce_fusion, pred[1024]{0:T(1024)(128)(4,1)S(1)} %get-tuple-element.26), kind=kOutput, calls=%fused_computation.32 | convolution fusion | flops 50626560 | bytes 1594368 | tf_op jit(solution)/shard_map/dot_general | solution.py:337
  13.6 0.6 %pad_maximum_fusion.refs_0_ = f32[32,384]{1,0:T(8,128)} fusion(f32[32,128]{1,0:T(8,128)S(1)} %fusion.15, f32[32,128]{1,0:T(8,128)S(1)} %fusion.20, f32[32,128]{1,0:T(8,128)S(1)} %fusion.25), kind=kLoop, calls=%fused_computation.57 | loop fusion | flops 24576 | bytes 98304 | tf_op jit(solution)/shard_map/concatenate | solution.py:338
  14.3 31.8 %shard_map.113 = (f32[32,384]{1,0:T(8,128)}, f32[32,1,1024]{2,1,0:T(1,128)}, f32[3,16,64,256]{3,2,1,0:T(8,128)}) custom-call(f32[32,384]{1,0:T(8,128)} %pad_maximum_fusion.refs_0_, f32[1,1024]{1,0:T(1,128)} %refs_1_.1, f32[3,16,64,256]{3,2,1,0:T(8,128)} %refs_2_.1), custom_call_target="tpu_custom_call" | custom-call | tf_op jit(solution)/shard_map/pallas_call | solution.py:187
  46.0 1.2 %fusion.13 = f32[32,1024]{1,0:T(8,128)S(1)} fusion(bf16[384,1024]{1,0:T(8,128)(2,1)S(1)} %copy-done, f32[32,1,1024]{2,1,0:T(1,128)} %get-tuple-element.18, f32[1024]{0:T(1024)S(1)} %copy-done.4, f32[32,384]{1,0:T(8,128)} %get-tuple-element.19), kind=kOutput, calls=%fused_computation.18 | convolution fusion | flops 25321472 | bytes 1101824 | tf_op jit(solution)/shard_map/dot_general | solution.py:342
  47.2 0.6 %constant_dynamic-slice_fusion = f32[1,1024]{1,0:T(1,128)} fusion(f32[32,1024]{1,0:T(8,128)S(1)} %fusion.13, s32[]{:T(128)S(6)} %select_n.39), kind=kLoop, calls=%fused_computation.75 | loop fusion | bytes 8196 | tf_op jit(solution)/shard_map/dynamic_slice | solution.py:347
  47.8 4.9 %convolution_convert_fusion = bf16[32,4096]{1,0:T(8,128)(2,1)S(1)} fusion(bf16[1024,4096]{1,0:T(8,128)(2,1)} %param.15, f32[32,1024]{1,0:T(8,128)S(1)} %fusion.13), kind=kOutput, calls=%fused_computation | convolution fusion | flops 268599296 | bytes 8781824 | tf_op jit(solution)/shard_map/dot_general | solution.py:344
  52.9 1.5 %broadcast_select_fusion = (bf16[1024,128]{1,0:T(8,128)(2,1)S(1)}, bf16[1024,128]{1,0:T(8,128)(2,1)S(1)}) fusion(pred[1024]{0:T(1024)(128)(4,1)S(1)} %get-tuple-element.25, pred[1024]{0:T(1024)(128)(4,1)S(1)} %get-tuple-element.26, bf16[1024,128]{1,0:T(8,128)(2,1)S(1)} %reshape.70, s32[1024]{0:T(1024)S(1)} %multiply_add_fusion), kind=kOutput, calls=%fused_computation.48 | convolution fusion | flops 269877248 | bytes 792576 | tf_op jit(solution)/shard_map/dot_general | solution.py:350
  54.4 0.8 %fusion.10 = f32[1024,256]{1,0:T(8,128)S(1)} fusion(s32[1024]{0:T(1024)S(1)} %add_select_fusion, bf16[1024,128]{1,0:T(8,128)(2,1)S(1)} %get-tuple-element.24, bf16[1024,128]{1,0:T(8,128)(2,1)S(1)} %get-tuple-element.23), kind=kOutput, calls=%fused_computation.14 | convolution fusion | flops 539230208 | bytes 1576960 | tf_op jit(solution)/shard_map/dot_general | solution.py:352
  55.2 1.1 %copy-done.1 = f32[3,16,64,256]{3,2,1,0:T(8,128)S(1)} copy-done((f32[3,16,64,256]{3,2,1,0:T(8,128)S(1)}, f32[3,16,64,256]{3,2,1,0:T(8,128)}, u32[]{:S(2)}) %copy-start.1) | copy-done | bytes 3145752
  56.3 0.3 add_dynamic-update-slice_fusion
  56.6 1.7 %copy.19 = f32[3,16,64,256]{3,2,1,0:T(8,128)} copy(f32[3,16,64,256]{3,2,1,0:T(8,128)S(1)} %add_dynamic-update-slice_fusion) | data formatting | bytes 6291456
  (11 shorter events, 0.3 us)
Async XLA Ops:
  0.6 45.4 %copy-start = (bf16[384,1024]{1,0:T(8,128)(2,1)S(1)}, bf16[384,1024]{1,0:T(8,128)(2,1)}, u32[]{:S(2)}) copy-start(bf16[384,1024]{1,0:T(8,128)(2,1)} %param.14) | copy-start | bytes 2359300
  8.4 1.3 %copy-start.2 = (f32[32,384]{1,0:T(8,128)S(1)}, f32[32,384]{1,0:T(8,128)}, u32[]{:S(2)}) copy-start(f32[32,384]{1,0:T(8,128)} %param.13) | copy-start | bytes 147460
  8.4 1.3 %copy-start.3 = (s32[1024]{0:T(1024)S(1)}, s32[1024]{0:T(1024)}, u32[]{:S(2)}) copy-start(s32[1024]{0:T(1024)} %param.21) | copy-start | bytes 12292
  11.0 35.0 %copy-start.4 = (f32[1024]{0:T(1024)S(1)}, f32[1024]{0:T(1024)}, u32[]{:S(2)}) copy-start(f32[1024]{0:T(1024)} %param.16) | copy-start | bytes 12292
  54.4 1.9 %copy-start.1 = (f32[3,16,64,256]{3,2,1,0:T(8,128)S(1)}, f32[3,16,64,256]{3,2,1,0:T(8,128)}, u32[]{:S(2)}) copy-start(f32[3,16,64,256]{3,2,1,0:T(8,128)} %get-tuple-element.17) | copy-start | bytes 9437188

commit v7 on v6

--- a/solution.py
+++ b/solution.py
@@ -315,11 +315,14 @@
     slots = jnp.sum(rotor_hot * slot_of_rotor[None, :], axis=1)
     sub_range = jnp.arange(NSUB, dtype=jnp.int32)
     sub_hot = (entry_sub[:, None] == sub_range[None, :]).astype(jnp.bfloat16)
-    high = shape_weight.astype(jnp.bfloat16)
-    rest = shape_weight - high.astype(jnp.float32)
-    middle = rest.astype(jnp.bfloat16)
-    low = (rest - middle.astype(jnp.float32)).astype(jnp.bfloat16)
-    gains = [jnp.dot(sub_hot, part, preferred_element_type=jnp.float32) for part in (high, middle, low)]
+    high = lax.reduce_precision(shape_weight, exponent_bits=8, mantissa_bits=7)
+    rest = shape_weight - high
+    middle = lax.reduce_precision(rest, exponent_bits=8, mantissa_bits=7)
+    low = rest - middle
+    gains = [
+        jnp.dot(sub_hot, part.astype(jnp.bfloat16), preferred_element_type=jnp.float32)
+        for part in (high, middle, low)
+    ]
     gains = (gains[0] + gains[1]) + gains[2]
     slot_hot = (slots[:, None] == jnp.arange(R, dtype=jnp.int32)[None, :]).astype(jnp.float32)
     cells_xy = local_x * local_y

time: 58.6 us -> 58.6 us (level)
  no operation moved by 1% of the time
where the time goes in v7:
time: 58.6 us; the launch traced here: 58.2 us
  Pallas kernels  31.8 us (54%)
  matrix products  16.1 us (27%)
  other arithmetic  5.97 us (10%)
  local copies, waits for them, and re-layouts  3.6 us (6%)
  between operations  0.81 us (1%)
    pallas_call x1, Pallas kernels, reduce_step(): pl.pallas_call(lambda *refs: step_kernel(rounds, *refs), out_shape=(jax.S...  31.8 us
    dot_general x1, matrix products, on_device(): jnp.dot(all_new.astype(jnp.bfloat16), w_out, preferred_element_type=jnp.f...  4.93 us
    dot_general x3, matrix products, on_device(): both = jnp.dot(place_hot.T, cells, preferred_element_type=jnp.float32)  3.82 us
    unnamed x11, local copies, waits for them, and re-layouts  2.76 us
    dot_general x3, matrix products, on_device(): jnp.dot(slot_hot.T, weighted, precision=lax.Precision.HIGHEST)  2.62 us
    another operation x1, other arithmetic  2.1 us
    dot_general x1, matrix products, on_device(): jnp.dot(row_hot, flat, preferred_element_type=jnp.float32)  1.49 us
    dot_general x3, matrix products, on_device(): jnp.dot(sub_hot, part.astype(jnp.bfloat16), preferred_element_type=jnp.fl...  1.26 us

profile of v7, /device:TPU:1, one launch (start us, length us, event | category | flops | bytes accessed | tf_op | source)
XLA Modules:
  0.0 58.2 jit_solution(15122863195200570799)
XLA Ops:
  0.6 0.8 %broadcast_compare_fusion.1 = (pred[1024]{0:T(1024)(128)(4,1)S(1)}, pred[1024]{0:T(1024)(128)(4,1)S(1)}) fusion(s32[1024]{0:T(1024)} %param.20), kind=kLoop, calls=%fused_computation.75 | loop fusion | flops 13312 | bytes 6144 | tf_op jit(solution)/shard_map/eq | solution.py:354
  1.4 0.8 %select_reduce_fusion = s32[1024]{0:T(1024)S(1)} fusion(s32[32]{0:T(128)} %param.18, s32[1024]{0:T(1024)} %bitcast.20), kind=kLoop, calls=%fused_computation.54 | loop fusion | flops 97280 | bytes 8320 | tf_op jit(solution)/shard_map/reduce_sum | solution.py:315
  2.2 0.7 %add_select_fusion = s32[1024]{0:T(1024)S(1)} fusion(s32[1024]{0:T(1024)} %param.20), kind=kLoop, calls=%fused_computation.65 | loop fusion | flops 15360 | bytes 8192 | tf_op jit(solution)/shard_map/jit(floor_divide)/jit(_where)/select_n | solution.py:331
  2.9 0.7 %multiply_add_fusion = s32[1024]{0:T(1024)S(1)} fusion(s32[1024]{0:T(1024)} %param.21, s32[1024]{0:T(1024)S(1)} %select_reduce_fusion), kind=kLoop, calls=%fused_computation.70 | loop fusion | flops 2048 | bytes 12288 | tf_op jit(solution)/shard_map/add | solution.py:352
  3.6 2.1 %convert.5 = bf16[3,16,64,256]{3,2,1,0:T(8,128)(2,1)S(1)} convert(f32[3,16,64,256]{3,2,1,0:T(8,128)} %refs_2_.1) | non-fusion elementwise | flops 786432 | bytes 4718592 | tf_op jit(solution)/shard_map/convert.2
  5.8 1.3 %fusion.1 = f32[1024,256]{1,0:T(8,128)S(1)} fusion(bf16[1024,256]{1,0:T(8,128)(2,1)S(1)} %bitcast.19, s32[1024]{0:T(1024)S(1)} %add_select_fusion), kind=kOutput, calls=%fused_computation.4 | convolution fusion | flops 537919488 | bytes 1576960 | tf_op jit(solution)/shard_map/dot_general | solution.py:335
  7.1 1.3 %fusion.3 = f32[1024,256]{1,0:T(8,128)S(1)} fusion(bf16[1024,256]{1,0:T(8,128)(2,1)S(1)} %bitcast.18, s32[1024]{0:T(1024)S(1)} %add_select_fusion), kind=kOutput, calls=%fused_computation.6 | convolution fusion | flops 537919488 | bytes 1576960 | tf_op jit(solution)/shard_map/dot_general | solution.py:335
  8.4 1.3 %fusion.2 = f32[1024,256]{1,0:T(8,128)S(1)} fusion(bf16[1024,256]{1,0:T(8,128)(2,1)S(1)} %bitcast.17, s32[1024]{0:T(1024)S(1)} %add_select_fusion), kind=kOutput, calls=%fused_computation.5 | convolution fusion | flops 537919488 | bytes 1576960 | tf_op jit(solution)/shard_map/dot_general | solution.py:335
  9.7 0.4 fusion.32
  10.1 0.4 fusion.33
  10.6 0.4 add_add_fusion
  11.0 0.9 %fusion.15 = f32[32,128]{1,0:T(8,128)S(1)} fusion(f32[1024,256]{1,0:T(8,128)S(1)} %fusion.1, f32[1024,384]{1,0:T(8,128)S(1)} %add_add_fusion, s32[1024]{0:T(1024)S(1)} %select_reduce_fusion, pred[1024]{0:T(1024)(128)(4,1)S(1)} %get-tuple-element.26), kind=kOutput, calls=%fused_computation.22 | convolution fusion | flops 50626560 | bytes 1594368 | tf_op jit(solution)/shard_map/dot_general | solution.py:340
  11.9 0.9 %fusion.20 = f32[32,128]{1,0:T(8,128)S(1)} fusion(f32[1024,256]{1,0:T(8,128)S(1)} %fusion.2, f32[1024,384]{1,0:T(8,128)S(1)} %add_add_fusion, s32[1024]{0:T(1024)S(1)} %select_reduce_fusion, pred[1024]{0:T(1024)(128)(4,1)S(1)} %get-tuple-element.26), kind=kOutput, calls=%fused_computation.27 | convolution fusion | flops 50626560 | bytes 1594368 | tf_op jit(solution)/shard_map/dot_general | solution.py:340
  12.7 0.9 %fusion.25 = f32[32,128]{1,0:T(8,128)S(1)} fusion(f32[1024,256]{1,0:T(8,128)S(1)} %fusion.3, f32[1024,384]{1,0:T(8,128)S(1)} %add_add_fusion, s32[1024]{0:T(1024)S(1)} %select_reduce_fusion, pred[1024]{0:T(1024)(128)(4,1)S(1)} %get-tuple-element.26), kind=kOutput, calls=%fused_computation.32 | convolution fusion | flops 50626560 | bytes 1594368 | tf_op jit(solution)/shard_map/dot_general | solution.py:340
  13.6 0.6 %pad_maximum_fusion.refs_0_ = f32[32,384]{1,0:T(8,128)} fusion(f32[32,128]{1,0:T(8,128)S(1)} %fusion.15, f32[32,128]{1,0:T(8,128)S(1)} %fusion.20, f32[32,128]{1,0:T(8,128)S(1)} %fusion.25), kind=kLoop, calls=%fused_computation.62 | loop fusion | flops 24576 | bytes 98304 | tf_op jit(solution)/shard_map/concatenate | solution.py:341
  14.3 31.8 %shard_map.113 = (f32[32,384]{1,0:T(8,128)}, f32[32,1,1024]{2,1,0:T(1,128)}, f32[3,16,64,256]{3,2,1,0:T(8,128)}) custom-call(f32[32,384]{1,0:T(8,128)} %pad_maximum_fusion.refs_0_, f32[1,1024]{1,0:T(1,128)} %refs_1_.1, f32[3,16,64,256]{3,2,1,0:T(8,128)} %refs_2_.1), custom_call_target="tpu_custom_call" | custom-call | tf_op jit(solution)/shard_map/pallas_call | solution.py:187
  46.0 1.2 %fusion.13 = f32[32,1024]{1,0:T(8,128)S(1)} fusion(bf16[384,1024]{1,0:T(8,128)(2,1)S(1)} %copy-done, f32[32,1,1024]{2,1,0:T(1,128)} %get-tuple-element.18, f32[1024]{0:T(1024)S(1)} %copy-done.4, f32[32,384]{1,0:T(8,128)} %get-tuple-element.19), kind=kOutput, calls=%fused_computation.18 | convolution fusion | flops 25321472 | bytes 1101824 | tf_op jit(solution)/shard_map/dot_general | solution.py:345
  47.2 0.6 %constant_dynamic-slice_fusion = f32[1,1024]{1,0:T(1,128)} fusion(f32[32,1024]{1,0:T(8,128)S(1)} %fusion.13, s32[]{:T(128)S(6)} %select_n.39), kind=kLoop, calls=%fused_computation.76 | loop fusion | bytes 8196 | tf_op jit(solution)/shard_map/dynamic_slice | solution.py:350
  47.8 4.9 %convolution_convert_fusion = bf16[32,4096]{1,0:T(8,128)(2,1)S(1)} fusion(bf16[1024,4096]{1,0:T(8,128)(2,1)} %param.15, f32[32,1024]{1,0:T(8,128)S(1)} %fusion.13), kind=kOutput, calls=%fused_computation | convolution fusion | flops 268599296 | bytes 8781824 | tf_op jit(solution)/shard_map/dot_general | solution.py:347
  52.9 1.5 %broadcast_select_fusion = (bf16[1024,128]{1,0:T(8,128)(2,1)S(1)}, bf16[1024,128]{1,0:T(8,128)(2,1)S(1)}) fusion(pred[1024]{0:T(1024)(128)(4,1)S(1)} %get-tuple-element.25, pred[1024]{0:T(1024)(128)(4,1)S(1)} %get-tuple-element.26, bf16[1024,128]{1,0:T(8,128)(2,1)S(1)} %reshape.70, s32[1024]{0:T(1024)S(1)} %multiply_add_fusion), kind=kOutput, calls=%fused_computation.48 | convolution fusion | flops 269877248 | bytes 792576 | tf_op jit(solution)/shard_map/dot_general | solution.py:353
  54.4 0.8 %fusion.10 = f32[1024,256]{1,0:T(8,128)S(1)} fusion(s32[1024]{0:T(1024)S(1)} %add_select_fusion, bf16[1024,128]{1,0:T(8,128)(2,1)S(1)} %get-tuple-element.24, bf16[1024,128]{1,0:T(8,128)(2,1)S(1)} %get-tuple-element.23), kind=kOutput, calls=%fused_computation.14 | convolution fusion | flops 539230208 | bytes 1576960 | tf_op jit(solution)/shard_map/dot_general | solution.py:355
  55.2 1.1 %copy-done.1 = f32[3,16,64,256]{3,2,1,0:T(8,128)S(1)} copy-done((f32[3,16,64,256]{3,2,1,0:T(8,128)S(1)}, f32[3,16,64,256]{3,2,1,0:T(8,128)}, u32[]{:S(2)}) %copy-start.1) | copy-done | bytes 3145752
  56.3 0.3 add_dynamic-update-slice_fusion
  56.6 1.7 %copy.19 = f32[3,16,64,256]{3,2,1,0:T(8,128)} copy(f32[3,16,64,256]{3,2,1,0:T(8,128)S(1)} %add_dynamic-update-slice_fusion) | data formatting | bytes 6291456
  (11 shorter events, 0.3 us)
Async XLA Ops:
  0.6 45.4 %copy-start = (bf16[384,1024]{1,0:T(8,128)(2,1)S(1)}, bf16[384,1024]{1,0:T(8,128)(2,1)}, u32[]{:S(2)}) copy-start(bf16[384,1024]{1,0:T(8,128)(2,1)} %param.14) | copy-start | bytes 2359300
  8.4 1.3 %copy-start.2 = (f32[32,384]{1,0:T(8,128)S(1)}, f32[32,384]{1,0:T(8,128)}, u32[]{:S(2)}) copy-start(f32[32,384]{1,0:T(8,128)} %param.13) | copy-start | bytes 147460
  8.4 1.3 %copy-start.3 = (s32[1024]{0:T(1024)S(1)}, s32[1024]{0:T(1024)}, u32[]{:S(2)}) copy-start(s32[1024]{0:T(1024)} %param.21) | copy-start | bytes 12292
  11.0 35.0 %copy-start.4 = (f32[1024]{0:T(1024)S(1)}, f32[1024]{0:T(1024)}, u32[]{:S(2)}) copy-start(f32[1024]{0:T(1024)} %param.16) | copy-start | bytes 12292
  54.4 1.9 %copy-start.1 = (f32[3,16,64,256]{3,2,1,0:T(8,128)S(1)}, f32[3,16,64,256]{3,2,1,0:T(8,128)}, u32[]{:S(2)}) copy-start(f32[3,16,64,256]{3,2,1,0:T(8,128)} %get-tuple-element.17) | copy-start | bytes 9437188

commit v8 on v7

--- a/solution.py
+++ b/solution.py
@@ -150,6 +150,16 @@
                 )
                 block.start()
                 copies.append(block)
+        if r == 1:
+            for send_if, recv_if, face in face_copies:
+
+                @pl.when(send_if)
+                def _():
+                    face.wait_send()
+
+                @pl.when(recv_if)
+                def _():
+                    face.wait_recv()
         if chunks[r] is not None:
             first, last = chunks[r]
 
@@ -167,16 +177,6 @@
         else:
             total = (pooled_ref[...] + held[r, 1]) + (held[r, 0] + held[r, 2])
         pooled_ref[...] = total
-        if r == 0:
-            for send_if, recv_if, copy in face_copies:
-
-                @pl.when(send_if)
-                def _():
-                    copy.wait_send()
-
-                @pl.when(recv_if)
-                def _():
-                    copy.wait_recv()
 
 
 def reduce_step(per_rotor, rotor_states, velocity):

time: 58.6 us -> 55.5 us (0.947)
  Pallas kernels: 31.8 us -> 28.2 us
    pallas_call x1, Pallas kernels: 31.8 us -> 28.2 us  [reduce_step(): pl.pallas_call(lambda *refs: step_kernel(rounds, *refs), out_shape=(jax.S...]
where the time goes in v8:
time: 55.5 us; the launch traced here: 54.7 us
  Pallas kernels  28.2 us (51%)
  matrix products  16.1 us (29%)
  other arithmetic  5.97 us (11%)
  local copies, waits for them, and re-layouts  3.6 us (6%)
  between operations  0.81 us (1%)
    pallas_call x1, Pallas kernels, reduce_step(): pl.pallas_call(lambda *refs: step_kernel(rounds, *refs), out_shape=(jax.S...  28.2 us
    dot_general x1, matrix products, on_device(): jnp.dot(all_new.astype(jnp.bfloat16), w_out, preferred_element_type=jnp.f...  4.93 us
    dot_general x3, matrix products, on_device(): both = jnp.dot(place_hot.T, cells, preferred_element_type=jnp.float32)  3.82 us
    unnamed x11, local copies, waits for them, and re-layouts  2.76 us
    dot_general x3, matrix products, on_device(): jnp.dot(slot_hot.T, weighted, precision=lax.Precision.HIGHEST)  2.62 us
    another operation x1, other arithmetic  2.1 us
    dot_general x1, matrix products, on_device(): jnp.dot(row_hot, flat, preferred_element_type=jnp.float32)  1.49 us
    dot_general x3, matrix products, on_device(): jnp.dot(sub_hot, part.astype(jnp.bfloat16), preferred_element_type=jnp.fl...  1.26 us

profile of v8, /device:TPU:1, one launch (start us, length us, event | category | flops | bytes accessed | tf_op | source)
XLA Modules:
  0.0 54.7 jit_solution(3431189296868497241)
XLA Ops:
  0.6 0.8 %broadcast_compare_fusion.1 = (pred[1024]{0:T(1024)(128)(4,1)S(1)}, pred[1024]{0:T(1024)(128)(4,1)S(1)}) fusion(s32[1024]{0:T(1024)} %param.20), kind=kLoop, calls=%fused_computation.75 | loop fusion | flops 13312 | bytes 6144 | tf_op jit(solution)/shard_map/eq | solution.py:354
  1.4 0.8 %select_reduce_fusion = s32[1024]{0:T(1024)S(1)} fusion(s32[32]{0:T(128)} %param.18, s32[1024]{0:T(1024)} %bitcast.20), kind=kLoop, calls=%fused_computation.54 | loop fusion | flops 97280 | bytes 8320 | tf_op jit(solution)/shard_map/reduce_sum | solution.py:315
  2.2 0.7 %add_select_fusion = s32[1024]{0:T(1024)S(1)} fusion(s32[1024]{0:T(1024)} %param.20), kind=kLoop, calls=%fused_computation.65 | loop fusion | flops 15360 | bytes 8192 | tf_op jit(solution)/shard_map/jit(floor_divide)/jit(_where)/select_n | solution.py:331
  2.9 0.7 %multiply_add_fusion = s32[1024]{0:T(1024)S(1)} fusion(s32[1024]{0:T(1024)} %param.21, s32[1024]{0:T(1024)S(1)} %select_reduce_fusion), kind=kLoop, calls=%fused_computation.70 | loop fusion | flops 2048 | bytes 12288 | tf_op jit(solution)/shard_map/add | solution.py:352
  3.6 2.1 %convert.5 = bf16[3,16,64,256]{3,2,1,0:T(8,128)(2,1)S(1)} convert(f32[3,16,64,256]{3,2,1,0:T(8,128)} %refs_2_.1) | non-fusion elementwise | flops 786432 | bytes 4718592 | tf_op jit(solution)/shard_map/convert.2
  5.8 1.3 %fusion.1 = f32[1024,256]{1,0:T(8,128)S(1)} fusion(bf16[1024,256]{1,0:T(8,128)(2,1)S(1)} %bitcast.19, s32[1024]{0:T(1024)S(1)} %add_select_fusion), kind=kOutput, calls=%fused_computation.4 | convolution fusion | flops 537919488 | bytes 1576960 | tf_op jit(solution)/shard_map/dot_general | solution.py:335
  7.1 1.3 %fusion.3 = f32[1024,256]{1,0:T(8,128)S(1)} fusion(bf16[1024,256]{1,0:T(8,128)(2,1)S(1)} %bitcast.18, s32[1024]{0:T(1024)S(1)} %add_select_fusion), kind=kOutput, calls=%fused_computation.6 | convolution fusion | flops 537919488 | bytes 1576960 | tf_op jit(solution)/shard_map/dot_general | solution.py:335
  8.4 1.3 %fusion.2 = f32[1024,256]{1,0:T(8,128)S(1)} fusion(bf16[1024,256]{1,0:T(8,128)(2,1)S(1)} %bitcast.17, s32[1024]{0:T(1024)S(1)} %add_select_fusion), kind=kOutput, calls=%fused_computation.5 | convolution fusion | flops 537919488 | bytes 1576960 | tf_op jit(solution)/shard_map/dot_general | solution.py:335
  9.7 0.4 fusion.32
  10.1 0.4 fusion.33
  10.6 0.4 add_add_fusion
  11.0 0.9 %fusion.15 = f32[32,128]{1,0:T(8,128)S(1)} fusion(f32[1024,256]{1,0:T(8,128)S(1)} %fusion.1, f32[1024,384]{1,0:T(8,128)S(1)} %add_add_fusion, s32[1024]{0:T(1024)S(1)} %select_reduce_fusion, pred[1024]{0:T(1024)(128)(4,1)S(1)} %get-tuple-element.26), kind=kOutput, calls=%fused_computation.22 | convolution fusion | flops 50626560 | bytes 1594368 | tf_op jit(solution)/shard_map/dot_general | solution.py:340
  11.9 0.9 %fusion.20 = f32[32,128]{1,0:T(8,128)S(1)} fusion(f32[1024,256]{1,0:T(8,128)S(1)} %fusion.2, f32[1024,384]{1,0:T(8,128)S(1)} %add_add_fusion, s32[1024]{0:T(1024)S(1)} %select_reduce_fusion, pred[1024]{0:T(1024)(128)(4,1)S(1)} %get-tuple-element.26), kind=kOutput, calls=%fused_computation.27 | convolution fusion | flops 50626560 | bytes 1594368 | tf_op jit(solution)/shard_map/dot_general | solution.py:340
  12.7 0.9 %fusion.25 = f32[32,128]{1,0:T(8,128)S(1)} fusion(f32[1024,256]{1,0:T(8,128)S(1)} %fusion.3, f32[1024,384]{1,0:T(8,128)S(1)} %add_add_fusion, s32[1024]{0:T(1024)S(1)} %select_reduce_fusion, pred[1024]{0:T(1024)(128)(4,1)S(1)} %get-tuple-element.26), kind=kOutput, calls=%fused_computation.32 | convolution fusion | flops 50626560 | bytes 1594368 | tf_op jit(solution)/shard_map/dot_general | solution.py:340
  13.6 0.6 %pad_maximum_fusion.refs_0_ = f32[32,384]{1,0:T(8,128)} fusion(f32[32,128]{1,0:T(8,128)S(1)} %fusion.15, f32[32,128]{1,0:T(8,128)S(1)} %fusion.20, f32[32,128]{1,0:T(8,128)S(1)} %fusion.25), kind=kLoop, calls=%fused_computation.62 | loop fusion | flops 24576 | bytes 98304 | tf_op jit(solution)/shard_map/concatenate | solution.py:341
  14.3 28.2 %shard_map.113 = (f32[32,384]{1,0:T(8,128)}, f32[32,1,1024]{2,1,0:T(1,128)}, f32[3,16,64,256]{3,2,1,0:T(8,128)}) custom-call(f32[32,384]{1,0:T(8,128)} %pad_maximum_fusion.refs_0_, f32[1,1024]{1,0:T(1,128)} %refs_1_.1, f32[3,16,64,256]{3,2,1,0:T(8,128)} %refs_2_.1), custom_call_target="tpu_custom_call" | custom-call | tf_op jit(solution)/shard_map/pallas_call | solution.py:187
  42.4 1.2 %fusion.13 = f32[32,1024]{1,0:T(8,128)S(1)} fusion(bf16[384,1024]{1,0:T(8,128)(2,1)S(1)} %copy-done, f32[32,1,1024]{2,1,0:T(1,128)} %get-tuple-element.18, f32[1024]{0:T(1024)S(1)} %copy-done.4, f32[32,384]{1,0:T(8,128)} %get-tuple-element.19), kind=kOutput, calls=%fused_computation.18 | convolution fusion | flops 25321472 | bytes 1101824 | tf_op jit(solution)/shard_map/dot_general | solution.py:345
  43.6 0.6 %constant_dynamic-slice_fusion = f32[1,1024]{1,0:T(1,128)} fusion(f32[32,1024]{1,0:T(8,128)S(1)} %fusion.13, s32[]{:T(128)S(6)} %select_n.39), kind=kLoop, calls=%fused_computation.76 | loop fusion | bytes 8196 | tf_op jit(solution)/shard_map/dynamic_slice | solution.py:350
  44.3 4.9 %convolution_convert_fusion = bf16[32,4096]{1,0:T(8,128)(2,1)S(1)} fusion(bf16[1024,4096]{1,0:T(8,128)(2,1)} %param.15, f32[32,1024]{1,0:T(8,128)S(1)} %fusion.13), kind=kOutput, calls=%fused_computation | convolution fusion | flops 268599296 | bytes 8781824 | tf_op jit(solution)/shard_map/dot_general | solution.py:347
  49.3 1.5 %broadcast_select_fusion = (bf16[1024,128]{1,0:T(8,128)(2,1)S(1)}, bf16[1024,128]{1,0:T(8,128)(2,1)S(1)}) fusion(pred[1024]{0:T(1024)(128)(4,1)S(1)} %get-tuple-element.25, pred[1024]{0:T(1024)(128)(4,1)S(1)} %get-tuple-element.26, bf16[1024,128]{1,0:T(8,128)(2,1)S(1)} %reshape.70, s32[1024]{0:T(1024)S(1)} %multiply_add_fusion), kind=kOutput, calls=%fused_computation.48 | convolution fusion | flops 269877248 | bytes 792576 | tf_op jit(solution)/shard_map/dot_general | solution.py:353
  50.8 0.8 %fusion.10 = f32[1024,256]{1,0:T(8,128)S(1)} fusion(s32[1024]{0:T(1024)S(1)} %add_select_fusion, bf16[1024,128]{1,0:T(8,128)(2,1)S(1)} %get-tuple-element.24, bf16[1024,128]{1,0:T(8,128)(2,1)S(1)} %get-tuple-element.23), kind=kOutput, calls=%fused_computation.14 | convolution fusion | flops 539230208 | bytes 1576960 | tf_op jit(solution)/shard_map/dot_general | solution.py:355
  51.6 1.1 %copy-done.1 = f32[3,16,64,256]{3,2,1,0:T(8,128)S(1)} copy-done((f32[3,16,64,256]{3,2,1,0:T(8,128)S(1)}, f32[3,16,64,256]{3,2,1,0:T(8,128)}, u32[]{:S(2)}) %copy-start.1) | copy-done | bytes 3145752
  52.7 0.3 add_dynamic-update-slice_fusion
  53.0 1.7 %copy.19 = f32[3,16,64,256]{3,2,1,0:T(8,128)} copy(f32[3,16,64,256]{3,2,1,0:T(8,128)S(1)} %add_dynamic-update-slice_fusion) | data formatting | bytes 6291456
  (11 shorter events, 0.3 us)
Async XLA Ops:
  0.6 41.8 %copy-start = (bf16[384,1024]{1,0:T(8,128)(2,1)S(1)}, bf16[384,1024]{1,0:T(8,128)(2,1)}, u32[]{:S(2)}) copy-start(bf16[384,1024]{1,0:T(8,128)(2,1)} %param.14) | copy-start | bytes 2359300
  8.4 1.3 %copy-start.2 = (f32[32,384]{1,0:T(8,128)S(1)}, f32[32,384]{1,0:T(8,128)}, u32[]{:S(2)}) copy-start(f32[32,384]{1,0:T(8,128)} %param.13) | copy-start | bytes 147460
  8.4 1.3 %copy-start.3 = (s32[1024]{0:T(1024)S(1)}, s32[1024]{0:T(1024)}, u32[]{:S(2)}) copy-start(s32[1024]{0:T(1024)} %param.21) | copy-start | bytes 12292
  11.0 31.5 %copy-start.4 = (f32[1024]{0:T(1024)S(1)}, f32[1024]{0:T(1024)}, u32[]{:S(2)}) copy-start(f32[1024]{0:T(1024)} %param.16) | copy-start | bytes 12292
  50.8 1.9 %copy-start.1 = (f32[3,16,64,256]{3,2,1,0:T(8,128)S(1)}, f32[3,16,64,256]{3,2,1,0:T(8,128)}, u32[]{:S(2)}) copy-start(f32[3,16,64,256]{3,2,1,0:T(8,128)} %get-tuple-element.17) | copy-start | bytes 9437188

commit v9 on v8

--- a/solution.py
+++ b/solution.py
@@ -77,8 +77,9 @@
     return me - pos * stride + ((pos + shift) % n) * stride
 
 
-def step_kernel(rounds, per_ref, st_ref, vel_ref, pooled_ref, states_ref, adv_ref, held, sends, recvs,
-                st_sends, st_recvs, xlo, xhi, ylo, yhi, face_sends, face_recvs):
+def step_kernel(rounds, per_ref, st_ref, vel_ref, w_in_ref, decay_ref, w_out_hbm, src_ref, own_ref, adv_ref,
+                states_ref, pooled_ref, held, sends, recvs, st_sends, st_recvs, xlo, xhi, ylo, yhi, face_sends,
+                face_recvs, w_out_ref, new_ref, w_sem):
     here = (lax.axis_index("slab"), lax.axis_index("cross"))
     slab, cross = lax.axis_size("slab"), lax.axis_size("cross")
     planes = vel_ref.shape[1]
@@ -121,6 +122,8 @@
 
         face_copies.append((send_if, recv_if, copy))
 
+    w_copy = pltpu.make_async_copy(w_out_hbm, w_out_ref, w_sem)
+    w_copy.start()
     states_ref[pl.ds(s, 1)] = st_ref[...][None]
     pooled_ref[...] = per_ref[...]
     chunks = [None, (0, 6), (6, 11), (11, planes)]
@@ -178,8 +181,22 @@
             total = (pooled_ref[...] + held[r, 1]) + (held[r, 0] + held[r, 2])
         pooled_ref[...] = total
 
-
-def reduce_step(per_rotor, rotor_states, velocity):
+    pooled_b = (pooled_ref[...] * pool_scale).astype(jnp.bfloat16)
+    drive = jnp.dot(pooled_b, w_in_ref[...], preferred_element_type=jnp.float32)
+    decay = decay_ref[...]
+    for k in range(states_ref.shape[0]):
+        row = states_ref[k]
+        new_ref[pl.ds(k, 1), :] = row + state_step * (drive[k:k + 1] - decay * row)
+    slot_rows = lax.broadcasted_iota(jnp.int32, drive.shape, 0)
+    own_drive = jnp.sum(jnp.where(slot_rows == s, drive, 0.0), axis=0, keepdims=True)
+    own = st_ref[...]
+    own_ref[...] = own + state_step * (own_drive - decay * own)
+    w_copy.wait()
+    src_ref[...] = jnp.dot(
+        new_ref[...].astype(jnp.bfloat16), w_out_ref[...], preferred_element_type=jnp.float32
+    ).astype(jnp.bfloat16)
+
+def reduce_step(per_rotor, rotor_states, velocity, w_in, decay, w_out):
     slab, cross = lax.axis_size("slab"), lax.axis_size("cross")
     rounds = ring_rounds(slab, cross)
     vmem = pl.BlockSpec(memory_space=pltpu.VMEM)
@@ -187,13 +204,15 @@
     return pl.pallas_call(
         lambda *refs: step_kernel(rounds, *refs),
         out_shape=(
-            jax.ShapeDtypeStruct(per_rotor.shape, jnp.float32),
-            jax.ShapeDtypeStruct((slab,) + rotor_states.shape, jnp.float32),
+            jax.ShapeDtypeStruct((slab, w_out.shape[1]), jnp.bfloat16),
+            jax.ShapeDtypeStruct(rotor_states.shape, jnp.float32),
             jax.ShapeDtypeStruct(velocity.shape, jnp.float32),
         ),
-        in_specs=[vmem, vmem, vmem],
+        in_specs=[vmem] * 5 + [pl.BlockSpec(memory_space=pl.ANY)],
         out_specs=(vmem, vmem, vmem),
         scratch_shapes=[
+            pltpu.VMEM((slab,) + rotor_states.shape, jnp.float32),
+            pltpu.VMEM(per_rotor.shape, jnp.float32),
             pltpu.VMEM((len(rounds), 3) + per_rotor.shape, jnp.float32),
             pltpu.SemaphoreType.DMA((len(rounds), 3)),
             pltpu.SemaphoreType.DMA((len(rounds), 3)),
@@ -205,10 +224,12 @@
             pltpu.VMEM((3, planes, 1, nz), jnp.float32),
             pltpu.SemaphoreType.DMA((4,)),
             pltpu.SemaphoreType.DMA((4,)),
+            pltpu.VMEM(w_out.shape, w_out.dtype),
+            pltpu.VMEM((slab, w_out.shape[0]), jnp.float32),
+            pltpu.SemaphoreType.DMA(()),
         ],
         compiler_params=pltpu.CompilerParams(collective_id=0, has_side_effects=True),
-    )(per_rotor, rotor_states, velocity)
-
+    )(per_rotor, rotor_states, velocity, w_in, decay.reshape(1, -1), w_out)
 
 def stencil_plane(x, planes, vel_ref, xlo_ref, xhi_ref, ylo_ref, yhi_ref):
     _, _, ny, nz = vel_ref.shape
@@ -339,15 +360,7 @@
         weighted = gains[:, c * TILE:(c + 1) * TILE] * picked
         per_rotor.append(jnp.dot(slot_hot.T, weighted, precision=lax.Precision.HIGHEST))
     per_rotor = jnp.concatenate(per_rotor, axis=1)
-    pooled, all_states, advanced = reduce_step(per_rotor, rotor_states, velocity)
-    all_states = all_states.reshape(-1, rotor_states.shape[1])
-    pooled_b = (pooled * pool_scale).astype(jnp.bfloat16)
-    drive = jnp.dot(pooled_b, w_in, preferred_element_type=jnp.float32)
-    all_new = all_states + state_step * (drive - decay[None, :] * all_states)
-    all_sources = jnp.dot(
-        all_new.astype(jnp.bfloat16), w_out, preferred_element_type=jnp.float32
-    ).astype(jnp.bfloat16)
-    new_states = lax.dynamic_slice_in_dim(all_new, lax.axis_index("slab"), 1, axis=0)
+    all_sources, new_states, advanced = reduce_step(per_rotor, rotor_states, velocity, w_in, decay, w_out)
     flat = all_sources.reshape(R * NSUB, TILE)
     row_hot = ((slots * NSUB + entry_sub)[:, None] == jnp.arange(R * NSUB, dtype=jnp.int32)[None, :]).astype(jnp.bfloat16)
     rows = jnp.dot(row_hot, flat, preferred_element_type=jnp.float32).astype(jnp.bfloat16)

time: 55.5 us -> 51.4 us (0.926)
  matrix products: 16.1 us -> 9.99 us
  Pallas kernels: 28.2 us -> 29.3 us
  local copies, waits for them, and re-layouts: 3.6 us -> 4.52 us
    dot_general x2 -> x0, matrix products: 6.11 us -> none  [the longest x1 4.93 us: on_device(): jnp.dot(all_new.astype(jnp.bfloat16), w_out, preferred_element_type=jnp.f...]
    pallas_call x1, Pallas kernels: 28.2 us -> 29.3 us  [reduce_step(): pl.pallas_call(lambda *refs: step_kernel(rounds, *refs), out_shape=(jax.S...]
    reshape x1, local copies, waits for them, and re-layouts: 0.13 us -> 1.07 us  [on_device(): flat = all_sources.reshape(R * NSUB, TILE)]
    dynamic_slice x1 -> x0, local copies, waits for them, and re-layouts: 0.61 us -> none  [on_device(): lax.dynamic_slice_in_dim(all_new, lax.axis_index('slab'), 1, axis=0)]
    unnamed x11 -> x10, local copies, waits for them, and re-layouts: 2.76 us -> 3.34 us
where the time goes in v9:
time: 51.4 us; the launch traced here: 50.5 us
  Pallas kernels  29.3 us (57%)
  matrix products  9.99 us (19%)
  other arithmetic  5.9 us (11%)
  local copies, waits for them, and re-layouts  4.52 us (9%)
  between operations  0.77 us (1%)
    pallas_call x1, Pallas kernels, reduce_step(): pl.pallas_call(lambda *refs: step_kernel(rounds, *refs), out_shape=(jax.S...  29.3 us
    dot_general x3, matrix products, on_device(): both = jnp.dot(place_hot.T, cells, preferred_element_type=jnp.float32)  3.82 us
    unnamed x10, local copies, waits for them, and re-layouts  3.34 us
    dot_general x3, matrix products, on_device(): jnp.dot(slot_hot.T, weighted, precision=lax.Precision.HIGHEST)  2.62 us
    another operation x1, other arithmetic  2.1 us
    dot_general x1, matrix products, on_device(): jnp.dot(row_hot, flat, preferred_element_type=jnp.float32)  1.49 us
    dot_general x3, matrix products, on_device(): jnp.dot(sub_hot, part.astype(jnp.bfloat16), preferred_element_type=jnp.fl...  1.26 us
    reshape x1, local copies, waits for them, and re-layouts, on_device(): flat = all_sources.reshape(R * NSUB, TILE)  1.07 us

profile of v9, /device:TPU:1, one launch (start us, length us, event | category | flops | bytes accessed | tf_op | source)
XLA Modules:
  0.0 50.5 jit_solution(17755837856107138646)
XLA Ops:
  0.6 0.7 %broadcast_compare_fusion.1 = (pred[1024]{0:T(1024)(128)(4,1)S(1)}, pred[1024]{0:T(1024)(128)(4,1)S(1)}) fusion(s32[1024]{0:T(1024)} %param.20), kind=kLoop, calls=%fused_computation.67 | loop fusion | flops 13312 | bytes 6144 | tf_op jit(solution)/shard_map/eq | solution.py:367
  1.3 0.8 %select_reduce_fusion = s32[1024]{0:T(1024)S(1)} fusion(s32[32]{0:T(128)} %param.18, s32[1024]{0:T(1024)} %bitcast.15), kind=kLoop, calls=%fused_computation.49 | loop fusion | flops 97280 | bytes 8320 | tf_op jit(solution)/shard_map/reduce_sum | solution.py:336
  2.1 0.7 %add_select_fusion = s32[1024]{0:T(1024)S(1)} fusion(s32[1024]{0:T(1024)} %param.20), kind=kLoop, calls=%fused_computation.57 | loop fusion | flops 15360 | bytes 8192 | tf_op jit(solution)/shard_map/jit(floor_divide)/jit(_where)/select_n | solution.py:352
  2.8 0.7 %multiply_add_fusion = s32[1024]{0:T(1024)S(1)} fusion(s32[1024]{0:T(1024)} %param.21, s32[1024]{0:T(1024)S(1)} %select_reduce_fusion), kind=kLoop, calls=%fused_computation.62 | loop fusion | flops 2048 | bytes 12288 | tf_op jit(solution)/shard_map/add | solution.py:365
  3.5 2.1 %convert.5 = bf16[3,16,64,256]{3,2,1,0:T(8,128)(2,1)S(1)} convert(f32[3,16,64,256]{3,2,1,0:T(8,128)} %refs_2_.1) | non-fusion elementwise | flops 786432 | bytes 4718592 | tf_op jit(solution)/shard_map/convert.2
  5.6 0.1 fusion.46
  5.7 1.3 %fusion.1 = f32[1024,256]{1,0:T(8,128)S(1)} fusion(bf16[1024,256]{1,0:T(8,128)(2,1)S(1)} %bitcast.13, s32[1024]{0:T(1024)S(1)} %add_select_fusion), kind=kOutput, calls=%fused_computation.3 | convolution fusion | flops 537919488 | bytes 1576960 | tf_op jit(solution)/shard_map/dot_general | solution.py:356
  7.0 1.3 %fusion.3 = f32[1024,256]{1,0:T(8,128)S(1)} fusion(bf16[1024,256]{1,0:T(8,128)(2,1)S(1)} %bitcast.12, s32[1024]{0:T(1024)S(1)} %add_select_fusion), kind=kOutput, calls=%fused_computation.5 | convolution fusion | flops 537919488 | bytes 1576960 | tf_op jit(solution)/shard_map/dot_general | solution.py:356
  8.3 1.3 %fusion.2 = f32[1024,256]{1,0:T(8,128)S(1)} fusion(bf16[1024,256]{1,0:T(8,128)(2,1)S(1)} %bitcast.11, s32[1024]{0:T(1024)S(1)} %add_select_fusion), kind=kOutput, calls=%fused_computation.4 | convolution fusion | flops 537919488 | bytes 1576960 | tf_op jit(solution)/shard_map/dot_general | solution.py:356
  9.6 0.4 fusion.30
  10.0 0.4 fusion.31
  10.5 0.4 add_add_fusion
  10.9 0.9 %fusion.13 = f32[32,128]{1,0:T(8,128)S(1)} fusion(f32[1024,256]{1,0:T(8,128)S(1)} %fusion.1, f32[1024,384]{1,0:T(8,128)S(1)} %add_add_fusion, s32[1024]{0:T(1024)S(1)} %select_reduce_fusion, pred[1024]{0:T(1024)(128)(4,1)S(1)} %get-tuple-element.26), kind=kOutput, calls=%fused_computation.18 | convolution fusion | flops 50626560 | bytes 1594368 | tf_op jit(solution)/shard_map/dot_general | solution.py:361
  11.8 0.9 %fusion.18 = f32[32,128]{1,0:T(8,128)S(1)} fusion(f32[1024,256]{1,0:T(8,128)S(1)} %fusion.2, f32[1024,384]{1,0:T(8,128)S(1)} %add_add_fusion, s32[1024]{0:T(1024)S(1)} %select_reduce_fusion, pred[1024]{0:T(1024)(128)(4,1)S(1)} %get-tuple-element.26), kind=kOutput, calls=%fused_computation.23 | convolution fusion | flops 50626560 | bytes 1594368 | tf_op jit(solution)/shard_map/dot_general | solution.py:361
  12.6 0.9 %fusion.23 = f32[32,128]{1,0:T(8,128)S(1)} fusion(f32[1024,256]{1,0:T(8,128)S(1)} %fusion.3, f32[1024,384]{1,0:T(8,128)S(1)} %add_add_fusion, s32[1024]{0:T(1024)S(1)} %select_reduce_fusion, pred[1024]{0:T(1024)(128)(4,1)S(1)} %get-tuple-element.26), kind=kOutput, calls=%fused_computation.28 | convolution fusion | flops 50626560 | bytes 1594368 | tf_op jit(solution)/shard_map/dot_general | solution.py:361
  13.5 0.6 %pad_maximum_fusion.refs_0_ = f32[32,384]{1,0:T(8,128)} fusion(f32[32,128]{1,0:T(8,128)S(1)} %fusion.13, f32[32,128]{1,0:T(8,128)S(1)} %fusion.18, f32[32,128]{1,0:T(8,128)S(1)} %fusion.23), kind=kLoop, calls=%fused_computation.56 | loop fusion | flops 24576 | bytes 98304 | tf_op jit(solution)/shard_map/concatenate | solution.py:362
  14.2 29.3 %shard_map.113 = (bf16[32,4096]{1,0:T(8,128)(2,1)}, f32[1,1024]{1,0:T(1,128)}, f32[3,16,64,256]{3,2,1,0:T(8,128)}) custom-call(f32[32,384]{1,0:T(8,128)} %pad_maximum_fusion.refs_0_, f32[1,1024]{1,0:T(1,128)} %refs_1_.1, f32[3,16,64,256]{3,2,1,0:T(8,128)} %refs_2_.1, bf16[384,1024]{1,0:T(8,128)(2,1)} %refs_3_.1, f32[1,1024]{1,0:T(1,128)} %bitcast.14, ...), custom_call_target="tpu_custom_call" | custom-call | tf_op jit(solution)/shard_map/pallas_call | solution.py:204
  43.5 1.1 %reshape.69 = bf16[1024,128]{1,0:T(8,128)(2,1)S(1)} reshape(bf16[32,4096]{1,0:T(8,128)(2,1)} %get-tuple-element.18) | data formatting | bytes 524288 | tf_op jit(solution)/shard_map/reshape | solution.py:364
  44.5 1.5 %broadcast_select_fusion = (bf16[1024,128]{1,0:T(8,128)(2,1)S(1)}, bf16[1024,128]{1,0:T(8,128)(2,1)S(1)}) fusion(pred[1024]{0:T(1024)(128)(4,1)S(1)} %get-tuple-element.25, pred[1024]{0:T(1024)(128)(4,1)S(1)} %get-tuple-element.26, bf16[1024,128]{1,0:T(8,128)(2,1)S(1)} %reshape.69, s32[1024]{0:T(1024)S(1)} %multiply_add_fusion), kind=kOutput, calls=%fused_computation.44 | convolution fusion | flops 269877248 | bytes 792576 | tf_op jit(solution)/shard_map/dot_general | solution.py:366
  46.0 0.8 %fusion.10 = f32[1024,256]{1,0:T(8,128)S(1)} fusion(s32[1024]{0:T(1024)S(1)} %add_select_fusion, bf16[1024,128]{1,0:T(8,128)(2,1)S(1)} %get-tuple-element.24, bf16[1024,128]{1,0:T(8,128)(2,1)S(1)} %get-tuple-element.23), kind=kOutput, calls=%fused_computation.13 | convolution fusion | flops 539230208 | bytes 1576960 | tf_op jit(solution)/shard_map/dot_general | solution.py:368
  46.9 1.1 %copy-done = f32[3,16,64,256]{3,2,1,0:T(8,128)S(1)} copy-done((f32[3,16,64,256]{3,2,1,0:T(8,128)S(1)}, f32[3,16,64,256]{3,2,1,0:T(8,128)}, u32[]{:S(2)}) %copy-start) | copy-done | bytes 3145752
  47.9 0.3 add_dynamic-update-slice_fusion
  48.2 1.7 %copy.18 = f32[3,16,64,256]{3,2,1,0:T(8,128)} copy(f32[3,16,64,256]{3,2,1,0:T(8,128)S(1)} %add_dynamic-update-slice_fusion) | data formatting | bytes 6291456
  49.9 0.6 %copy.19 = f32[1,1024]{1,0:T(1,128)} copy(f32[1,1024]{1,0:T(1,128)S(1)} %copy-done.3) | data formatting | bytes 8192
  (7 shorter events, 0.0 us)
Async XLA Ops:
  8.3 1.3 %copy-start.1 = (f32[32,384]{1,0:T(8,128)S(1)}, f32[32,384]{1,0:T(8,128)}, u32[]{:S(2)}) copy-start(f32[32,384]{1,0:T(8,128)} %param.13) | copy-start | bytes 147460
  8.3 1.3 %copy-start.2 = (s32[1024]{0:T(1024)S(1)}, s32[1024]{0:T(1024)}, u32[]{:S(2)}) copy-start(s32[1024]{0:T(1024)} %param.21) | copy-start | bytes 12292
  46.0 1.9 %copy-start = (f32[3,16,64,256]{3,2,1,0:T(8,128)S(1)}, f32[3,16,64,256]{3,2,1,0:T(8,128)}, u32[]{:S(2)}) copy-start(f32[3,16,64,256]{3,2,1,0:T(8,128)} %get-tuple-element.17) | copy-start | bytes 9437188
  48.2 1.7 %copy-start.3 = (f32[1,1024]{1,0:T(1,128)S(1)}, f32[1,1024]{1,0:T(1,128)}, u32[]{:S(2)}) copy-start(f32[1,1024]{1,0:T(1,128)} %get-tuple-element.30) | copy-start | bytes 12292

commit v10 on v9

--- a/solution.py
+++ b/solution.py
@@ -77,7 +77,30 @@
     return me - pos * stride + ((pos + shift) % n) * stride
 
 
-def step_kernel(rounds, per_ref, st_ref, vel_ref, w_in_ref, decay_ref, w_out_hbm, src_ref, own_ref, adv_ref,
+def pool_samples(vel_ref, parts_ref, sub_ref, pos_ref, half_ref, slot_ref):
+    _, planes, ny, nz = vel_ref.shape
+    entries = sub_ref.shape[0]
+    cells_xy = planes * ny
+    sub_hot = (sub_ref[...] == lax.broadcasted_iota(jnp.int32, (entries, parts_ref.shape[1]), 1)).astype(jnp.bfloat16)
+    gains = [jnp.dot(sub_hot, parts_ref[k], preferred_element_type=jnp.float32) for k in range(3)]
+    gains = (gains[0] + gains[1]) + gains[2]
+    pick_hot = (pos_ref[...] == lax.broadcasted_iota(jnp.int32, (entries, cells_xy), 1)).astype(jnp.bfloat16)
+    slot_hot = (slot_ref[...] == lax.broadcasted_iota(jnp.int32, (R, entries), 0)).astype(jnp.float32)
+    half = half_ref[...]
+    pooled = []
+    for c in range(3):
+        cells = vel_ref[c].reshape(cells_xy, nz).astype(jnp.bfloat16)
+        both = jnp.dot(pick_hot, cells, preferred_element_type=jnp.float32)
+        picked = both[:, :TILE]
+        for h in range(1, nz // TILE):
+            picked = jnp.where(half == h, both[:, h * TILE:(h + 1) * TILE], picked)
+        weighted = gains[:, c * TILE:(c + 1) * TILE] * picked
+        pooled.append(jnp.dot(slot_hot, weighted, precision=lax.Precision.HIGHEST, preferred_element_type=jnp.float32))
+    return pooled
+
+
+def step_kernel(rounds, parts_ref, sub_ref, pos_ref, half_ref, slot_ref, st_ref, vel_ref, w_in_ref, decay_ref,
+                w_out_hbm, src_ref, own_ref, adv_ref,
                 states_ref, pooled_ref, held, sends, recvs, st_sends, st_recvs, xlo, xhi, ylo, yhi, face_sends,
                 face_recvs, w_out_ref, new_ref, w_sem):
     here = (lax.axis_index("slab"), lax.axis_index("cross"))
@@ -97,6 +120,12 @@
             pl.semaphore_signal(barrier, inc=1, device_id=device(axis, partner(here[axis], stride, n, j)), device_id_type=MESH)
             count += 1
     pl.semaphore_signal(barrier, inc=1, device_id=((extra + slab) % slab, c), device_id_type=MESH)
+    w_copy = pltpu.make_async_copy(w_out_hbm, w_out_ref, w_sem)
+    w_copy.start()
+    pooled = pool_samples(vel_ref, parts_ref, sub_ref, pos_ref, half_ref, slot_ref)
+    for k in range(3):
+        pooled_ref[:, k * TILE:(k + 1) * TILE] = pooled[k]
+    states_ref[pl.ds(s, 1)] = st_ref[...][None]
     pl.semaphore_wait(barrier, count + 1)
 
     faces = [
@@ -122,10 +151,7 @@
 
         face_copies.append((send_if, recv_if, copy))
 
-    w_copy = pltpu.make_async_copy(w_out_hbm, w_out_ref, w_sem)
-    w_copy.start()
-    states_ref[pl.ds(s, 1)] = st_ref[...][None]
-    pooled_ref[...] = per_ref[...]
+
     chunks = [None, (0, 6), (6, 11), (11, planes)]
     for r, (axis, stride, n) in enumerate(rounds):
         copies = []
@@ -196,7 +222,7 @@
         new_ref[...].astype(jnp.bfloat16), w_out_ref[...], preferred_element_type=jnp.float32
     ).astype(jnp.bfloat16)
 
-def reduce_step(per_rotor, rotor_states, velocity, w_in, decay, w_out):
+def reduce_step(index_parts, rotor_states, velocity, w_in, decay, w_out):
     slab, cross = lax.axis_size("slab"), lax.axis_size("cross")
     rounds = ring_rounds(slab, cross)
     vmem = pl.BlockSpec(memory_space=pltpu.VMEM)
@@ -208,12 +234,12 @@
             jax.ShapeDtypeStruct(rotor_states.shape, jnp.float32),
             jax.ShapeDtypeStruct(velocity.shape, jnp.float32),
         ),
-        in_specs=[vmem] * 5 + [pl.BlockSpec(memory_space=pl.ANY)],
+        in_specs=[vmem] * 9 + [pl.BlockSpec(memory_space=pl.ANY)],
         out_specs=(vmem, vmem, vmem),
         scratch_shapes=[
             pltpu.VMEM((slab,) + rotor_states.shape, jnp.float32),
-            pltpu.VMEM(per_rotor.shape, jnp.float32),
-            pltpu.VMEM((len(rounds), 3) + per_rotor.shape, jnp.float32),
+            pltpu.VMEM((R, 3 * TILE), jnp.float32),
+            pltpu.VMEM((len(rounds), 3, R, 3 * TILE), jnp.float32),
             pltpu.SemaphoreType.DMA((len(rounds), 3)),
             pltpu.SemaphoreType.DMA((len(rounds), 3)),
             pltpu.SemaphoreType.DMA((len(rounds), 3)),
@@ -229,7 +255,7 @@
             pltpu.SemaphoreType.DMA(()),
         ],
         compiler_params=pltpu.CompilerParams(collective_id=0, has_side_effects=True),
-    )(per_rotor, rotor_states, velocity, w_in, decay.reshape(1, -1), w_out)
+    )(*index_parts, rotor_states, velocity, w_in, decay.reshape(1, -1), w_out)
 
 def stencil_plane(x, planes, vel_ref, xlo_ref, xhi_ref, ylo_ref, yhi_ref):
     _, _, ny, nz = vel_ref.shape
@@ -334,37 +360,21 @@
     tile_count = local_x * local_y * local_z // TILE
     rotor_hot = (entry_rotor == jnp.arange(R, dtype=jnp.int32)[None, :]).astype(jnp.int32)
     slots = jnp.sum(rotor_hot * slot_of_rotor[None, :], axis=1)
-    sub_range = jnp.arange(NSUB, dtype=jnp.int32)
-    sub_hot = (entry_sub[:, None] == sub_range[None, :]).astype(jnp.bfloat16)
     high = lax.reduce_precision(shape_weight, exponent_bits=8, mantissa_bits=7)
     rest = shape_weight - high
     middle = lax.reduce_precision(rest, exponent_bits=8, mantissa_bits=7)
     low = rest - middle
-    gains = [
-        jnp.dot(sub_hot, part.astype(jnp.bfloat16), preferred_element_type=jnp.float32)
-        for part in (high, middle, low)
-    ]
-    gains = (gains[0] + gains[1]) + gains[2]
-    slot_hot = (slots[:, None] == jnp.arange(R, dtype=jnp.int32)[None, :]).astype(jnp.float32)
+    parts = jnp.stack([high, middle, low]).astype(jnp.bfloat16)
     cells_xy = local_x * local_y
     halves = local_z // TILE
     half = (entry_tile % halves)[:, None]
-    place_hot = (jnp.arange(cells_xy, dtype=jnp.int32)[:, None] == (entry_tile // halves)[None, :]).astype(jnp.bfloat16)
-    per_rotor = []
-    for c in range(3):
-        cells = velocity[c].reshape(cells_xy, local_z).astype(jnp.bfloat16)
-        both = jnp.dot(place_hot.T, cells, preferred_element_type=jnp.float32)
-        picked = both[:, :TILE]
-        for h in range(1, halves):
-            picked = jnp.where(half == h, both[:, h * TILE:(h + 1) * TILE], picked)
-        weighted = gains[:, c * TILE:(c + 1) * TILE] * picked
-        per_rotor.append(jnp.dot(slot_hot.T, weighted, precision=lax.Precision.HIGHEST))
-    per_rotor = jnp.concatenate(per_rotor, axis=1)
-    all_sources, new_states, advanced = reduce_step(per_rotor, rotor_states, velocity, w_in, decay, w_out)
+    index_parts = (parts, entry_sub[:, None], (entry_tile // halves)[:, None], half, slots[None, :])
+    all_sources, new_states, advanced = reduce_step(index_parts, rotor_states, velocity, w_in, decay, w_out)
     flat = all_sources.reshape(R * NSUB, TILE)
     row_hot = ((slots * NSUB + entry_sub)[:, None] == jnp.arange(R * NSUB, dtype=jnp.int32)[None, :]).astype(jnp.bfloat16)
     rows = jnp.dot(row_hot, flat, preferred_element_type=jnp.float32).astype(jnp.bfloat16)
     wide = jnp.concatenate([jnp.where(half == h, rows, jnp.zeros_like(rows)) for h in range(halves)], axis=1)
+    place_hot = (jnp.arange(cells_xy, dtype=jnp.int32)[:, None] == (entry_tile // halves)[None, :]).astype(jnp.bfloat16)
     forcing = jnp.dot(place_hot, wide, preferred_element_type=jnp.float32).reshape(local_x, local_y, local_z)
     advanced = advanced.at[0].add(-force_scale * forcing)
     return (advanced, new_states)

time: 51.4 us -> 48.1 us (0.936)
  matrix products: 9.99 us -> 1.88 us
  Pallas kernels: 29.3 us -> 32.9 us
  local copies, waits for them, and re-layouts: 4.52 us -> 7.09 us
  other arithmetic: 5.9 us -> 4.6 us
    dot_general x9 -> x0, matrix products: 7.7 us -> none  [the longest x3 3.82 us: on_device(): both = jnp.dot(place_hot.T, cells, preferred_element_type=jnp.float32)]
    broadcast_in_dim x0 -> x3, local copies, waits for them, and re-layouts: none -> 3.74 us  [the longest x1 1.71 us: on_device(): entry_sub[:, None]]
    pallas_call x1, Pallas kernels: 29.3 us -> 32.9 us  [reduce_step(): pl.pallas_call(lambda *refs: step_kernel(rounds, *refs), out_shape=(jax.S...]
    unnamed x10 -> x8, local copies, waits for them, and re-layouts: 3.34 us -> 2.27 us
    another operation x1 -> x2, other arithmetic: 2.1 us -> 1.46 us  [on_device(): parts = jnp.stack([high, middle, low]).astype(jnp.bfloat16)]
    concatenate x1 -> x0, other arithmetic: 0.64 us -> none  [on_device(): per_rotor = jnp.concatenate(per_rotor, axis=1)]
where the time goes in v10:
time: 48.1 us; the launch traced here: 47.2 us
  Pallas kernels  32.9 us (68%)
  local copies, waits for them, and re-layouts  7.09 us (15%)
  other arithmetic  4.6 us (10%)
  matrix products  1.88 us (4%)
  between operations  0.7 us (1%)
    pallas_call x1, Pallas kernels, reduce_step(): pl.pallas_call(lambda *refs: step_kernel(rounds, *refs), out_shape=(jax.S...  32.9 us
    unnamed x8, local copies, waits for them, and re-layouts  2.27 us
    broadcast_in_dim x1, local copies, waits for them, and re-layouts, on_device(): entry_sub[:, None]  1.71 us
    another operation x2, other arithmetic, on_device(): parts = jnp.stack([high, middle, low]).astype(jnp.bfloat16)  1.46 us
    reshape x1, local copies, waits for them, and re-layouts, on_device(): flat = all_sources.reshape(R * NSUB, TILE)  1.07 us
    dot_general x1, matrix products, on_device(): jnp.dot(row_hot, flat, preferred_element_type=jnp.float32)  1.03 us
    broadcast_in_dim x1, local copies, waits for them, and re-layouts, on_device(): half = (entry_tile % halves)[:, None]  1.02 us
    broadcast_in_dim x1, local copies, waits for them, and re-layouts, on_device(): (entry_tile // halves)[:, None]  1.02 us

profile of v10, /device:TPU:1, one launch (start us, length us, event | category | flops | bytes accessed | tf_op | source)
XLA Modules:
  0.0 47.2 jit_solution(5693890560023047769)
XLA Ops:
  0.6 0.8 %select_reduce_fusion = s32[1024]{0:T(1024)S(1)} fusion(s32[32]{0:T(128)} %param.18, s32[1024]{0:T(1024)} %bitcast.20), kind=kLoop, calls=%fused_computation.14 | loop fusion | flops 97280 | bytes 8320 | tf_op jit(solution)/shard_map/reduce_sum | solution.py:362
  1.4 0.0 copy-start.1
  1.4 0.7 %add_select_fusion.1 = s32[1024]{0:T(1024)S(1)} fusion(s32[1024]{0:T(1024)} %param.20), kind=kLoop, calls=%fused_computation.26 | loop fusion | flops 15360 | bytes 8192 | tf_op jit(solution)/shard_map/jit(floor_divide)/jit(_where)/select_n | solution.py:371
  2.1 0.7 %multiply_add_fusion = s32[1024]{0:T(1024)S(1)} fusion(s32[1024]{0:T(1024)} %param.21, s32[1024]{0:T(1024)S(1)} %select_reduce_fusion), kind=kLoop, calls=%fused_computation.30 | loop fusion | flops 2048 | bytes 12288 | tf_op jit(solution)/shard_map/add | solution.py:374
  2.8 0.7 %broadcast_compare_fusion = (pred[1024]{0:T(1024)(128)(4,1)S(1)}, s32[1024]{0:T(1024)S(1)}) fusion(s32[1024]{0:T(1024)} %param.20), kind=kLoop, calls=%fused_computation.34 | loop fusion | flops 12288 | bytes 9216 | tf_op jit(solution)/shard_map/eq | solution.py:376
  3.5 0.8 %fusion.11 = (bf16[1,32,384]{2,1,0:T(8,128)(2,1)S(1)}, bf16[1,32,384]{2,1,0:T(8,128)(2,1)S(1)}, bf16[1,32,384]{2,1,0:T(8,128)(2,1)S(1)}) fusion(f32[32,384]{1,0:T(8,128)} %param.13), kind=kLoop, calls=%fused_computation.23 | loop fusion | flops 86016 | bytes 122880 | tf_op jit(solution)/shard_map/stack | solution.py:367
  4.3 0.6 %pad_maximum_fusion.refs_0_ = bf16[3,32,384]{2,1,0:T(8,128)(2,1)} fusion(bf16[1,32,384]{2,1,0:T(8,128)(2,1)S(1)} %get-tuple-element.25, bf16[1,32,384]{2,1,0:T(8,128)(2,1)S(1)} %get-tuple-element.26, bf16[1,32,384]{2,1,0:T(8,128)(2,1)S(1)} %get-tuple-element.24), kind=kLoop, calls=%fused_computation.16 | loop fusion | flops 73728 | bytes 147456 | tf_op jit(solution)/shard_map/stack | solution.py:367
  5.0 1.0 %copy.17.refs_3_ = s32[1024,1]{1,0:T(8,128)} copy(s32[1024,1]{0,1:T(1,128)S(1)} %bitcast.16) | data formatting | bytes 8192 | tf_op jit(solution)/shard_map/broadcast_in_dim | solution.py:370
  6.0 1.0 %copy.16.refs_2_ = s32[1024,1]{1,0:T(8,128)} copy(s32[1024,1]{0,1:T(1,128)S(1)} %bitcast.18) | data formatting | bytes 8192 | tf_op jit(solution)/shard_map/broadcast_in_dim | solution.py:371
  7.0 1.7 %copy.15.refs_1_ = s32[1024,1]{1,0:T(8,128)} copy(s32[1024,1]{0,1:T(1,128)} %bitcast.17) | data formatting | bytes 8192 | tf_op jit(solution)/shard_map/broadcast_in_dim | solution.py:371
  8.7 0.0 copy-done.1
  8.7 32.9 %shard_map.113 = (bf16[32,4096]{1,0:T(8,128)(2,1)}, f32[1,1024]{1,0:T(1,128)}, f32[3,16,64,256]{3,2,1,0:T(8,128)}) custom-call(bf16[3,32,384]{2,1,0:T(8,128)(2,1)} %pad_maximum_fusion.refs_0_, s32[1024,1]{1,0:T(8,128)} %copy.15.refs_1_, s32[1024,1]{1,0:T(8,128)} %copy.16.refs_2_, s32[1024,1]{1,0:T(8,128)} %copy.17.refs_3_, s32[1,1024]{1,0:T(1,128)} %bitcast.15, ...), custom_call_target="tpu_custom_call" | custom-call | tf_op jit(solution)/shard_map/pallas_call | solution.py:230
  41.6 1.1 %reshape.64 = bf16[1024,128]{1,0:T(8,128)(2,1)S(1)} reshape(bf16[32,4096]{1,0:T(8,128)(2,1)} %get-tuple-element.18) | data formatting | bytes 524288 | tf_op jit(solution)/shard_map/reshape | solution.py:373
  42.7 0.0 copy-start
  42.7 1.0 %broadcast_select_fusion.1 = (bf16[1024,128]{0,1:T(8,128)(2,1)S(1)}, bf16[1024,128]{0,1:T(8,128)(2,1)S(1)}) fusion(pred[1024]{0:T(1024)(128)(4,1)S(1)} %get-tuple-element.20, pred[1024]{0:T(1024)(128)(4,1)S(1)} %broadcast_compare_fusion.1, bf16[1024,128]{1,0:T(8,128)(2,1)S(1)} %reshape.64, s32[1024]{0:T(1024)S(1)} %multiply_add_fusion), kind=kOutput, calls=%fused_computation.13 | convolution fusion | flops 269877248 | bytes 792576 | tf_op jit(solution)/shard_map/dot_general | solution.py:375
  43.8 0.9 %fusion.4 = f32[1024,256]{1,0:T(8,128)S(1)} fusion(s32[1024]{0:T(1024)S(1)} %add_select_fusion.1, bf16[1024,128]{0,1:T(8,128)(2,1)S(1)} %get-tuple-element.23, bf16[1024,128]{0,1:T(8,128)(2,1)S(1)} %get-tuple-element.22), kind=kOutput, calls=%fused_computation.6 | convolution fusion | flops 539230208 | bytes 1576960 | tf_op jit(solution)/shard_map/dot_general | solution.py:378
  44.6 0.0 copy-done
  44.6 0.3 add_dynamic-update-slice_fusion
  44.9 0.0 copy-start.2
  44.9 1.7 %copy.21 = f32[3,16,64,256]{3,2,1,0:T(8,128)} copy(f32[3,16,64,256]{3,2,1,0:T(8,128)S(1)} %add_dynamic-update-slice_fusion) | data formatting | bytes 6291456
  46.6 0.0 copy-done.2
  46.6 0.6 %copy.22 = f32[1,1024]{1,0:T(1,128)} copy(f32[1,1024]{1,0:T(1,128)S(1)} %copy-done.2) | data formatting | bytes 8192
  (1 shorter events, 0.0 us)
Async XLA Ops:
  1.4 7.3 %copy-start.1 = (s32[1024]{0:T(1024)}, s32[1024]{0:T(1024)S(1)}, u32[]{:S(2)}) copy-start(s32[1024]{0:T(1024)S(1)} %select_reduce_fusion) | copy-start | bytes 12292
  42.7 1.9 %copy-start = (f32[3,16,64,256]{3,2,1,0:T(8,128)S(1)}, f32[3,16,64,256]{3,2,1,0:T(8,128)}, u32[]{:S(2)}) copy-start(f32[3,16,64,256]{3,2,1,0:T(8,128)} %get-tuple-element.17) | copy-start | bytes 9437188
  44.9 1.7 %copy-start.2 = (f32[1,1024]{1,0:T(1,128)S(1)}, f32[1,1024]{1,0:T(1,128)}, u32[]{:S(2)}) copy-start(f32[1,1024]{1,0:T(1,128)} %get-tuple-element.30) | copy-start | bytes 12292

commit v11 on v10

--- a/solution.py
+++ b/solution.py
@@ -77,16 +77,25 @@
     return me - pos * stride + ((pos + shift) % n) * stride
 
 
-def pool_samples(vel_ref, parts_ref, sub_ref, pos_ref, half_ref, slot_ref):
+def unpack(code_ref):
+    code = code_ref[...]
+    half = code % 2
+    slot = (code // 2) % R
+    sub = (code // (2 * R)) % NSUB
+    pos = code // (2 * R * NSUB)
+    return pos, sub, slot, half
+
+
+def pool_samples(vel_ref, parts_ref, code_ref):
     _, planes, ny, nz = vel_ref.shape
-    entries = sub_ref.shape[0]
+    entries = code_ref.shape[0]
     cells_xy = planes * ny
-    sub_hot = (sub_ref[...] == lax.broadcasted_iota(jnp.int32, (entries, parts_ref.shape[1]), 1)).astype(jnp.bfloat16)
+    pos, sub, slot, half = unpack(code_ref)
+    sub_hot = (sub == lax.broadcasted_iota(jnp.int32, (entries, parts_ref.shape[1]), 1)).astype(jnp.bfloat16)
     gains = [jnp.dot(sub_hot, parts_ref[k], preferred_element_type=jnp.float32) for k in range(3)]
     gains = (gains[0] + gains[1]) + gains[2]
-    pick_hot = (pos_ref[...] == lax.broadcasted_iota(jnp.int32, (entries, cells_xy), 1)).astype(jnp.bfloat16)
-    slot_hot = (slot_ref[...] == lax.broadcasted_iota(jnp.int32, (R, entries), 0)).astype(jnp.float32)
-    half = half_ref[...]
+    pick_hot = (pos == lax.broadcasted_iota(jnp.int32, (entries, cells_xy), 1)).astype(jnp.bfloat16)
+    slot_hot = (slot == lax.broadcasted_iota(jnp.int32, (entries, R), 1)).astype(jnp.float32)
     pooled = []
     for c in range(3):
         cells = vel_ref[c].reshape(cells_xy, nz).astype(jnp.bfloat16)
@@ -95,14 +104,34 @@
         for h in range(1, nz // TILE):
             picked = jnp.where(half == h, both[:, h * TILE:(h + 1) * TILE], picked)
         weighted = gains[:, c * TILE:(c + 1) * TILE] * picked
-        pooled.append(jnp.dot(slot_hot, weighted, precision=lax.Precision.HIGHEST, preferred_element_type=jnp.float32))
+        pooled.append(
+            lax.dot_general(
+                slot_hot, weighted, (((0,), (0,)), ((), ())),
+                precision=lax.Precision.HIGHEST, preferred_element_type=jnp.float32,
+            )
+        )
     return pooled
 
 
-def step_kernel(rounds, parts_ref, sub_ref, pos_ref, half_ref, slot_ref, st_ref, vel_ref, w_in_ref, decay_ref,
-                w_out_hbm, src_ref, own_ref, adv_ref,
+def place_forcing(src, code_ref, flat_ref, adv_ref):
+    _, planes, ny, nz = adv_ref.shape
+    entries = code_ref.shape[0]
+    pos, sub, slot, half = unpack(code_ref)
+    for j in range(NSUB):
+        flat_ref[j * R:(j + 1) * R, :] = src[:, j * TILE:(j + 1) * TILE]
+    row_hot = ((sub * R + slot) == lax.broadcasted_iota(jnp.int32, (entries, NSUB * R), 1)).astype(jnp.bfloat16)
+    rows = jnp.dot(row_hot, flat_ref[...], preferred_element_type=jnp.float32)
+    wide = jnp.concatenate(
+        [jnp.where(half == h, rows, 0.0) for h in range(nz // TILE)], axis=1
+    ).astype(jnp.bfloat16)
+    pick_hot = (pos == lax.broadcasted_iota(jnp.int32, (entries, planes * ny), 1)).astype(jnp.bfloat16)
+    forcing = lax.dot_general(pick_hot, wide, (((0,), (0,)), ((), ())), preferred_element_type=jnp.float32)
+    adv_ref[0] = adv_ref[0] - force_scale * forcing.reshape(planes, ny, nz)
+
+def step_kernel(rounds, parts_ref, code_ref, st_ref, vel_ref, w_in_ref, decay_ref,
+                w_out_hbm, own_ref, adv_ref,
                 states_ref, pooled_ref, held, sends, recvs, st_sends, st_recvs, xlo, xhi, ylo, yhi, face_sends,
-                face_recvs, w_out_ref, new_ref, w_sem):
+                face_recvs, w_out_ref, new_ref, w_sem, flat_ref):
     here = (lax.axis_index("slab"), lax.axis_index("cross"))
     slab, cross = lax.axis_size("slab"), lax.axis_size("cross")
     planes = vel_ref.shape[1]
@@ -122,7 +151,7 @@
     pl.semaphore_signal(barrier, inc=1, device_id=((extra + slab) % slab, c), device_id_type=MESH)
     w_copy = pltpu.make_async_copy(w_out_hbm, w_out_ref, w_sem)
     w_copy.start()
-    pooled = pool_samples(vel_ref, parts_ref, sub_ref, pos_ref, half_ref, slot_ref)
+    pooled = pool_samples(vel_ref, parts_ref, code_ref)
     for k in range(3):
         pooled_ref[:, k * TILE:(k + 1) * TILE] = pooled[k]
     states_ref[pl.ds(s, 1)] = st_ref[...][None]
@@ -218,9 +247,10 @@
     own = st_ref[...]
     own_ref[...] = own + state_step * (own_drive - decay * own)
     w_copy.wait()
-    src_ref[...] = jnp.dot(
+    src = jnp.dot(
         new_ref[...].astype(jnp.bfloat16), w_out_ref[...], preferred_element_type=jnp.float32
     ).astype(jnp.bfloat16)
+    place_forcing(src, code_ref, flat_ref, adv_ref)
 
 def reduce_step(index_parts, rotor_states, velocity, w_in, decay, w_out):
     slab, cross = lax.axis_size("slab"), lax.axis_size("cross")
@@ -230,12 +260,11 @@
     return pl.pallas_call(
         lambda *refs: step_kernel(rounds, *refs),
         out_shape=(
-            jax.ShapeDtypeStruct((slab, w_out.shape[1]), jnp.bfloat16),
             jax.ShapeDtypeStruct(rotor_states.shape, jnp.float32),
             jax.ShapeDtypeStruct(velocity.shape, jnp.float32),
         ),
-        in_specs=[vmem] * 9 + [pl.BlockSpec(memory_space=pl.ANY)],
-        out_specs=(vmem, vmem, vmem),
+        in_specs=[vmem] * 6 + [pl.BlockSpec(memory_space=pl.ANY)],
+        out_specs=(vmem, vmem),
         scratch_shapes=[
             pltpu.VMEM((slab,) + rotor_states.shape, jnp.float32),
             pltpu.VMEM((R, 3 * TILE), jnp.float32),
@@ -253,6 +282,7 @@
             pltpu.VMEM(w_out.shape, w_out.dtype),
             pltpu.VMEM((slab, w_out.shape[0]), jnp.float32),
             pltpu.SemaphoreType.DMA(()),
+            pltpu.VMEM((NSUB * R, TILE), jnp.bfloat16),
         ],
         compiler_params=pltpu.CompilerParams(collective_id=0, has_side_effects=True),
     )(*index_parts, rotor_states, velocity, w_in, decay.reshape(1, -1), w_out)
@@ -365,18 +395,9 @@
     middle = lax.reduce_precision(rest, exponent_bits=8, mantissa_bits=7)
     low = rest - middle
     parts = jnp.stack([high, middle, low]).astype(jnp.bfloat16)
-    cells_xy = local_x * local_y
     halves = local_z // TILE
-    half = (entry_tile % halves)[:, None]
-    index_parts = (parts, entry_sub[:, None], (entry_tile // halves)[:, None], half, slots[None, :])
-    all_sources, new_states, advanced = reduce_step(index_parts, rotor_states, velocity, w_in, decay, w_out)
-    flat = all_sources.reshape(R * NSUB, TILE)
-    row_hot = ((slots * NSUB + entry_sub)[:, None] == jnp.arange(R * NSUB, dtype=jnp.int32)[None, :]).astype(jnp.bfloat16)
-    rows = jnp.dot(row_hot, flat, preferred_element_type=jnp.float32).astype(jnp.bfloat16)
-    wide = jnp.concatenate([jnp.where(half == h, rows, jnp.zeros_like(rows)) for h in range(halves)], axis=1)
-    place_hot = (jnp.arange(cells_xy, dtype=jnp.int32)[:, None] == (entry_tile // halves)[None, :]).astype(jnp.bfloat16)
-    forcing = jnp.dot(place_hot, wide, preferred_element_type=jnp.float32).reshape(local_x, local_y, local_z)
-    advanced = advanced.at[0].add(-force_scale * forcing)
+    code = (((entry_tile // halves) * NSUB + entry_sub) * R + slots) * halves + entry_tile % halves
+    new_states, advanced = reduce_step((parts, code[:, None]), rotor_states, velocity, w_in, decay, w_out)
     return (advanced, new_states)
 
 

time: 48.1 us -> 46.8 us (0.973)
  Pallas kernels: 32.9 us -> 36.9 us
  matrix products: 1.88 us -> 0 us
  other arithmetic: 4.6 us -> 2.97 us
  local copies, waits for them, and re-layouts: 7.09 us -> 5.53 us
    pallas_call x1, Pallas kernels: 32.9 us -> 36.9 us  [reduce_step(): pl.pallas_call(lambda *refs: step_kernel(rounds, *refs), out_shape=(jax.S...]
    broadcast_in_dim x3 -> x1, local copies, waits for them, and re-layouts: 3.74 us -> 1.02 us  [on_device(): code[:, None]]
    unnamed x8 -> x4, local copies, waits for them, and re-layouts: 2.27 us -> 4.5 us
    dot_general x2 -> x0, matrix products: 1.88 us -> none  [the longest x1 1.03 us: on_device(): jnp.dot(row_hot, flat, preferred_element_type=jnp.float32)]
    reshape x1 -> x0, local copies, waits for them, and re-layouts: 1.07 us -> none  [on_device(): flat = all_sources.reshape(R * NSUB, TILE)]
    eq x2 -> x0, other arithmetic: 0.7 us -> none  [on_device(): half == h]
    select_n x1 -> x0, other arithmetic: 0.7 us -> none  [on_device(): entry_tile // halves]
where the time goes in v11:
time: 46.8 us; the launch traced here: 46 us
  Pallas kernels  36.9 us (79%)
  local copies, waits for them, and re-layouts  5.53 us (12%)
  other arithmetic  2.97 us (6%)
  between operations  0.65 us (1%)
    pallas_call x1, Pallas kernels, reduce_step(): pl.pallas_call(lambda *refs: step_kernel(rounds, *refs), out_shape=(jax.S...  36.9 us
    unnamed x4, local copies, waits for them, and re-layouts  4.5 us
    another operation x2, other arithmetic, on_device(): parts = jnp.stack([high, middle, low]).astype(jnp.bfloat16)  1.45 us
    broadcast_in_dim x1, local copies, waits for them, and re-layouts, on_device(): code[:, None]  1.02 us

profile of v11, /device:TPU:1, one launch (start us, length us, event | category | flops | bytes accessed | tf_op | source)
XLA Modules:
  0.0 46.0 jit_solution(15338792293687757742)
XLA Ops:
  0.6 0.8 %select_reduce_fusion = s32[1024]{0:T(1024)S(1)} fusion(s32[32]{0:T(128)} %param.16, s32[1024]{0:T(1024)} %bitcast.11), kind=kLoop, calls=%fused_computation | loop fusion | flops 97280 | bytes 8320 | tf_op jit(solution)/shard_map/reduce_sum | solution.py:392
  1.4 0.7 %fusion.9 = s32[1024]{0:T(1024)S(1)} fusion(s32[1024]{0:T(1024)S(1)} %select_reduce_fusion, s32[1024]{0:T(1024)} %param.19, s32[1024]{0:T(1024)} %param.18), kind=kLoop, calls=%fused_computation.21 | loop fusion | flops 25600 | bytes 16384 | tf_op jit(solution)/shard_map/add | solution.py:399
  2.1 0.8 %fusion.2 = (bf16[1,32,384]{2,1,0:T(8,128)(2,1)S(1)}, bf16[1,32,384]{2,1,0:T(8,128)(2,1)S(1)}, bf16[1,32,384]{2,1,0:T(8,128)(2,1)S(1)}) fusion(f32[32,384]{1,0:T(8,128)} %param.11), kind=kLoop, calls=%fused_computation.9 | loop fusion | flops 86016 | bytes 122880 | tf_op jit(solution)/shard_map/stack | solution.py:397
  3.0 0.6 %pad_maximum_fusion.refs_0_ = bf16[3,32,384]{2,1,0:T(8,128)(2,1)} fusion(bf16[1,32,384]{2,1,0:T(8,128)(2,1)S(1)} %get-tuple-element.7, bf16[1,32,384]{2,1,0:T(8,128)(2,1)S(1)} %get-tuple-element.8, bf16[1,32,384]{2,1,0:T(8,128)(2,1)S(1)} %get-tuple-element.6), kind=kLoop, calls=%fused_computation.2 | loop fusion | flops 73728 | bytes 147456 | tf_op jit(solution)/shard_map/stack | solution.py:397
  3.6 1.0 %copy.13.refs_1_ = s32[1024,1]{1,0:T(8,128)} copy(s32[1024,1]{0,1:T(1,128)S(1)} %bitcast.9) | data formatting | bytes 8192 | tf_op jit(solution)/shard_map/broadcast_in_dim | solution.py:400
  4.6 36.9 %shard_map.113 = (f32[1,1024]{1,0:T(1,128)}, f32[3,16,64,256]{3,2,1,0:T(8,128)}) custom-call(bf16[3,32,384]{2,1,0:T(8,128)(2,1)} %pad_maximum_fusion.refs_0_, s32[1024,1]{1,0:T(8,128)} %copy.13.refs_1_, f32[1,1024]{1,0:T(1,128)} %refs_2_.1, f32[3,16,64,256]{3,2,1,0:T(8,128)} %refs_3_.1, bf16[384,1024]{1,0:T(8,128)(2,1)} %refs_4_.1, f32[1,1024]{1,0:T(1,128)} %bitcast.10, ...), custom_call_target="tpu_custom_call" | custom-call | tf_op jit(solution)/shard_map/pallas_call | solution.py:260
  41.5 0.0 copy-start
  41.5 3.9 %copy.16 = f32[3,16,64,256]{3,2,1,0:T(8,128)} copy(f32[3,16,64,256]{3,2,1,0:T(8,128)} %get-tuple-element.11) | data formatting | bytes 6291456
  45.5 0.0 copy-done
  45.5 0.6 %copy.17 = f32[1,1024]{1,0:T(1,128)} copy(f32[1,1024]{1,0:T(1,128)S(1)} %copy-done) | data formatting | bytes 8192
Async XLA Ops:
  41.5 3.9 %copy-start = (f32[1,1024]{1,0:T(1,128)S(1)}, f32[1,1024]{1,0:T(1,128)}, u32[]{:S(2)}) copy-start(f32[1,1024]{1,0:T(1,128)} %get-tuple-element.12) | copy-start | bytes 12292

commit v12 on v11

--- a/solution.py
+++ b/solution.py
@@ -131,7 +131,7 @@
 def step_kernel(rounds, parts_ref, code_ref, st_ref, vel_ref, w_in_ref, decay_ref,
                 w_out_hbm, own_ref, adv_ref,
                 states_ref, pooled_ref, held, sends, recvs, st_sends, st_recvs, xlo, xhi, ylo, yhi, face_sends,
-                face_recvs, w_out_ref, new_ref, w_sem, flat_ref):
+                face_recvs, w_out_ref, new_ref, w_sem, flat_ref, swap_sems, swap_ref):
     here = (lax.axis_index("slab"), lax.axis_index("cross"))
     slab, cross = lax.axis_size("slab"), lax.axis_size("cross")
     planes = vel_ref.shape[1]
@@ -182,13 +182,15 @@
 
 
     chunks = [None, (0, 6), (6, 11), (11, planes)]
+    share = R // 2
+    mine = pl.ds(pl.multiple_of((s % 2) * share, share), share)
     for r, (axis, stride, n) in enumerate(rounds):
         copies = []
         for j in range(1, n):
             dev = device(axis, partner(here[axis], stride, n, j))
             copy = pltpu.make_async_remote_copy(
-                src_ref=pooled_ref,
-                dst_ref=held.at[r, j - 1],
+                src_ref=pooled_ref if r == 0 else pooled_ref.at[mine],
+                dst_ref=held.at[r, j - 1] if r == 0 else held.at[r, j - 1, pl.ds(0, share)],
                 send_sem=sends.at[r, j - 1],
                 recv_sem=recvs.at[r, j - 1],
                 device_id=dev,
@@ -230,11 +232,24 @@
             lax.fori_loop(first, last, body, 0)
         for copy in copies:
             copy.wait()
-        if n == 2:
-            total = pooled_ref[...] + held[r, 0]
+        if r == 0:
+            pooled_ref[mine, :] = pooled_ref[mine, :] + held[r, 0, mine, :]
+        elif n == 2:
+            pooled_ref[mine, :] = pooled_ref[mine, :] + held[r, 0, pl.ds(0, share)]
         else:
-            total = (pooled_ref[...] + held[r, 1]) + (held[r, 0] + held[r, 2])
-        pooled_ref[...] = total
+            got = [held[r, k, pl.ds(0, share)] for k in range(3)]
+            pooled_ref[mine, :] = (pooled_ref[mine, :] + got[1]) + (got[0] + got[2])
+    swap = pltpu.make_async_remote_copy(
+        src_ref=pooled_ref.at[mine],
+        dst_ref=swap_ref,
+        send_sem=swap_sems.at[0],
+        recv_sem=swap_sems.at[1],
+        device_id=(s + 1 - 2 * (s % 2), c),
+        device_id_type=MESH,
+    )
+    swap.start()
+    swap.wait()
+    pooled_ref[pl.ds(pl.multiple_of((1 - s % 2) * share, share), share), :] = swap_ref[...]
 
     pooled_b = (pooled_ref[...] * pool_scale).astype(jnp.bfloat16)
     drive = jnp.dot(pooled_b, w_in_ref[...], preferred_element_type=jnp.float32)
@@ -283,6 +298,8 @@
             pltpu.VMEM((slab, w_out.shape[0]), jnp.float32),
             pltpu.SemaphoreType.DMA(()),
             pltpu.VMEM((NSUB * R, TILE), jnp.bfloat16),
+            pltpu.SemaphoreType.DMA((2,)),
+            pltpu.VMEM((R // 2, 3 * TILE), jnp.float32),
         ],
         compiler_params=pltpu.CompilerParams(collective_id=0, has_side_effects=True),
     )(*index_parts, rotor_states, velocity, w_in, decay.reshape(1, -1), w_out)

time: 46.8 us -> 46.5 us (level); the launches traced: 46 us -> 46.3 us
  no operation moved by 1% of the time
where the time goes in v12:
time: 46.5 us; the launch traced here: 46.3 us
  Pallas kernels  37.1 us (80%)
  local copies, waits for them, and re-layouts  5.53 us (12%)
  other arithmetic  2.97 us (6%)
  between operations  0.65 us (1%)
    pallas_call x1, Pallas kernels, reduce_step(): pl.pallas_call(lambda *refs: step_kernel(rounds, *refs), out_shape=(jax.S...  37.1 us
    unnamed x4, local copies, waits for them, and re-layouts  4.5 us
    another operation x2, other arithmetic, on_device(): parts = jnp.stack([high, middle, low]).astype(jnp.bfloat16)  1.45 us
    broadcast_in_dim x1, local copies, waits for them, and re-layouts, on_device(): code[:, None]  1.02 us

profile of v12, /device:TPU:1, one launch (start us, length us, event | category | flops | bytes accessed | tf_op | source)
XLA Modules:
  0.0 46.3 jit_solution(16848876350436254715)
XLA Ops:
  0.6 0.8 %select_reduce_fusion = s32[1024]{0:T(1024)S(1)} fusion(s32[32]{0:T(128)} %param.16, s32[1024]{0:T(1024)} %bitcast.11), kind=kLoop, calls=%fused_computation | loop fusion | flops 97280 | bytes 8320 | tf_op jit(solution)/shard_map/reduce_sum | solution.py:409
  1.4 0.7 %fusion.9 = s32[1024]{0:T(1024)S(1)} fusion(s32[1024]{0:T(1024)S(1)} %select_reduce_fusion, s32[1024]{0:T(1024)} %param.19, s32[1024]{0:T(1024)} %param.18), kind=kLoop, calls=%fused_computation.21 | loop fusion | flops 25600 | bytes 16384 | tf_op jit(solution)/shard_map/add | solution.py:416
  2.1 0.8 %fusion.2 = (bf16[1,32,384]{2,1,0:T(8,128)(2,1)S(1)}, bf16[1,32,384]{2,1,0:T(8,128)(2,1)S(1)}, bf16[1,32,384]{2,1,0:T(8,128)(2,1)S(1)}) fusion(f32[32,384]{1,0:T(8,128)} %param.11), kind=kLoop, calls=%fused_computation.9 | loop fusion | flops 86016 | bytes 122880 | tf_op jit(solution)/shard_map/stack | solution.py:414
  3.0 0.6 %pad_maximum_fusion.refs_0_ = bf16[3,32,384]{2,1,0:T(8,128)(2,1)} fusion(bf16[1,32,384]{2,1,0:T(8,128)(2,1)S(1)} %get-tuple-element.7, bf16[1,32,384]{2,1,0:T(8,128)(2,1)S(1)} %get-tuple-element.8, bf16[1,32,384]{2,1,0:T(8,128)(2,1)S(1)} %get-tuple-element.6), kind=kLoop, calls=%fused_computation.2 | loop fusion | flops 73728 | bytes 147456 | tf_op jit(solution)/shard_map/stack | solution.py:414
  3.6 1.0 %copy.13.refs_1_ = s32[1024,1]{1,0:T(8,128)} copy(s32[1024,1]{0,1:T(1,128)S(1)} %bitcast.9) | data formatting | bytes 8192 | tf_op jit(solution)/shard_map/broadcast_in_dim | solution.py:417
  4.6 37.1 %shard_map.113 = (f32[1,1024]{1,0:T(1,128)}, f32[3,16,64,256]{3,2,1,0:T(8,128)}) custom-call(bf16[3,32,384]{2,1,0:T(8,128)(2,1)} %pad_maximum_fusion.refs_0_, s32[1024,1]{1,0:T(8,128)} %copy.13.refs_1_, f32[1,1024]{1,0:T(1,128)} %refs_2_.1, f32[3,16,64,256]{3,2,1,0:T(8,128)} %refs_3_.1, bf16[384,1024]{1,0:T(8,128)(2,1)} %refs_4_.1, f32[1,1024]{1,0:T(1,128)} %bitcast.10, ...), custom_call_target="tpu_custom_call" | custom-call | tf_op jit(solution)/shard_map/pallas_call | solution.py:275
  41.8 0.0 copy-start
  41.8 3.9 %copy.16 = f32[3,16,64,256]{3,2,1,0:T(8,128)} copy(f32[3,16,64,256]{3,2,1,0:T(8,128)} %get-tuple-element.11) | data formatting | bytes 6291456
  45.7 0.0 copy-done
  45.7 0.6 %copy.17 = f32[1,1024]{1,0:T(1,128)} copy(f32[1,1024]{1,0:T(1,128)S(1)} %copy-done) | data formatting | bytes 8192
Async XLA Ops:
  41.8 3.9 %copy-start = (f32[1,1024]{1,0:T(1,128)S(1)}, f32[1,1024]{1,0:T(1,128)}, u32[]{:S(2)}) copy-start(f32[1,1024]{1,0:T(1,128)} %get-tuple-element.12) | copy-start | bytes 12292

commit v13 on v12

--- a/solution.py
+++ b/solution.py
@@ -130,7 +130,7 @@
 
 def step_kernel(rounds, parts_ref, code_ref, st_ref, vel_ref, w_in_ref, decay_ref,
                 w_out_hbm, own_ref, adv_ref,
-                states_ref, pooled_ref, held, sends, recvs, st_sends, st_recvs, xlo, xhi, ylo, yhi, face_sends,
+                states_ref, p0, p1, p2, p3, p4, held, sends, recvs, st_sends, st_recvs, xlo, xhi, ylo, yhi, face_sends,
                 face_recvs, w_out_ref, new_ref, w_sem, flat_ref, swap_sems, swap_ref):
     here = (lax.axis_index("slab"), lax.axis_index("cross"))
     slab, cross = lax.axis_size("slab"), lax.axis_size("cross")
@@ -153,7 +153,7 @@
     w_copy.start()
     pooled = pool_samples(vel_ref, parts_ref, code_ref)
     for k in range(3):
-        pooled_ref[:, k * TILE:(k + 1) * TILE] = pooled[k]
+        p0[:, k * TILE:(k + 1) * TILE] = pooled[k]
     states_ref[pl.ds(s, 1)] = st_ref[...][None]
     pl.semaphore_wait(barrier, count + 1)
 
@@ -184,12 +184,15 @@
     chunks = [None, (0, 6), (6, 11), (11, planes)]
     share = R // 2
     mine = pl.ds(pl.multiple_of((s % 2) * share, share), share)
+    final = len(rounds)
+    bufs = [p0, p1, p2, p3, p4]
+    sent = []
     for r, (axis, stride, n) in enumerate(rounds):
         copies = []
         for j in range(1, n):
             dev = device(axis, partner(here[axis], stride, n, j))
             copy = pltpu.make_async_remote_copy(
-                src_ref=pooled_ref if r == 0 else pooled_ref.at[mine],
+                src_ref=bufs[0] if r == 0 else bufs[r].at[mine],
                 dst_ref=held.at[r, j - 1] if r == 0 else held.at[r, j - 1, pl.ds(0, share)],
                 send_sem=sends.at[r, j - 1],
                 recv_sem=recvs.at[r, j - 1],
@@ -213,9 +216,6 @@
         if r == 1:
             for send_if, recv_if, face in face_copies:
 
-                @pl.when(send_if)
-                def _():
-                    face.wait_send()
 
                 @pl.when(recv_if)
                 def _():
@@ -231,16 +231,17 @@
 
             lax.fori_loop(first, last, body, 0)
         for copy in copies:
-            copy.wait()
+            copy.wait_recv()
+        sent += copies
         if r == 0:
-            pooled_ref[mine, :] = pooled_ref[mine, :] + held[r, 0, mine, :]
+            bufs[r + 1][mine, :] = bufs[r][mine, :] + held[r, 0, mine, :]
         elif n == 2:
-            pooled_ref[mine, :] = pooled_ref[mine, :] + held[r, 0, pl.ds(0, share)]
+            bufs[r + 1][mine, :] = bufs[r][mine, :] + held[r, 0, pl.ds(0, share)]
         else:
             got = [held[r, k, pl.ds(0, share)] for k in range(3)]
-            pooled_ref[mine, :] = (pooled_ref[mine, :] + got[1]) + (got[0] + got[2])
+            bufs[r + 1][mine, :] = (bufs[r][mine, :] + got[1]) + (got[0] + got[2])
     swap = pltpu.make_async_remote_copy(
-        src_ref=pooled_ref.at[mine],
+        src_ref=bufs[final].at[mine],
         dst_ref=swap_ref,
         send_sem=swap_sems.at[0],
         recv_sem=swap_sems.at[1],
@@ -249,9 +250,9 @@
     )
     swap.start()
     swap.wait()
-    pooled_ref[pl.ds(pl.multiple_of((1 - s % 2) * share, share), share), :] = swap_ref[...]
-
-    pooled_b = (pooled_ref[...] * pool_scale).astype(jnp.bfloat16)
+    bufs[final][pl.ds(pl.multiple_of((1 - s % 2) * share, share), share), :] = swap_ref[...]
+
+    pooled_b = (bufs[final][...] * pool_scale).astype(jnp.bfloat16)
     drive = jnp.dot(pooled_b, w_in_ref[...], preferred_element_type=jnp.float32)
     decay = decay_ref[...]
     for k in range(states_ref.shape[0]):
@@ -266,6 +267,13 @@
         new_ref[...].astype(jnp.bfloat16), w_out_ref[...], preferred_element_type=jnp.float32
     ).astype(jnp.bfloat16)
     place_forcing(src, code_ref, flat_ref, adv_ref)
+    for copy in sent:
+        copy.wait_send()
+    for send_if, recv_if, face in face_copies:
+
+        @pl.when(send_if)
+        def _():
+            face.wait_send()
 
 def reduce_step(index_parts, rotor_states, velocity, w_in, decay, w_out):
     slab, cross = lax.axis_size("slab"), lax.axis_size("cross")
@@ -282,7 +290,7 @@
         out_specs=(vmem, vmem),
         scratch_shapes=[
             pltpu.VMEM((slab,) + rotor_states.shape, jnp.float32),
-            pltpu.VMEM((R, 3 * TILE), jnp.float32),
+            *[pltpu.VMEM((R, 3 * TILE), jnp.float32) for _ in range(len(rounds) + 1)],
             pltpu.VMEM((len(rounds), 3, R, 3 * TILE), jnp.float32),
             pltpu.SemaphoreType.DMA((len(rounds), 3)),
             pltpu.SemaphoreType.DMA((len(rounds), 3)),

time: 46.5 us -> 46.5 us (level)
  no operation moved by 1% of the time
where the time goes in v13:
time: 46.5 us; the launch traced here: 46.3 us
  Pallas kernels  37.1 us (80%)
  local copies, waits for them, and re-layouts  5.53 us (12%)
  other arithmetic  2.97 us (6%)
  between operations  0.65 us (1%)
    pallas_call x1, Pallas kernels, reduce_step(): pl.pallas_call(lambda *refs: step_kernel(rounds, *refs), out_shape=(jax.S...  37.1 us
    unnamed x4, local copies, waits for them, and re-layouts  4.5 us
    another operation x2, other arithmetic, on_device(): parts = jnp.stack([high, middle, low]).astype(jnp.bfloat16)  1.45 us
    broadcast_in_dim x1, local copies, waits for them, and re-layouts, on_device(): code[:, None]  1.02 us

profile of v13, /device:TPU:1, one launch (start us, length us, event | category | flops | bytes accessed | tf_op | source)
XLA Modules:
  0.0 46.3 jit_solution(17726581245019180513)
XLA Ops:
  0.6 0.8 %select_reduce_fusion = s32[1024]{0:T(1024)S(1)} fusion(s32[32]{0:T(128)} %param.16, s32[1024]{0:T(1024)} %bitcast.11), kind=kLoop, calls=%fused_computation | loop fusion | flops 97280 | bytes 8320 | tf_op jit(solution)/shard_map/reduce_sum | solution.py:417
  1.4 0.7 %fusion.9 = s32[1024]{0:T(1024)S(1)} fusion(s32[1024]{0:T(1024)S(1)} %select_reduce_fusion, s32[1024]{0:T(1024)} %param.19, s32[1024]{0:T(1024)} %param.18), kind=kLoop, calls=%fused_computation.21 | loop fusion | flops 25600 | bytes 16384 | tf_op jit(solution)/shard_map/add | solution.py:424
  2.1 0.8 %fusion.2 = (bf16[1,32,384]{2,1,0:T(8,128)(2,1)S(1)}, bf16[1,32,384]{2,1,0:T(8,128)(2,1)S(1)}, bf16[1,32,384]{2,1,0:T(8,128)(2,1)S(1)}) fusion(f32[32,384]{1,0:T(8,128)} %param.11), kind=kLoop, calls=%fused_computation.9 | loop fusion | flops 86016 | bytes 122880 | tf_op jit(solution)/shard_map/stack | solution.py:422
  3.0 0.6 %pad_maximum_fusion.refs_0_ = bf16[3,32,384]{2,1,0:T(8,128)(2,1)} fusion(bf16[1,32,384]{2,1,0:T(8,128)(2,1)S(1)} %get-tuple-element.7, bf16[1,32,384]{2,1,0:T(8,128)(2,1)S(1)} %get-tuple-element.8, bf16[1,32,384]{2,1,0:T(8,128)(2,1)S(1)} %get-tuple-element.6), kind=kLoop, calls=%fused_computation.2 | loop fusion | flops 73728 | bytes 147456 | tf_op jit(solution)/shard_map/stack | solution.py:422
  3.6 1.0 %copy.13.refs_1_ = s32[1024,1]{1,0:T(8,128)} copy(s32[1024,1]{0,1:T(1,128)S(1)} %bitcast.9) | data formatting | bytes 8192 | tf_op jit(solution)/shard_map/broadcast_in_dim | solution.py:425
  4.6 37.1 %shard_map.113 = (f32[1,1024]{1,0:T(1,128)}, f32[3,16,64,256]{3,2,1,0:T(8,128)}) custom-call(bf16[3,32,384]{2,1,0:T(8,128)(2,1)} %pad_maximum_fusion.refs_0_, s32[1024,1]{1,0:T(8,128)} %copy.13.refs_1_, f32[1,1024]{1,0:T(1,128)} %refs_2_.1, f32[3,16,64,256]{3,2,1,0:T(8,128)} %refs_3_.1, bf16[384,1024]{1,0:T(8,128)(2,1)} %refs_4_.1, f32[1,1024]{1,0:T(1,128)} %bitcast.10, ...), custom_call_target="tpu_custom_call" | custom-call | tf_op jit(solution)/shard_map/pallas_call | solution.py:283
  41.8 0.0 copy-start
  41.8 3.9 %copy.16 = f32[3,16,64,256]{3,2,1,0:T(8,128)} copy(f32[3,16,64,256]{3,2,1,0:T(8,128)} %get-tuple-element.11) | data formatting | bytes 6291456
  45.7 0.0 copy-done
  45.7 0.6 %copy.17 = f32[1,1024]{1,0:T(1,128)} copy(f32[1,1024]{1,0:T(1,128)S(1)} %copy-done) | data formatting | bytes 8192
Async XLA Ops:
  41.8 3.9 %copy-start = (f32[1,1024]{1,0:T(1,128)S(1)}, f32[1,1024]{1,0:T(1,128)}, u32[]{:S(2)}) copy-start(f32[1,1024]{1,0:T(1,128)} %get-tuple-element.12) | copy-start | bytes 12292

commit v14 on v13

--- a/solution.py
+++ b/solution.py
@@ -129,9 +129,9 @@
     adv_ref[0] = adv_ref[0] - force_scale * forcing.reshape(planes, ny, nz)
 
 def step_kernel(rounds, parts_ref, code_ref, st_ref, vel_ref, w_in_ref, decay_ref,
-                w_out_hbm, own_ref, adv_ref,
+                w_out_hbm, own_ref, adv_hbm,
                 states_ref, p0, p1, p2, p3, p4, held, sends, recvs, st_sends, st_recvs, xlo, xhi, ylo, yhi, face_sends,
-                face_recvs, w_out_ref, new_ref, w_sem, flat_ref, swap_sems, swap_ref):
+                face_recvs, w_out_ref, new_ref, w_sem, flat_ref, swap_sems, swap_ref, adv_ref, adv_sems):
     here = (lax.axis_index("slab"), lax.axis_index("cross"))
     slab, cross = lax.axis_size("slab"), lax.axis_size("cross")
     planes = vel_ref.shape[1]
@@ -186,6 +186,7 @@
     mine = pl.ds(pl.multiple_of((s % 2) * share, share), share)
     final = len(rounds)
     bufs = [p0, p1, p2, p3, p4]
+    outs = []
     sent = []
     for r, (axis, stride, n) in enumerate(rounds):
         copies = []
@@ -230,6 +231,13 @@
                 return carry
 
             lax.fori_loop(first, last, body, 0)
+            out = pltpu.make_async_copy(
+                adv_ref.at[pl.ds(1, 2), pl.ds(first, last - first)],
+                adv_hbm.at[pl.ds(1, 2), pl.ds(first, last - first)],
+                adv_sems.at[r - 1],
+            )
+            out.start()
+            outs.append(out)
         for copy in copies:
             copy.wait_recv()
         sent += copies
@@ -267,6 +275,11 @@
         new_ref[...].astype(jnp.bfloat16), w_out_ref[...], preferred_element_type=jnp.float32
     ).astype(jnp.bfloat16)
     place_forcing(src, code_ref, flat_ref, adv_ref)
+    out = pltpu.make_async_copy(adv_ref.at[0], adv_hbm.at[0], adv_sems.at[len(rounds) - 1])
+    out.start()
+    outs.append(out)
+    for out in outs:
+        out.wait()
     for copy in sent:
         copy.wait_send()
     for send_if, recv_if, face in face_copies:
@@ -287,7 +300,7 @@
             jax.ShapeDtypeStruct(velocity.shape, jnp.float32),
         ),
         in_specs=[vmem] * 6 + [pl.BlockSpec(memory_space=pl.ANY)],
-        out_specs=(vmem, vmem),
+        out_specs=(vmem, pl.BlockSpec(memory_space=pl.ANY)),
         scratch_shapes=[
             pltpu.VMEM((slab,) + rotor_states.shape, jnp.float32),
             *[pltpu.VMEM((R, 3 * TILE), jnp.float32) for _ in range(len(rounds) + 1)],
@@ -308,6 +321,8 @@
             pltpu.VMEM((NSUB * R, TILE), jnp.bfloat16),
             pltpu.SemaphoreType.DMA((2,)),
             pltpu.VMEM((R // 2, 3 * TILE), jnp.float32),
+            pltpu.VMEM(velocity.shape, jnp.float32),
+            pltpu.SemaphoreType.DMA((len(rounds),)),
         ],
         compiler_params=pltpu.CompilerParams(collective_id=0, has_side_effects=True),
     )(*index_parts, rotor_states, velocity, w_in, decay.reshape(1, -1), w_out)

time: 46.5 us -> 46.5 us (level)
  no operation moved by 1% of the time
where the time goes in v14:
time: 46.5 us; the launch traced here: 46.2 us
  Pallas kernels  37.1 us (80%)
  local copies, waits for them, and re-layouts  5.53 us (12%)
  other arithmetic  2.97 us (6%)
  between operations  0.65 us (1%)
    pallas_call x1, Pallas kernels, reduce_step(): pl.pallas_call(lambda *refs: step_kernel(rounds, *refs), out_shape=(jax.S...  37.1 us
    unnamed x4, local copies, waits for them, and re-layouts  4.5 us
    another operation x2, other arithmetic, on_device(): parts = jnp.stack([high, middle, low]).astype(jnp.bfloat16)  1.45 us
    broadcast_in_dim x1, local copies, waits for them, and re-layouts, on_device(): code[:, None]  1.02 us

profile of v14, /device:TPU:1, one launch (start us, length us, event | category | flops | bytes accessed | tf_op | source)
XLA Modules:
  0.0 46.2 jit_solution(17807492355353718667)
XLA Ops:
  0.6 0.8 %select_reduce_fusion = s32[1024]{0:T(1024)S(1)} fusion(s32[32]{0:T(128)} %param.16, s32[1024]{0:T(1024)} %bitcast.11), kind=kLoop, calls=%fused_computation | loop fusion | flops 97280 | bytes 8320 | tf_op jit(solution)/shard_map/reduce_sum | solution.py:432
  1.4 0.7 %fusion.9 = s32[1024]{0:T(1024)S(1)} fusion(s32[1024]{0:T(1024)S(1)} %select_reduce_fusion, s32[1024]{0:T(1024)} %param.19, s32[1024]{0:T(1024)} %param.18), kind=kLoop, calls=%fused_computation.21 | loop fusion | flops 25600 | bytes 16384 | tf_op jit(solution)/shard_map/add | solution.py:439
  2.1 0.8 %fusion.2 = (bf16[1,32,384]{2,1,0:T(8,128)(2,1)S(1)}, bf16[1,32,384]{2,1,0:T(8,128)(2,1)S(1)}, bf16[1,32,384]{2,1,0:T(8,128)(2,1)S(1)}) fusion(f32[32,384]{1,0:T(8,128)} %param.11), kind=kLoop, calls=%fused_computation.9 | loop fusion | flops 86016 | bytes 122880 | tf_op jit(solution)/shard_map/stack | solution.py:437
  3.0 0.6 %pad_maximum_fusion.refs_0_ = bf16[3,32,384]{2,1,0:T(8,128)(2,1)} fusion(bf16[1,32,384]{2,1,0:T(8,128)(2,1)S(1)} %get-tuple-element.7, bf16[1,32,384]{2,1,0:T(8,128)(2,1)S(1)} %get-tuple-element.8, bf16[1,32,384]{2,1,0:T(8,128)(2,1)S(1)} %get-tuple-element.6), kind=kLoop, calls=%fused_computation.2 | loop fusion | flops 73728 | bytes 147456 | tf_op jit(solution)/shard_map/stack | solution.py:437
  3.6 1.0 %copy.13.refs_1_ = s32[1024,1]{1,0:T(8,128)} copy(s32[1024,1]{0,1:T(1,128)S(1)} %bitcast.9) | data formatting | bytes 8192 | tf_op jit(solution)/shard_map/broadcast_in_dim | solution.py:440
  4.6 37.1 %shard_map.113 = (f32[1,1024]{1,0:T(1,128)}, f32[3,16,64,256]{3,2,1,0:T(8,128)}) custom-call(bf16[3,32,384]{2,1,0:T(8,128)(2,1)} %pad_maximum_fusion.refs_0_, s32[1024,1]{1,0:T(8,128)} %copy.13.refs_1_, f32[1,1024]{1,0:T(1,128)} %refs_2_.1, f32[3,16,64,256]{3,2,1,0:T(8,128)} %refs_3_.1, bf16[384,1024]{1,0:T(8,128)(2,1)} %refs_4_.1, f32[1,1024]{1,0:T(1,128)} %bitcast.10, ...), custom_call_target="tpu_custom_call" | custom-call | tf_op jit(solution)/shard_map/pallas_call | solution.py:296
  41.7 0.0 copy-start
  41.7 3.9 %copy.16 = f32[3,16,64,256]{3,2,1,0:T(8,128)} copy(f32[3,16,64,256]{3,2,1,0:T(8,128)} %get-tuple-element.11) | data formatting | bytes 6291456
  45.6 0.0 copy-done
  45.6 0.6 %copy.17 = f32[1,1024]{1,0:T(1,128)} copy(f32[1,1024]{1,0:T(1,128)S(1)} %copy-done) | data formatting | bytes 8192
Async XLA Ops:
  41.7 3.9 %copy-start = (f32[1,1024]{1,0:T(1,128)S(1)}, f32[1,1024]{1,0:T(1,128)}, u32[]{:S(2)}) copy-start(f32[1,1024]{1,0:T(1,128)} %get-tuple-element.12) | copy-start | bytes 12292

commit v15 on v14

--- a/solution.py
+++ b/solution.py
@@ -113,25 +113,23 @@
     return pooled
 
 
-def place_forcing(src, code_ref, flat_ref, adv_ref):
+def place_forcing(src, code_ref, flat_ref, adv_ref, row_hot_ref, pick_ref):
     _, planes, ny, nz = adv_ref.shape
-    entries = code_ref.shape[0]
     pos, sub, slot, half = unpack(code_ref)
     for j in range(NSUB):
         flat_ref[j * R:(j + 1) * R, :] = src[:, j * TILE:(j + 1) * TILE]
-    row_hot = ((sub * R + slot) == lax.broadcasted_iota(jnp.int32, (entries, NSUB * R), 1)).astype(jnp.bfloat16)
-    rows = jnp.dot(row_hot, flat_ref[...], preferred_element_type=jnp.float32)
+    rows = jnp.dot(row_hot_ref[...], flat_ref[...], preferred_element_type=jnp.float32)
     wide = jnp.concatenate(
         [jnp.where(half == h, rows, 0.0) for h in range(nz // TILE)], axis=1
     ).astype(jnp.bfloat16)
-    pick_hot = (pos == lax.broadcasted_iota(jnp.int32, (entries, planes * ny), 1)).astype(jnp.bfloat16)
+    pick_hot = pick_ref[...]
     forcing = lax.dot_general(pick_hot, wide, (((0,), (0,)), ((), ())), preferred_element_type=jnp.float32)
     adv_ref[0] = adv_ref[0] - force_scale * forcing.reshape(planes, ny, nz)
 
 def step_kernel(rounds, parts_ref, code_ref, st_ref, vel_ref, w_in_ref, decay_ref,
                 w_out_hbm, own_ref, adv_hbm,
                 states_ref, p0, p1, p2, p3, p4, held, sends, recvs, st_sends, st_recvs, xlo, xhi, ylo, yhi, face_sends,
-                face_recvs, w_out_ref, new_ref, w_sem, flat_ref, swap_sems, swap_ref, adv_ref, adv_sems):
+                face_recvs, w_out_ref, new_ref, w_sem, flat_ref, swap_sems, swap_ref, adv_ref, adv_sems, row_hot_ref, pick_ref):
     here = (lax.axis_index("slab"), lax.axis_index("cross"))
     slab, cross = lax.axis_size("slab"), lax.axis_size("cross")
     planes = vel_ref.shape[1]
@@ -238,6 +236,13 @@
             )
             out.start()
             outs.append(out)
+            if r == len(rounds) - 1:
+                pos, sub, slot, half = unpack(code_ref)
+                entries = code_ref.shape[0]
+                row_hot_ref[...] = (
+                    (sub * R + slot) == lax.broadcasted_iota(jnp.int32, (entries, NSUB * R), 1)
+                ).astype(jnp.bfloat16)
+                pick_ref[...] = (pos == lax.broadcasted_iota(jnp.int32, (entries, planes * ny), 1)).astype(jnp.bfloat16)
         for copy in copies:
             copy.wait_recv()
         sent += copies
@@ -274,7 +279,7 @@
     src = jnp.dot(
         new_ref[...].astype(jnp.bfloat16), w_out_ref[...], preferred_element_type=jnp.float32
     ).astype(jnp.bfloat16)
-    place_forcing(src, code_ref, flat_ref, adv_ref)
+    place_forcing(src, code_ref, flat_ref, adv_ref, row_hot_ref, pick_ref)
     out = pltpu.make_async_copy(adv_ref.at[0], adv_hbm.at[0], adv_sems.at[len(rounds) - 1])
     out.start()
     outs.append(out)
@@ -288,7 +293,7 @@
         def _():
             face.wait_send()
 
-def reduce_step(index_parts, rotor_states, velocity, w_in, decay, w_out):
+def reduce_step(code_parts, rotor_states, velocity, w_in, decay, w_out):
     slab, cross = lax.axis_size("slab"), lax.axis_size("cross")
     rounds = ring_rounds(slab, cross)
     vmem = pl.BlockSpec(memory_space=pltpu.VMEM)
@@ -323,9 +328,11 @@
             pltpu.VMEM((R // 2, 3 * TILE), jnp.float32),
             pltpu.VMEM(velocity.shape, jnp.float32),
             pltpu.SemaphoreType.DMA((len(rounds),)),
+            pltpu.VMEM((code_parts[1].shape[0], NSUB * R), jnp.bfloat16),
+            pltpu.VMEM((code_parts[1].shape[0], planes * ny), jnp.bfloat16),
         ],
         compiler_params=pltpu.CompilerParams(collective_id=0, has_side_effects=True),
-    )(*index_parts, rotor_states, velocity, w_in, decay.reshape(1, -1), w_out)
+    )(*code_parts, rotor_states, velocity, w_in, decay.reshape(1, -1), w_out)
 
 def stencil_plane(x, planes, vel_ref, xlo_ref, xhi_ref, ylo_ref, yhi_ref):
     _, _, ny, nz = vel_ref.shape

time: 46.5 us -> 45.7 us (0.983)
  Pallas kernels: 37.1 us -> 36.3 us
    pallas_call x1, Pallas kernels: 37.1 us -> 36.3 us  [reduce_step(): pl.pallas_call(lambda *refs: step_kernel(rounds, *refs), out_shape=(jax.S...]
where the time goes in v15:
time: 45.7 us; the launch traced here: 45.4 us
  Pallas kernels  36.3 us (79%)
  local copies, waits for them, and re-layouts  5.53 us (12%)
  other arithmetic  2.97 us (6%)
  between operations  0.65 us (1%)
    pallas_call x1, Pallas kernels, reduce_step(): pl.pallas_call(lambda *refs: step_kernel(rounds, *refs), out_shape=(jax.S...  36.3 us
    unnamed x4, local copies, waits for them, and re-layouts  4.5 us
    another operation x2, other arithmetic, on_device(): parts = jnp.stack([high, middle, low]).astype(jnp.bfloat16)  1.45 us
    broadcast_in_dim x1, local copies, waits for them, and re-layouts, on_device(): code[:, None]  1.02 us

profile of v15, /device:TPU:1, one launch (start us, length us, event | category | flops | bytes accessed | tf_op | source)
XLA Modules:
  0.0 45.4 jit_solution(4886982801559139329)
XLA Ops:
  0.6 0.8 %select_reduce_fusion = s32[1024]{0:T(1024)S(1)} fusion(s32[32]{0:T(128)} %param.16, s32[1024]{0:T(1024)} %bitcast.11), kind=kLoop, calls=%fused_computation | loop fusion | flops 97280 | bytes 8320 | tf_op jit(solution)/shard_map/reduce_sum | solution.py:439
  1.4 0.7 %fusion.9 = s32[1024]{0:T(1024)S(1)} fusion(s32[1024]{0:T(1024)S(1)} %select_reduce_fusion, s32[1024]{0:T(1024)} %param.19, s32[1024]{0:T(1024)} %param.18), kind=kLoop, calls=%fused_computation.21 | loop fusion | flops 25600 | bytes 16384 | tf_op jit(solution)/shard_map/add | solution.py:446
  2.1 0.8 %fusion.2 = (bf16[1,32,384]{2,1,0:T(8,128)(2,1)S(1)}, bf16[1,32,384]{2,1,0:T(8,128)(2,1)S(1)}, bf16[1,32,384]{2,1,0:T(8,128)(2,1)S(1)}) fusion(f32[32,384]{1,0:T(8,128)} %param.11), kind=kLoop, calls=%fused_computation.9 | loop fusion | flops 86016 | bytes 122880 | tf_op jit(solution)/shard_map/stack | solution.py:444
  3.0 0.6 %pad_maximum_fusion.refs_0_ = bf16[3,32,384]{2,1,0:T(8,128)(2,1)} fusion(bf16[1,32,384]{2,1,0:T(8,128)(2,1)S(1)} %get-tuple-element.7, bf16[1,32,384]{2,1,0:T(8,128)(2,1)S(1)} %get-tuple-element.8, bf16[1,32,384]{2,1,0:T(8,128)(2,1)S(1)} %get-tuple-element.6), kind=kLoop, calls=%fused_computation.2 | loop fusion | flops 73728 | bytes 147456 | tf_op jit(solution)/shard_map/stack | solution.py:444
  3.6 1.0 %copy.13.refs_1_ = s32[1024,1]{1,0:T(8,128)} copy(s32[1024,1]{0,1:T(1,128)S(1)} %bitcast.9) | data formatting | bytes 8192 | tf_op jit(solution)/shard_map/broadcast_in_dim | solution.py:447
  4.6 36.3 %shard_map.113 = (f32[1,1024]{1,0:T(1,128)}, f32[3,16,64,256]{3,2,1,0:T(8,128)}) custom-call(bf16[3,32,384]{2,1,0:T(8,128)(2,1)} %pad_maximum_fusion.refs_0_, s32[1024,1]{1,0:T(8,128)} %copy.13.refs_1_, f32[1,1024]{1,0:T(1,128)} %refs_2_.1, f32[3,16,64,256]{3,2,1,0:T(8,128)} %refs_3_.1, bf16[384,1024]{1,0:T(8,128)(2,1)} %refs_4_.1, f32[1,1024]{1,0:T(1,128)} %bitcast.10, ...), custom_call_target="tpu_custom_call" | custom-call | tf_op jit(solution)/shard_map/pallas_call | solution.py:301
  40.9 0.0 copy-start
  40.9 3.9 %copy.16 = f32[3,16,64,256]{3,2,1,0:T(8,128)} copy(f32[3,16,64,256]{3,2,1,0:T(8,128)} %get-tuple-element.11) | data formatting | bytes 6291456
  44.8 0.0 copy-done
  44.8 0.6 %copy.17 = f32[1,1024]{1,0:T(1,128)} copy(f32[1,1024]{1,0:T(1,128)S(1)} %copy-done) | data formatting | bytes 8192
Async XLA Ops:
  40.9 3.9 %copy-start = (f32[1,1024]{1,0:T(1,128)S(1)}, f32[1,1024]{1,0:T(1,128)}, u32[]{:S(2)}) copy-start(f32[1,1024]{1,0:T(1,128)} %get-tuple-element.12) | copy-start | bytes 12292

commit v16 on v15

--- a/solution.py
+++ b/solution.py
@@ -86,13 +86,13 @@
     return pos, sub, slot, half
 
 
-def pool_samples(vel_ref, parts_ref, code_ref):
+def pool_samples(vel_ref, parts, code_ref):
     _, planes, ny, nz = vel_ref.shape
     entries = code_ref.shape[0]
     cells_xy = planes * ny
     pos, sub, slot, half = unpack(code_ref)
-    sub_hot = (sub == lax.broadcasted_iota(jnp.int32, (entries, parts_ref.shape[1]), 1)).astype(jnp.bfloat16)
-    gains = [jnp.dot(sub_hot, parts_ref[k], preferred_element_type=jnp.float32) for k in range(3)]
+    sub_hot = (sub == lax.broadcasted_iota(jnp.int32, (entries, parts[0].shape[0]), 1)).astype(jnp.bfloat16)
+    gains = [jnp.dot(sub_hot, part[...], preferred_element_type=jnp.float32) for part in parts]
     gains = (gains[0] + gains[1]) + gains[2]
     pick_hot = (pos == lax.broadcasted_iota(jnp.int32, (entries, cells_xy), 1)).astype(jnp.bfloat16)
     slot_hot = (slot == lax.broadcasted_iota(jnp.int32, (entries, R), 1)).astype(jnp.float32)
@@ -126,7 +126,7 @@
     forcing = lax.dot_general(pick_hot, wide, (((0,), (0,)), ((), ())), preferred_element_type=jnp.float32)
     adv_ref[0] = adv_ref[0] - force_scale * forcing.reshape(planes, ny, nz)
 
-def step_kernel(rounds, parts_ref, code_ref, st_ref, vel_ref, w_in_ref, decay_ref,
+def step_kernel(rounds, high_ref, middle_ref, low_ref, code_ref, st_ref, vel_ref, w_in_ref, decay_ref,
                 w_out_hbm, own_ref, adv_hbm,
                 states_ref, p0, p1, p2, p3, p4, held, sends, recvs, st_sends, st_recvs, xlo, xhi, ylo, yhi, face_sends,
                 face_recvs, w_out_ref, new_ref, w_sem, flat_ref, swap_sems, swap_ref, adv_ref, adv_sems, row_hot_ref, pick_ref):
@@ -149,7 +149,7 @@
     pl.semaphore_signal(barrier, inc=1, device_id=((extra + slab) % slab, c), device_id_type=MESH)
     w_copy = pltpu.make_async_copy(w_out_hbm, w_out_ref, w_sem)
     w_copy.start()
-    pooled = pool_samples(vel_ref, parts_ref, code_ref)
+    pooled = pool_samples(vel_ref, (high_ref, middle_ref, low_ref), code_ref)
     for k in range(3):
         p0[:, k * TILE:(k + 1) * TILE] = pooled[k]
     states_ref[pl.ds(s, 1)] = st_ref[...][None]
@@ -304,7 +304,7 @@
             jax.ShapeDtypeStruct(rotor_states.shape, jnp.float32),
             jax.ShapeDtypeStruct(velocity.shape, jnp.float32),
         ),
-        in_specs=[vmem] * 6 + [pl.BlockSpec(memory_space=pl.ANY)],
+        in_specs=[vmem] * 8 + [pl.BlockSpec(memory_space=pl.ANY)],
         out_specs=(vmem, pl.BlockSpec(memory_space=pl.ANY)),
         scratch_shapes=[
             pltpu.VMEM((slab,) + rotor_states.shape, jnp.float32),
@@ -328,8 +328,8 @@
             pltpu.VMEM((R // 2, 3 * TILE), jnp.float32),
             pltpu.VMEM(velocity.shape, jnp.float32),
             pltpu.SemaphoreType.DMA((len(rounds),)),
-            pltpu.VMEM((code_parts[1].shape[0], NSUB * R), jnp.bfloat16),
-            pltpu.VMEM((code_parts[1].shape[0], planes * ny), jnp.bfloat16),
+            pltpu.VMEM((code_parts[-1].shape[0], NSUB * R), jnp.bfloat16),
+            pltpu.VMEM((code_parts[-1].shape[0], planes * ny), jnp.bfloat16),
         ],
         compiler_params=pltpu.CompilerParams(collective_id=0, has_side_effects=True),
     )(*code_parts, rotor_states, velocity, w_in, decay.reshape(1, -1), w_out)
@@ -441,10 +441,10 @@
     rest = shape_weight - high
     middle = lax.reduce_precision(rest, exponent_bits=8, mantissa_bits=7)
     low = rest - middle
-    parts = jnp.stack([high, middle, low]).astype(jnp.bfloat16)
+    parts = tuple(part.astype(jnp.bfloat16) for part in (high, middle, low))
     halves = local_z // TILE
     code = (((entry_tile // halves) * NSUB + entry_sub) * R + slots) * halves + entry_tile % halves
-    new_states, advanced = reduce_step((parts, code[:, None]), rotor_states, velocity, w_in, decay, w_out)
+    new_states, advanced = reduce_step(parts + (code[:, None],), rotor_states, velocity, w_in, decay, w_out)
     return (advanced, new_states)
 
 

time: 45.7 us -> 45.7 us (level)
    another operation x2 -> x0, other arithmetic: 1.45 us -> none  [on_device(): parts = jnp.stack([high, middle, low]).astype(jnp.bfloat16)]
    convert_element_type x0 -> x1, other arithmetic: none -> 1.43 us  [on_device(): parts = tuple((part.astype(jnp.bfloat16) for part in (high, middle, low)))]
where the time goes in v16:
time: 45.7 us; the launch traced here: 45.4 us
  Pallas kernels  36.3 us (79%)
  local copies, waits for them, and re-layouts  5.53 us (12%)
  other arithmetic  2.95 us (6%)
  between operations  0.65 us (1%)
    pallas_call x1, Pallas kernels, reduce_step(): pl.pallas_call(lambda *refs: step_kernel(rounds, *refs), out_shape=(jax.S...  36.3 us
    unnamed x4, local copies, waits for them, and re-layouts  4.5 us
    convert_element_type x1, other arithmetic, on_device(): parts = tuple((part.astype(jnp.bfloat16) for part in (high, middle, low)))  1.43 us
    broadcast_in_dim x1, local copies, waits for them, and re-layouts, on_device(): code[:, None]  1.02 us

profile of v16, /device:TPU:1, one launch (start us, length us, event | category | flops | bytes accessed | tf_op | source)
XLA Modules:
  0.0 45.4 jit_solution(1859307892578351312)
XLA Ops:
  0.6 0.8 %select_reduce_fusion = s32[1024]{0:T(1024)S(1)} fusion(s32[32]{0:T(128)} %param.16, s32[1024]{0:T(1024)} %bitcast.5), kind=kLoop, calls=%fused_computation | loop fusion | flops 97280 | bytes 8320 | tf_op jit(solution)/shard_map/reduce_sum | solution.py:439
  1.4 0.7 %fusion.6 = s32[1024]{0:T(1024)S(1)} fusion(s32[1024]{0:T(1024)S(1)} %select_reduce_fusion, s32[1024]{0:T(1024)} %param.19, s32[1024]{0:T(1024)} %param.18), kind=kLoop, calls=%fused_computation.17 | loop fusion | flops 25600 | bytes 16384 | tf_op jit(solution)/shard_map/add | solution.py:446
  2.1 1.4 %fusion = (bf16[32,384]{1,0:T(8,128)(2,1)}, bf16[32,384]{1,0:T(8,128)(2,1)}, bf16[32,384]{1,0:T(8,128)(2,1)}) fusion(f32[32,384]{1,0:T(8,128)} %param.11), kind=kLoop, calls=%fused_computation.6 | loop fusion | flops 86016 | bytes 122880 | tf_op jit(solution)/shard_map/convert_element_type | solution.py:444
  3.6 1.0 %copy.13.refs_3_ = s32[1024,1]{1,0:T(8,128)} copy(s32[1024,1]{0,1:T(1,128)S(1)} %bitcast.3) | data formatting | bytes 8192 | tf_op jit(solution)/shard_map/broadcast_in_dim | solution.py:447
  4.6 36.3 %shard_map.113 = (f32[1,1024]{1,0:T(1,128)}, f32[3,16,64,256]{3,2,1,0:T(8,128)}) custom-call(bf16[32,384]{1,0:T(8,128)(2,1)} %get-tuple-element.8.refs_0_, bf16[32,384]{1,0:T(8,128)(2,1)} %get-tuple-element.7.refs_1_, bf16[32,384]{1,0:T(8,128)(2,1)} %get-tuple-element.6.refs_2_, s32[1024,1]{1,0:T(8,128)} %copy.13.refs_3_, f32[1,1024]{1,0:T(1,128)} %refs_4_.1, ...), custom_call_target="tpu_custom_call" | custom-call | tf_op jit(solution)/shard_map/pallas_call | solution.py:301
  40.9 0.0 copy-start
  40.9 3.9 %copy.16 = f32[3,16,64,256]{3,2,1,0:T(8,128)} copy(f32[3,16,64,256]{3,2,1,0:T(8,128)} %get-tuple-element.11) | data formatting | bytes 6291456
  44.8 0.0 copy-done
  44.8 0.6 %copy.17 = f32[1,1024]{1,0:T(1,128)} copy(f32[1,1024]{1,0:T(1,128)S(1)} %copy-done) | data formatting | bytes 8192
Async XLA Ops:
  40.9 3.9 %copy-start = (f32[1,1024]{1,0:T(1,128)S(1)}, f32[1,1024]{1,0:T(1,128)}, u32[]{:S(2)}) copy-start(f32[1,1024]{1,0:T(1,128)} %get-tuple-element.12) | copy-start | bytes 12292

commit v17 on v15

--- a/solution.py
+++ b/solution.py
@@ -86,7 +86,7 @@
     return pos, sub, slot, half
 
 
-def pool_samples(vel_ref, parts_ref, code_ref):
+def pool_samples(vel_ref, parts_ref, code_ref, emit):
     _, planes, ny, nz = vel_ref.shape
     entries = code_ref.shape[0]
     cells_xy = planes * ny
@@ -110,6 +110,7 @@
                 precision=lax.Precision.HIGHEST, preferred_element_type=jnp.float32,
             )
         )
+        emit(c, pooled[-1])
     return pooled
 
 
@@ -149,11 +150,26 @@
     pl.semaphore_signal(barrier, inc=1, device_id=((extra + slab) % slab, c), device_id_type=MESH)
     w_copy = pltpu.make_async_copy(w_out_hbm, w_out_ref, w_sem)
     w_copy.start()
-    pooled = pool_samples(vel_ref, parts_ref, code_ref)
-    for k in range(3):
-        p0[:, k * TILE:(k + 1) * TILE] = pooled[k]
     states_ref[pl.ds(s, 1)] = st_ref[...][None]
-    pl.semaphore_wait(barrier, count + 1)
+    first_round = []
+
+    def emit(k, value):
+        columns = pl.ds(k * TILE, TILE)
+        p0[:, columns] = value
+        if k == 0:
+            pl.semaphore_wait(barrier, count + 1)
+        part = pltpu.make_async_remote_copy(
+            src_ref=p0.at[:, columns],
+            dst_ref=held.at[0, 0, :, columns],
+            send_sem=sends.at[0, k],
+            recv_sem=recvs.at[0, k],
+            device_id=(s + 1 - 2 * (s % 2), c),
+            device_id_type=MESH,
+        )
+        part.start()
+        first_round.append(part)
+
+    pool_samples(vel_ref, parts_ref, code_ref, emit)
 
     faces = [
         (s > 0, s < slab - 1, vel_ref.at[:, 0], xhi, ((s + slab - 1) % slab, c)),
@@ -187,7 +203,7 @@
     outs = []
     sent = []
     for r, (axis, stride, n) in enumerate(rounds):
-        copies = []
+        copies = list(first_round) if r == 0 else []
         for j in range(1, n):
             dev = device(axis, partner(here[axis], stride, n, j))
             copy = pltpu.make_async_remote_copy(
@@ -198,8 +214,9 @@
                 device_id=dev,
                 device_id_type=MESH,
             )
-            copy.start()
-            copies.append(copy)
+            if r > 0:
+                copy.start()
+                copies.append(copy)
             if axis == 0:
                 rows = pl.ds(s - s % stride, stride)
                 block = pltpu.make_async_remote_copy(

time: 45.7 us -> 45.9 us (level)
  no operation moved by 1% of the time
where the time goes in v17:
time: 45.9 us; the launch traced here: 45.7 us
  Pallas kernels  36.5 us (80%)
  local copies, waits for them, and re-layouts  5.53 us (12%)
  other arithmetic  2.97 us (6%)
  between operations  0.65 us (1%)
    pallas_call x1, Pallas kernels, reduce_step(): pl.pallas_call(lambda *refs: step_kernel(rounds, *refs), out_shape=(jax.S...  36.5 us
    unnamed x4, local copies, waits for them, and re-layouts  4.5 us
    another operation x2, other arithmetic, on_device(): parts = jnp.stack([high, middle, low]).astype(jnp.bfloat16)  1.45 us
    broadcast_in_dim x1, local copies, waits for them, and re-layouts, on_device(): code[:, None]  1.02 us

profile of v17, /device:TPU:1, one launch (start us, length us, event | category | flops | bytes accessed | tf_op | source)
XLA Modules:
  0.0 45.7 jit_solution(4522400803465525522)
XLA Ops:
  0.6 0.8 %select_reduce_fusion = s32[1024]{0:T(1024)S(1)} fusion(s32[32]{0:T(128)} %param.16, s32[1024]{0:T(1024)} %bitcast.11), kind=kLoop, calls=%fused_computation | loop fusion | flops 97280 | bytes 8320 | tf_op jit(solution)/shard_map/reduce_sum | solution.py:456
  1.4 0.7 %fusion.9 = s32[1024]{0:T(1024)S(1)} fusion(s32[1024]{0:T(1024)S(1)} %select_reduce_fusion, s32[1024]{0:T(1024)} %param.19, s32[1024]{0:T(1024)} %param.18), kind=kLoop, calls=%fused_computation.21 | loop fusion | flops 25600 | bytes 16384 | tf_op jit(solution)/shard_map/add | solution.py:463
  2.1 0.8 %fusion.2 = (bf16[1,32,384]{2,1,0:T(8,128)(2,1)S(1)}, bf16[1,32,384]{2,1,0:T(8,128)(2,1)S(1)}, bf16[1,32,384]{2,1,0:T(8,128)(2,1)S(1)}) fusion(f32[32,384]{1,0:T(8,128)} %param.11), kind=kLoop, calls=%fused_computation.9 | loop fusion | flops 86016 | bytes 122880 | tf_op jit(solution)/shard_map/stack | solution.py:461
  3.0 0.6 %pad_maximum_fusion.refs_0_ = bf16[3,32,384]{2,1,0:T(8,128)(2,1)} fusion(bf16[1,32,384]{2,1,0:T(8,128)(2,1)S(1)} %get-tuple-element.7, bf16[1,32,384]{2,1,0:T(8,128)(2,1)S(1)} %get-tuple-element.8, bf16[1,32,384]{2,1,0:T(8,128)(2,1)S(1)} %get-tuple-element.6), kind=kLoop, calls=%fused_computation.2 | loop fusion | flops 73728 | bytes 147456 | tf_op jit(solution)/shard_map/stack | solution.py:461
  3.6 1.0 %copy.13.refs_1_ = s32[1024,1]{1,0:T(8,128)} copy(s32[1024,1]{0,1:T(1,128)S(1)} %bitcast.9) | data formatting | bytes 8192 | tf_op jit(solution)/shard_map/broadcast_in_dim | solution.py:464
  4.6 36.5 %shard_map.113 = (f32[1,1024]{1,0:T(1,128)}, f32[3,16,64,256]{3,2,1,0:T(8,128)}) custom-call(bf16[3,32,384]{2,1,0:T(8,128)(2,1)} %pad_maximum_fusion.refs_0_, s32[1024,1]{1,0:T(8,128)} %copy.13.refs_1_, f32[1,1024]{1,0:T(1,128)} %refs_2_.1, f32[3,16,64,256]{3,2,1,0:T(8,128)} %refs_3_.1, bf16[384,1024]{1,0:T(8,128)(2,1)} %refs_4_.1, f32[1,1024]{1,0:T(1,128)} %bitcast.10, ...), custom_call_target="tpu_custom_call" | custom-call | tf_op jit(solution)/shard_map/pallas_call | solution.py:318
  41.1 0.0 copy-start
  41.2 3.9 %copy.16 = f32[3,16,64,256]{3,2,1,0:T(8,128)} copy(f32[3,16,64,256]{3,2,1,0:T(8,128)} %get-tuple-element.11) | data formatting | bytes 6291456
  45.1 0.0 copy-done
  45.1 0.6 %copy.17 = f32[1,1024]{1,0:T(1,128)} copy(f32[1,1024]{1,0:T(1,128)S(1)} %copy-done) | data formatting | bytes 8192
Async XLA Ops:
  41.1 3.9 %copy-start = (f32[1,1024]{1,0:T(1,128)S(1)}, f32[1,1024]{1,0:T(1,128)}, u32[]{:S(2)}) copy-start(f32[1,1024]{1,0:T(1,128)} %get-tuple-element.12) | copy-start | bytes 12292

commit v18 on v15

--- a/solution.py
+++ b/solution.py
@@ -129,7 +129,7 @@
 def step_kernel(rounds, parts_ref, code_ref, st_ref, vel_ref, w_in_ref, decay_ref,
                 w_out_hbm, own_ref, adv_hbm,
                 states_ref, p0, p1, p2, p3, p4, held, sends, recvs, st_sends, st_recvs, xlo, xhi, ylo, yhi, face_sends,
-                face_recvs, w_out_ref, new_ref, w_sem, flat_ref, swap_sems, swap_ref, adv_ref, adv_sems, row_hot_ref, pick_ref):
+                face_recvs, w_out_ref, new_ref, w_sem, flat_ref, swap_sems, swap_ref, adv_ref, adv_sems, row_hot_ref, pick_ref, held2, msends, mrecvs):
     here = (lax.axis_index("slab"), lax.axis_index("cross"))
     slab, cross = lax.axis_size("slab"), lax.axis_size("cross")
     planes = vel_ref.shape[1]
@@ -147,6 +147,10 @@
             pl.semaphore_signal(barrier, inc=1, device_id=device(axis, partner(here[axis], stride, n, j)), device_id_type=MESH)
             count += 1
     pl.semaphore_signal(barrier, inc=1, device_id=((extra + slab) % slab, c), device_id_type=MESH)
+    for dz in range(1, 4):
+        for dy in range(1, cross):
+            pl.semaphore_signal(barrier, inc=1, device_id=(partner(s, 8, 4, dz), partner(c, 1, cross, dy)), device_id_type=MESH)
+            count += 1
     w_copy = pltpu.make_async_copy(w_out_hbm, w_out_ref, w_sem)
     w_copy.start()
     pooled = pool_samples(vel_ref, parts_ref, code_ref)
@@ -179,16 +183,40 @@
         face_copies.append((send_if, recv_if, copy))
 
 
-    chunks = [None, (0, 6), (6, 11), (11, planes)]
+    chunks = [None, (0, 6), (6, planes), None]
     share = R // 2
     mine = pl.ds(pl.multiple_of((s % 2) * share, share), share)
-    final = len(rounds)
+    final = 3
     bufs = [p0, p1, p2, p3, p4]
     outs = []
     sent = []
     for r, (axis, stride, n) in enumerate(rounds):
+        if r == 3:
+            continue
         copies = []
-        for j in range(1, n):
+        if r == 2:
+            for dz in range(4):
+                for dy in range(cross):
+                    if dz == 0 and dy == 0:
+                        continue
+                    m = dz * cross + dy - 1
+                    dev = (partner(s, 8, 4, dz), partner(c, 1, cross, dy))
+                    copy = pltpu.make_async_remote_copy(
+                        src_ref=bufs[r].at[mine], dst_ref=held2.at[m], send_sem=msends.at[m],
+                        recv_sem=mrecvs.at[m], device_id=dev, device_id_type=MESH,
+                    )
+                    copy.start()
+                    copies.append(copy)
+                    if dy == 0:
+                        rows = pl.ds(s - s % 8, 8)
+                        block = pltpu.make_async_remote_copy(
+                            src_ref=states_ref.at[rows], dst_ref=states_ref.at[rows],
+                            send_sem=st_sends.at[r, dz - 1], recv_sem=st_recvs.at[r, dz - 1],
+                            device_id=dev, device_id_type=MESH,
+                        )
+                        block.start()
+                        copies.append(block)
+        for j in range(1, n if r < 2 else 1):
             dev = device(axis, partner(here[axis], stride, n, j))
             copy = pltpu.make_async_remote_copy(
                 src_ref=bufs[0] if r == 0 else bufs[r].at[mine],
@@ -236,7 +264,7 @@
             )
             out.start()
             outs.append(out)
-            if r == len(rounds) - 1:
+            if r == 2:
                 pos, sub, slot, half = unpack(code_ref)
                 entries = code_ref.shape[0]
                 row_hot_ref[...] = (
@@ -246,7 +274,14 @@
         for copy in copies:
             copy.wait_recv()
         sent += copies
-        if r == 0:
+        if r == 2:
+
+            def got(dz, dy):
+                return bufs[r][mine, :] if dz == 0 and dy == 0 else held2[dz * cross + dy - 1]
+
+            rows_sum = [(got(dz, 0) + got(dz, 2)) + (got(dz, 1) + got(dz, 3)) for dz in range(4)]
+            bufs[r + 1][mine, :] = (rows_sum[0] + rows_sum[2]) + (rows_sum[1] + rows_sum[3])
+        elif r == 0:
             bufs[r + 1][mine, :] = bufs[r][mine, :] + held[r, 0, mine, :]
         elif n == 2:
             bufs[r + 1][mine, :] = bufs[r][mine, :] + held[r, 0, pl.ds(0, share)]
@@ -330,6 +365,9 @@
             pltpu.SemaphoreType.DMA((len(rounds),)),
             pltpu.VMEM((code_parts[1].shape[0], NSUB * R), jnp.bfloat16),
             pltpu.VMEM((code_parts[1].shape[0], planes * ny), jnp.bfloat16),
+            pltpu.VMEM((15, R // 2, 3 * TILE), jnp.float32),
+            pltpu.SemaphoreType.DMA((15,)),
+            pltpu.SemaphoreType.DMA((15,)),
         ],
         compiler_params=pltpu.CompilerParams(collective_id=0, has_side_effects=True),
     )(*code_parts, rotor_states, velocity, w_in, decay.reshape(1, -1), w_out)

time: 45.7 us -> 44.1 us (0.965)
  Pallas kernels: 36.3 us -> 34.7 us
    pallas_call x1, Pallas kernels: 36.3 us -> 34.7 us  [reduce_step(): pl.pallas_call(lambda *refs: step_kernel(rounds, *refs), out_shape=(jax.S...]
where the time goes in v18:
time: 44.1 us; the launch traced here: 43.9 us
  Pallas kernels  34.7 us (79%)
  local copies, waits for them, and re-layouts  5.53 us (13%)
  other arithmetic  2.97 us (7%)
  between operations  0.65 us (1%)
    pallas_call x1, Pallas kernels, reduce_step(): pl.pallas_call(lambda *refs: step_kernel(rounds, *refs), out_shape=(jax.S...  34.7 us
    unnamed x4, local copies, waits for them, and re-layouts  4.5 us
    another operation x2, other arithmetic, on_device(): parts = jnp.stack([high, middle, low]).astype(jnp.bfloat16)  1.45 us
    broadcast_in_dim x1, local copies, waits for them, and re-layouts, on_device(): code[:, None]  1.02 us

profile of v18, /device:TPU:1, one launch (start us, length us, event | category | flops | bytes accessed | tf_op | source)
XLA Modules:
  0.0 43.9 jit_solution(393577097449905280)
XLA Ops:
  0.6 0.8 %select_reduce_fusion = s32[1024]{0:T(1024)S(1)} fusion(s32[32]{0:T(128)} %param.16, s32[1024]{0:T(1024)} %bitcast.11), kind=kLoop, calls=%fused_computation | loop fusion | flops 97280 | bytes 8320 | tf_op jit(solution)/shard_map/reduce_sum | solution.py:477
  1.4 0.7 %fusion.9 = s32[1024]{0:T(1024)S(1)} fusion(s32[1024]{0:T(1024)S(1)} %select_reduce_fusion, s32[1024]{0:T(1024)} %param.19, s32[1024]{0:T(1024)} %param.18), kind=kLoop, calls=%fused_computation.21 | loop fusion | flops 25600 | bytes 16384 | tf_op jit(solution)/shard_map/add | solution.py:484
  2.1 0.8 %fusion.2 = (bf16[1,32,384]{2,1,0:T(8,128)(2,1)S(1)}, bf16[1,32,384]{2,1,0:T(8,128)(2,1)S(1)}, bf16[1,32,384]{2,1,0:T(8,128)(2,1)S(1)}) fusion(f32[32,384]{1,0:T(8,128)} %param.11), kind=kLoop, calls=%fused_computation.9 | loop fusion | flops 86016 | bytes 122880 | tf_op jit(solution)/shard_map/stack | solution.py:482
  3.0 0.6 %pad_maximum_fusion.refs_0_ = bf16[3,32,384]{2,1,0:T(8,128)(2,1)} fusion(bf16[1,32,384]{2,1,0:T(8,128)(2,1)S(1)} %get-tuple-element.7, bf16[1,32,384]{2,1,0:T(8,128)(2,1)S(1)} %get-tuple-element.8, bf16[1,32,384]{2,1,0:T(8,128)(2,1)S(1)} %get-tuple-element.6), kind=kLoop, calls=%fused_computation.2 | loop fusion | flops 73728 | bytes 147456 | tf_op jit(solution)/shard_map/stack | solution.py:482
  3.6 1.0 %copy.13.refs_1_ = s32[1024,1]{1,0:T(8,128)} copy(s32[1024,1]{0,1:T(1,128)S(1)} %bitcast.9) | data formatting | bytes 8192 | tf_op jit(solution)/shard_map/broadcast_in_dim | solution.py:485
  4.6 34.7 %shard_map.113 = (f32[1,1024]{1,0:T(1,128)}, f32[3,16,64,256]{3,2,1,0:T(8,128)}) custom-call(bf16[3,32,384]{2,1,0:T(8,128)(2,1)} %pad_maximum_fusion.refs_0_, s32[1024,1]{1,0:T(8,128)} %copy.13.refs_1_, f32[1,1024]{1,0:T(1,128)} %refs_2_.1, f32[3,16,64,256]{3,2,1,0:T(8,128)} %refs_3_.1, bf16[384,1024]{1,0:T(8,128)(2,1)} %refs_4_.1, f32[1,1024]{1,0:T(1,128)} %bitcast.10, ...), custom_call_target="tpu_custom_call" | custom-call | tf_op jit(solution)/shard_map/pallas_call | solution.py:336
  39.4 0.0 copy-start
  39.4 3.9 %copy.16 = f32[3,16,64,256]{3,2,1,0:T(8,128)} copy(f32[3,16,64,256]{3,2,1,0:T(8,128)} %get-tuple-element.11) | data formatting | bytes 6291456
  43.3 0.0 copy-done
  43.3 0.6 %copy.17 = f32[1,1024]{1,0:T(1,128)} copy(f32[1,1024]{1,0:T(1,128)S(1)} %copy-done) | data formatting | bytes 8192
Async XLA Ops:
  39.4 3.9 %copy-start = (f32[1,1024]{1,0:T(1,128)S(1)}, f32[1,1024]{1,0:T(1,128)}, u32[]{:S(2)}) copy-start(f32[1,1024]{1,0:T(1,128)} %get-tuple-element.12) | copy-start | bytes 12292

commit v19 on v18

--- a/solution.py
+++ b/solution.py
@@ -183,7 +183,7 @@
         face_copies.append((send_if, recv_if, copy))
 
 
-    chunks = [None, (0, 6), (6, planes), None]
+    chunks = [None, (0, planes // 2), (planes // 2, planes), None]
     share = R // 2
     mine = pl.ds(pl.multiple_of((s % 2) * share, share), share)
     final = 3

time: 44.1 us -> 44.6 us (1.011)
  Pallas kernels: 34.7 us -> 35.2 us
    pallas_call x1, Pallas kernels: 34.7 us -> 35.2 us  [reduce_step(): pl.pallas_call(lambda *refs: step_kernel(rounds, *refs), out_shape=(jax.S...]
where the time goes in v19:
time: 44.6 us; the launch traced here: 44.4 us
  Pallas kernels  35.2 us (79%)
  local copies, waits for them, and re-layouts  5.53 us (12%)
  other arithmetic  2.97 us (7%)
  between operations  0.65 us (1%)
    pallas_call x1, Pallas kernels, reduce_step(): pl.pallas_call(lambda *refs: step_kernel(rounds, *refs), out_shape=(jax.S...  35.2 us
    unnamed x4, local copies, waits for them, and re-layouts  4.5 us
    another operation x2, other arithmetic, on_device(): parts = jnp.stack([high, middle, low]).astype(jnp.bfloat16)  1.45 us
    broadcast_in_dim x1, local copies, waits for them, and re-layouts, on_device(): code[:, None]  1.02 us

profile of v19, /device:TPU:1, one launch (start us, length us, event | category | flops | bytes accessed | tf_op | source)
XLA Modules:
  0.0 44.4 jit_solution(6509764687538569959)
XLA Ops:
  0.6 0.8 %select_reduce_fusion = s32[1024]{0:T(1024)S(1)} fusion(s32[32]{0:T(128)} %param.16, s32[1024]{0:T(1024)} %bitcast.11), kind=kLoop, calls=%fused_computation | loop fusion | flops 97280 | bytes 8320 | tf_op jit(solution)/shard_map/reduce_sum | solution.py:477
  1.4 0.7 %fusion.9 = s32[1024]{0:T(1024)S(1)} fusion(s32[1024]{0:T(1024)S(1)} %select_reduce_fusion, s32[1024]{0:T(1024)} %param.19, s32[1024]{0:T(1024)} %param.18), kind=kLoop, calls=%fused_computation.21 | loop fusion | flops 25600 | bytes 16384 | tf_op jit(solution)/shard_map/add | solution.py:484
  2.1 0.8 %fusion.2 = (bf16[1,32,384]{2,1,0:T(8,128)(2,1)S(1)}, bf16[1,32,384]{2,1,0:T(8,128)(2,1)S(1)}, bf16[1,32,384]{2,1,0:T(8,128)(2,1)S(1)}) fusion(f32[32,384]{1,0:T(8,128)} %param.11), kind=kLoop, calls=%fused_computation.9 | loop fusion | flops 86016 | bytes 122880 | tf_op jit(solution)/shard_map/stack | solution.py:482
  3.0 0.6 %pad_maximum_fusion.refs_0_ = bf16[3,32,384]{2,1,0:T(8,128)(2,1)} fusion(bf16[1,32,384]{2,1,0:T(8,128)(2,1)S(1)} %get-tuple-element.7, bf16[1,32,384]{2,1,0:T(8,128)(2,1)S(1)} %get-tuple-element.8, bf16[1,32,384]{2,1,0:T(8,128)(2,1)S(1)} %get-tuple-element.6), kind=kLoop, calls=%fused_computation.2 | loop fusion | flops 73728 | bytes 147456 | tf_op jit(solution)/shard_map/stack | solution.py:482
  3.6 1.0 %copy.13.refs_1_ = s32[1024,1]{1,0:T(8,128)} copy(s32[1024,1]{0,1:T(1,128)S(1)} %bitcast.9) | data formatting | bytes 8192 | tf_op jit(solution)/shard_map/broadcast_in_dim | solution.py:485
  4.6 35.2 %shard_map.113 = (f32[1,1024]{1,0:T(1,128)}, f32[3,16,64,256]{3,2,1,0:T(8,128)}) custom-call(bf16[3,32,384]{2,1,0:T(8,128)(2,1)} %pad_maximum_fusion.refs_0_, s32[1024,1]{1,0:T(8,128)} %copy.13.refs_1_, f32[1,1024]{1,0:T(1,128)} %refs_2_.1, f32[3,16,64,256]{3,2,1,0:T(8,128)} %refs_3_.1, bf16[384,1024]{1,0:T(8,128)(2,1)} %refs_4_.1, f32[1,1024]{1,0:T(1,128)} %bitcast.10, ...), custom_call_target="tpu_custom_call" | custom-call | tf_op jit(solution)/shard_map/pallas_call | solution.py:336
  39.9 0.0 copy-start
  39.9 3.9 %copy.16 = f32[3,16,64,256]{3,2,1,0:T(8,128)} copy(f32[3,16,64,256]{3,2,1,0:T(8,128)} %get-tuple-element.11) | data formatting | bytes 6291456
  43.8 0.0 copy-done
  43.8 0.6 %copy.17 = f32[1,1024]{1,0:T(1,128)} copy(f32[1,1024]{1,0:T(1,128)S(1)} %copy-done) | data formatting | bytes 8192
Async XLA Ops:
  39.9 3.9 %copy-start = (f32[1,1024]{1,0:T(1,128)S(1)}, f32[1,1024]{1,0:T(1,128)}, u32[]{:S(2)}) copy-start(f32[1,1024]{1,0:T(1,128)} %get-tuple-element.12) | copy-start | bytes 12292

commit v20 on v19

--- a/solution.py
+++ b/solution.py
@@ -240,6 +240,13 @@
                 )
                 block.start()
                 copies.append(block)
+        if r == 0:
+            pos, sub, slot, half = unpack(code_ref)
+            entries = code_ref.shape[0]
+            row_hot_ref[...] = (
+                (sub * R + slot) == lax.broadcasted_iota(jnp.int32, (entries, NSUB * R), 1)
+            ).astype(jnp.bfloat16)
+            pick_ref[...] = (pos == lax.broadcasted_iota(jnp.int32, (entries, planes * ny), 1)).astype(jnp.bfloat16)
         if r == 1:
             for send_if, recv_if, face in face_copies:
 
@@ -264,13 +271,6 @@
             )
             out.start()
             outs.append(out)
-            if r == 2:
-                pos, sub, slot, half = unpack(code_ref)
-                entries = code_ref.shape[0]
-                row_hot_ref[...] = (
-                    (sub * R + slot) == lax.broadcasted_iota(jnp.int32, (entries, NSUB * R), 1)
-                ).astype(jnp.bfloat16)
-                pick_ref[...] = (pos == lax.broadcasted_iota(jnp.int32, (entries, planes * ny), 1)).astype(jnp.bfloat16)
         for copy in copies:
             copy.wait_recv()
         sent += copies

time: 44.6 us -> 44.4 us (level)
  no operation moved by 1% of the time
where the time goes in v20:
time: 44.4 us; the launch traced here: 44.1 us
  Pallas kernels  35 us (79%)
  local copies, waits for them, and re-layouts  5.53 us (12%)
  other arithmetic  2.97 us (7%)
  between operations  0.65 us (1%)
    pallas_call x1, Pallas kernels, reduce_step(): pl.pallas_call(lambda *refs: step_kernel(rounds, *refs), out_shape=(jax.S...  35 us
    unnamed x4, local copies, waits for them, and re-layouts  4.5 us
    another operation x2, other arithmetic, on_device(): parts = jnp.stack([high, middle, low]).astype(jnp.bfloat16)  1.45 us
    broadcast_in_dim x1, local copies, waits for them, and re-layouts, on_device(): code[:, None]  1.02 us

profile of v20, /device:TPU:1, one launch (start us, length us, event | category | flops | bytes accessed | tf_op | source)
XLA Modules:
  0.0 44.1 jit_solution(4588337442528650692)
XLA Ops:
  0.6 0.8 %select_reduce_fusion = s32[1024]{0:T(1024)S(1)} fusion(s32[32]{0:T(128)} %param.16, s32[1024]{0:T(1024)} %bitcast.11), kind=kLoop, calls=%fused_computation | loop fusion | flops 97280 | bytes 8320 | tf_op jit(solution)/shard_map/reduce_sum | solution.py:477
  1.4 0.7 %fusion.9 = s32[1024]{0:T(1024)S(1)} fusion(s32[1024]{0:T(1024)S(1)} %select_reduce_fusion, s32[1024]{0:T(1024)} %param.19, s32[1024]{0:T(1024)} %param.18), kind=kLoop, calls=%fused_computation.21 | loop fusion | flops 25600 | bytes 16384 | tf_op jit(solution)/shard_map/add | solution.py:484
  2.1 0.8 %fusion.2 = (bf16[1,32,384]{2,1,0:T(8,128)(2,1)S(1)}, bf16[1,32,384]{2,1,0:T(8,128)(2,1)S(1)}, bf16[1,32,384]{2,1,0:T(8,128)(2,1)S(1)}) fusion(f32[32,384]{1,0:T(8,128)} %param.11), kind=kLoop, calls=%fused_computation.9 | loop fusion | flops 86016 | bytes 122880 | tf_op jit(solution)/shard_map/stack | solution.py:482
  3.0 0.6 %pad_maximum_fusion.refs_0_ = bf16[3,32,384]{2,1,0:T(8,128)(2,1)} fusion(bf16[1,32,384]{2,1,0:T(8,128)(2,1)S(1)} %get-tuple-element.7, bf16[1,32,384]{2,1,0:T(8,128)(2,1)S(1)} %get-tuple-element.8, bf16[1,32,384]{2,1,0:T(8,128)(2,1)S(1)} %get-tuple-element.6), kind=kLoop, calls=%fused_computation.2 | loop fusion | flops 73728 | bytes 147456 | tf_op jit(solution)/shard_map/stack | solution.py:482
  3.6 1.0 %copy.13.refs_1_ = s32[1024,1]{1,0:T(8,128)} copy(s32[1024,1]{0,1:T(1,128)S(1)} %bitcast.9) | data formatting | bytes 8192 | tf_op jit(solution)/shard_map/broadcast_in_dim | solution.py:485
  4.6 35.0 %shard_map.113 = (f32[1,1024]{1,0:T(1,128)}, f32[3,16,64,256]{3,2,1,0:T(8,128)}) custom-call(bf16[3,32,384]{2,1,0:T(8,128)(2,1)} %pad_maximum_fusion.refs_0_, s32[1024,1]{1,0:T(8,128)} %copy.13.refs_1_, f32[1,1024]{1,0:T(1,128)} %refs_2_.1, f32[3,16,64,256]{3,2,1,0:T(8,128)} %refs_3_.1, bf16[384,1024]{1,0:T(8,128)(2,1)} %refs_4_.1, f32[1,1024]{1,0:T(1,128)} %bitcast.10, ...), custom_call_target="tpu_custom_call" | custom-call | tf_op jit(solution)/shard_map/pallas_call | solution.py:336
  39.6 0.0 copy-start
  39.6 3.9 %copy.16 = f32[3,16,64,256]{3,2,1,0:T(8,128)} copy(f32[3,16,64,256]{3,2,1,0:T(8,128)} %get-tuple-element.11) | data formatting | bytes 6291456
  43.5 0.0 copy-done
  43.5 0.6 %copy.17 = f32[1,1024]{1,0:T(1,128)} copy(f32[1,1024]{1,0:T(1,128)S(1)} %copy-done) | data formatting | bytes 8192
Async XLA Ops:
  39.6 3.9 %copy-start = (f32[1,1024]{1,0:T(1,128)S(1)}, f32[1,1024]{1,0:T(1,128)}, u32[]{:S(2)}) copy-start(f32[1,1024]{1,0:T(1,128)} %get-tuple-element.12) | copy-start | bytes 12292
